TPU v7x, 32 devices: a whole 2x2x4 slice. The times are simulated.
32 devices in a mesh: dp: 2 (over x), ep: 16 (over z, y, core).
Axes of the slice: x: 2, y: 2, z: 4, core: 2. Of those that a mesh axis runs over, the one named last changes fastest.
Arguments:
- queries: bfloat16 [2048, 36864], P('ep', 'dp'), may hold values from -40 to 40
- suffix_latent: bfloat16 [2048, 576], P('ep'), may hold values from -10 to 10
- page_pool: bfloat16 [128, 36864], P('ep'), may hold values from -6 to 6
- page_owner: int32 [16, 32], P('ep'), may hold values from 0 to 15, as said below
- page_slot: int32 [16, 32], P('ep'), may hold values from 0 to 7
- prefix_len: int32 [16], P('ep'), may hold values from 1025 to 2048, as said below
- moe_input: bfloat16 [512, 3584], P(('dp', 'ep')), may hold values from -6 to 6
- expert_ids: int32 [512, 8], P(('dp', 'ep')), may hold values from 0 to 15, all different within a row; in each aligned block of 16 rows (0 to 15, 16 to 31, ...) at most 10 rows name the same one
- gate_weights: float32 [512, 8], P(('dp', 'ep')), may hold values from 0.1 to 0.6
- w_gate: bfloat16 [16, 3584, 1024], P('ep', None, 'dp'), may hold values from -0.09375 to 0.09375
- w_up: bfloat16 [16, 3584, 1024], P('ep', None, 'dp'), may hold values from -0.09375 to 0.09375
- w_down: bfloat16 [16, 1024, 3584], P('ep', 'dp'), may hold values from -0.1875 to 0.1875
Outputs:
- attn_context: bfloat16 [2048, 32768], P('ep', 'dp')
- moe_output: bfloat16 [512, 3584], P(('dp', 'ep'))
Inputs may be any that keep to these rules, and one draw needn't show every extreme that they name: `page_owner`: for a multiple m of the ep axis's size, the pages m, m + 1, ... of one request up to m + that size - 1 have distinct owners, so page k is the (k div that size)-th page of its request on its owner; entries past a request's prefix are valid page references too. `prefix_len`: some request has the longest prefix, 2048 tokens. `expert_ids`: in the 16 rows of one device no expert is named by more than 10 rows.
All inputs are finite; a program needn't handle non-finite values.
Results may differ from a plain program's by a relative error of at most 0.0057.
Values may be sent and summed in bfloat16 or wider, within the bound.
No kernel may reach another device: no remote copies, remote signals or barrier semaphores. Data moves between devices by JAX's collectives and lax.ppermute only.
A program may use at most 192 MiB of HBM per device.

v0:
```python
import functools
import math

import jax
import jax.numpy as jnp
from jax import lax
from jax.experimental import pallas as pl
from jax.experimental.pallas import tpu as pltpu
from jax.sharding import PartitionSpec as P


LATENT = 512
ROPE = 64
KEY = LATENT + ROPE
PAGE = 64

score_scale = 0.07216878364870322
neg_large = -1e30


def pull(values, axis, stride, size, shift):
    total = lax.axis_size(axis)
    pairs = []
    for dst in range(total):
        pos = (dst // stride) % size
        src = dst + (((pos + shift) % size) - pos) * stride
        pairs.append((src, dst))
    return lax.ppermute(values, axis, pairs)


def push(values, axis, stride, size, shift):
    return pull(values, axis, stride, size, size - shift)


def gather_stages():
    ep_size = lax.axis_size("ep")
    inner = 2 if ep_size % 2 == 0 else 1
    middle = 2 if ep_size % (2 * inner) == 0 else 1
    outer = ep_size // (inner * middle)
    stages = [
        ("ep", inner * middle, outer),
        ("dp", 1, lax.axis_size("dp")),
        ("ep", inner, middle),
        ("ep", 1, inner),
    ]
    return [stage for stage in stages if stage[2] > 1]


def attention_body(bias_ref, q_ref, *refs, heads, together, pieces, aliased):
    piece_refs = refs[:pieces]
    o_ref, k_ref, sem = refs[pieces + aliased :]
    tokens = q_ref.shape[0]
    keys = k_ref.shape[0]
    prefix = bias_ref.shape[1]
    factor = score_scale * math.log2(math.e)

    @pl.when(pl.program_id(0) == 0)
    def load_keys():
        copies = []
        start = 0
        for n, piece in enumerate(piece_refs):
            rows = piece.shape[0]
            copy = pltpu.make_async_copy(piece, k_ref.at[pl.ds(start, rows)], sem.at[n])
            copy.start()
            copies.append(copy)
            start += rows
        for copy in copies:
            copy.wait()

    bias = bias_ref[...]
    row = lax.broadcasted_iota(jnp.int32, (tokens, keys - prefix), 0)
    col = lax.broadcasted_iota(jnp.int32, (tokens, keys - prefix), 1)
    causal = jnp.where(col <= row, 0.0, neg_large).astype(jnp.float32)
    causal = jnp.concatenate([causal] * together, axis=0)
    for first in range(0, heads, together):
        group = range(first, first + together)
        q = jnp.concatenate([q_ref[:, h * KEY : (h + 1) * KEY] for h in group], axis=0)
        s = lax.dot_general(
            q, k_ref[...], (((1,), (1,)), ((), ())), preferred_element_type=jnp.float32
        )
        sp = s[:, :prefix] + bias
        ss = s[:, prefix:] + causal
        m = jnp.maximum(jnp.max(sp, axis=1, keepdims=True), jnp.max(ss, axis=1, keepdims=True))
        shift = m * factor
        pp = jnp.exp2(sp * factor - shift)
        ps = jnp.exp2(ss * factor - shift)
        total = jnp.sum(pp, axis=1, keepdims=True) + jnp.sum(ps, axis=1, keepdims=True)
        p = jnp.concatenate([pp.astype(jnp.bfloat16), ps.astype(jnp.bfloat16)], axis=1)
        acc = jnp.dot(p, k_ref[:, :LATENT], preferred_element_type=jnp.float32) / total
        for n, h in enumerate(group):
            part = acc[n * tokens : (n + 1) * tokens]
            o_ref[:, h * LATENT : (h + 1) * LATENT] = part.astype(jnp.bfloat16)


def attend(queries, pieces, bias, start, count, heads, so_far=None):
    tokens = queries.shape[0]
    head_count = queries.shape[1] // KEY
    keys = sum(piece.shape[0] for piece in pieces)
    together = 4 if heads % 4 == 0 and keys <= 2304 else 2
    offset = start // heads
    aliased = 0 if so_far is None else 1
    anywhere = pl.BlockSpec(memory_space=pl.ANY)
    extra = [so_far] if aliased else []
    return pl.pallas_call(
        functools.partial(
            attention_body, heads=heads, together=together, pieces=len(pieces), aliased=aliased
        ),
        grid=(count // heads,),
        in_specs=[
            pl.BlockSpec(bias.shape, lambda i: (0, 0)),
            pl.BlockSpec((tokens, heads * KEY), lambda i: (0, i + offset)),
            *[anywhere] * (len(pieces) + aliased),
        ],
        out_specs=pl.BlockSpec((tokens, heads * LATENT), lambda i: (0, i + offset)),
        out_shape=jax.ShapeDtypeStruct((tokens, head_count * LATENT), jnp.bfloat16),
        scratch_shapes=[
            pltpu.VMEM((keys, KEY), jnp.bfloat16),
            pltpu.SemaphoreType.DMA((len(pieces),)),
        ],
        input_output_aliases={2 + len(pieces): 0} if aliased else {},
        compiler_params=pltpu.CompilerParams(vmem_limit_bytes=56 << 20),
        name="attend",
    )(bias, queries, *pieces, *extra)


def pull_block(values, a, b, inner):
    total = lax.axis_size("ep")
    outer = total // inner
    pairs = []
    for dst in range(total):
        src = (dst // inner + a) % outer * inner + (dst % inner + b) % inner
        pairs.append((src, dst))
    return lax.ppermute(values, "ep", pairs)


def fetch_pages(page_pool, page_owner, page_slot, length):
    ep_size = lax.axis_size("ep")
    dp_size = lax.axis_size("dp")
    me = lax.axis_index("ep")
    plane = lax.axis_index("dp")
    pages = page_owner.shape[1]
    ranks = (pages + ep_size - 1) // ep_size
    planes = dp_size if ranks % dp_size == 0 else 1
    own_ranks = ranks // planes
    inner = 4 if ep_size % 4 == 0 else 1
    outer = ep_size // inner
    page_id = jnp.arange(pages, dtype=jnp.int32)
    owners = jnp.arange(ep_size, dtype=jnp.int32)
    rank_id = jnp.arange(ranks, dtype=jnp.int32)
    match = (page_owner[0][None, None, :] == owners[:, None, None]) & (
        page_id[None, None, :] // ep_size == rank_id[None, :, None]
    )
    wanted = jnp.sum(jnp.where(match, page_slot[0][None, None, :], 0), axis=2)
    asked = lax.all_to_all(wanted, "ep", split_axis=0, concat_axis=0, tiled=True)
    steps = jnp.arange(ep_size, dtype=jnp.int32)
    serve = (me // inner - steps // inner) % outer * inner + (me % inner - steps % inner) % inner
    hear = (me // inner + steps // inner) % outer * inner + (me % inner + steps % inner) % inner
    slots = asked[serve]
    first = (plane * own_ranks) % ranks if planes > 1 else 0
    mine = lax.dynamic_slice_in_dim(slots, first, own_ranks, axis=1)
    pool = page_pool.reshape(page_pool.shape[0], PAGE, KEY)
    chosen = pick_pages(pool, mine, ep_size, own_ranks)
    pieces = []
    for step in range(ep_size):
        a, b = step // inner, step % inner
        pieces.append(pull_block(chosen[step], a, b, inner) if step else chosen[step])
    blocks = list(pieces)
    for shift in range(1, planes):
        for step in range(ep_size):
            blocks.append(pull(pieces[step], "dp", 1, dp_size, shift))
    number = jnp.sum(jnp.where(match, page_id[None, None, :], 0), axis=2)
    number = jnp.where(jnp.any(match, axis=2), number, pages)[hear]
    by_plane = number.reshape(ep_size, planes, own_ranks).transpose(1, 0, 2)
    if planes > 1:
        by_plane = by_plane[(plane + jnp.arange(planes, dtype=jnp.int32)) % planes]
    position = by_plane.reshape(-1)[:, None] * PAGE + jnp.arange(PAGE, dtype=jnp.int32)[None, :]
    seen = (position < length) & (position < pages * PAGE)
    bias = jnp.where(seen, 0.0, neg_large).astype(jnp.float32).reshape(1, -1)
    return blocks, bias


def pick_body(slots_ref, pool_ref, *refs, count):
    outs = refs[:-1]
    sem = refs[-1]
    copies = []
    for n, out in enumerate(outs):
        for r in range(count):
            copies.append(
                pltpu.make_async_copy(
                    pool_ref.at[slots_ref[n, r]], out.at[pl.ds(r * PAGE, PAGE)], sem.at[n, r]
                )
            )
    for copy in copies:
        copy.start()
    for copy in copies:
        copy.wait()


def pick_pages(pool, slots, steps, count):
    anywhere = pl.BlockSpec(memory_space=pl.ANY)
    return pl.pallas_call(
        functools.partial(pick_body, count=count),
        in_specs=[pl.BlockSpec(memory_space=pltpu.SMEM), anywhere],
        out_specs=[anywhere] * steps,
        out_shape=[jax.ShapeDtypeStruct((count * PAGE, KEY), pool.dtype)] * steps,
        scratch_shapes=[pltpu.SemaphoreType.DMA((steps, count))],
        name="pick",
    )(slots, pool)


def split_exact(values):
    high = values.astype(jnp.bfloat16)
    rest = values - high.astype(jnp.float32)
    mid = rest.astype(jnp.bfloat16)
    low = (rest - mid.astype(jnp.float32)).astype(jnp.bfloat16)
    return jnp.concatenate([high, mid, low], axis=1)


def experts_staged(moe_input, expert_ids, gate_weights, w_gate, w_up, w_down):
    ep_size = lax.axis_size("ep")
    _, features = moe_input.shape
    experts = jnp.arange(ep_size, dtype=jnp.int32)
    named = expert_ids[:, :, None] == experts[None, None, :]
    dense = jnp.sum(jnp.where(named, gate_weights[:, :, None], 0.0), axis=1)
    extra = split_exact(dense)
    lanes = -(-extra.shape[1] // 128) * 128
    extra = jnp.pad(extra, ((0, 0), (0, lanes - extra.shape[1])))
    rows = jnp.concatenate([moe_input, extra], axis=1)
    stages = gather_stages()
    for axis, stride, size in stages:
        rows = jnp.concatenate(
            [rows] + [pull(rows, axis, stride, size, shift) for shift in range(1, size)], axis=0
        )
    inputs = rows[:, :features]
    parts = rows[:, features : features + 3 * ep_size].astype(jnp.float32)
    parts = parts.reshape(-1, 3, ep_size)
    here = (experts == lax.axis_index("ep"))[None, None, :]
    parts = jnp.sum(jnp.where(here, parts, 0.0), axis=2)
    weight = (parts[:, 0] + parts[:, 1] + parts[:, 2])[:, None]
    gate_proj = jnp.dot(inputs, w_gate[0], preferred_element_type=jnp.float32)
    up_proj = jnp.dot(inputs, w_up[0], preferred_element_type=jnp.float32)
    hidden = (jax.nn.silu(gate_proj) * up_proj).astype(jnp.bfloat16)
    kept = jnp.dot(hidden, w_down[0], preferred_element_type=jnp.float32) * weight
    for axis, stride, size in reversed(stages):
        count = kept.shape[0] // size
        moved = [
            push(kept[s * count : (s + 1) * count].astype(jnp.bfloat16), axis, stride, size, s)
            for s in range(1, size)
        ]
        kept = kept[:count]
        for m in moved:
            kept = kept + m.astype(jnp.float32)
    return kept.astype(jnp.bfloat16)


def expert_body(weight_ref, *refs, places, hidden_steps):
    pieces = refs[: len(places)]
    gate_ref, up_ref, down_ref, keep_ref, send_ref, x_ref, acc_ref, sem = refs[len(places) :]
    step = pl.program_id(0)

    @pl.when(step == 0)
    def load_rows():
        copies = []
        for n, (piece, (row, lane, lanes)) in enumerate(zip(pieces, places, strict=True)):
            rows = piece.shape[0]
            copies.append(
                pltpu.make_async_copy(
                    piece.at[:, pl.ds(0, lanes)],
                    x_ref.at[pl.ds(row, rows), pl.ds(lane, lanes)],
                    sem.at[n],
                )
            )
        for copy in copies:
            copy.start()
        for copy in copies:
            copy.wait()

    x = x_ref[...]
    gate = jnp.dot(x, gate_ref[...], preferred_element_type=jnp.float32)
    up = jnp.dot(x, up_ref[...], preferred_element_type=jnp.float32)
    hidden = (gate / (1.0 + jnp.exp(-gate)) * up).astype(jnp.bfloat16)
    part = jnp.dot(hidden, down_ref[...], preferred_element_type=jnp.float32)

    @pl.when(step == 0)
    def begin():
        acc_ref[...] = part

    @pl.when((step > 0) & (step < hidden_steps - 1))
    def add():
        acc_ref[...] += part

    @pl.when(step == hidden_steps - 1)
    def finish():
        total = (acc_ref[...] + part) * weight_ref[...]
        half = keep_ref.shape[0]
        keep_ref[...] = total[:half]
        send_ref[...] = total[half:].astype(jnp.bfloat16)


def expert_call(weight, pieces, places, w_gate, w_up, w_down):
    rows = weight.shape[0]
    features, hidden = w_gate.shape
    block = 256
    anywhere = pl.BlockSpec(memory_space=pl.ANY)
    return pl.pallas_call(
        functools.partial(expert_body, places=places, hidden_steps=hidden // block),
        grid=(hidden // block,),
        in_specs=[
            pl.BlockSpec((rows, 1), lambda i: (0, 0)),
            *[anywhere] * len(pieces),
            pl.BlockSpec((features, block), lambda i: (0, i)),
            pl.BlockSpec((features, block), lambda i: (0, i)),
            pl.BlockSpec((block, features), lambda i: (i, 0)),
        ],
        out_specs=[
            pl.BlockSpec((rows // 2, features), lambda i: (0, 0)),
            pl.BlockSpec((rows // 2, features), lambda i: (0, 0)),
        ],
        out_shape=[
            jax.ShapeDtypeStruct((rows // 2, features), jnp.float32),
            jax.ShapeDtypeStruct((rows // 2, features), jnp.bfloat16),
        ],
        scratch_shapes=[
            pltpu.VMEM((rows, features), jnp.bfloat16),
            pltpu.VMEM((rows, features), jnp.float32),
            pltpu.SemaphoreType.DMA((len(pieces),)),
        ],
        compiler_params=pltpu.CompilerParams(vmem_limit_bytes=58 << 20),
        name="expert",
    )(weight, *pieces, w_gate, w_up, w_down)


def can_square(tokens, hidden):
    ep_size = lax.axis_size("ep")
    total = tokens * ep_size * lax.axis_size("dp")
    return lax.axis_size("dp") == 2 and ep_size % 4 == 0 and total <= 512 and hidden % 256 == 0


def experts_square(moe_input, expert_ids, gate_weights, w_gate, w_up, w_down):
    ep_size = lax.axis_size("ep")
    outer = ep_size // 4
    tokens, features = moe_input.shape
    left = features // 256 * 128
    experts = jnp.arange(ep_size, dtype=jnp.int32)
    named = expert_ids[:, :, None] == experts[None, None, :]
    dense = jnp.sum(jnp.where(named, gate_weights[:, :, None], 0.0), axis=1)
    extra = split_exact(dense)
    lanes = -(-extra.shape[1] // 128) * 128
    extra = jnp.pad(extra, ((0, 0), (0, lanes - extra.shape[1])))
    rows = jnp.concatenate([moe_input, extra], axis=1)
    far = []
    for shift in range(1, outer):
        far.append(pull(rows, "ep", 4, outer, shift))
    own = jnp.concatenate([rows] + far, axis=0)
    by_x = pull(own, "dp", 1, 2, 1)
    by_y = pull(own, "ep", 2, 2, 1)
    both_a = pull(by_x[:, :left], "ep", 2, 2, 1)
    both_b = pull(by_y[:, left:], "dp", 1, 2, 1)
    near = [own, by_x, by_y, both_a, both_b]
    partner = []
    for piece in near:
        partner.append(pull(piece, "ep", 1, 2, 1))
    block = own.shape[0]
    places = []
    for base in (0, 4 * block):
        places += [(base + n * block, 0, features) for n in range(3)]
        places += [(base + 3 * block, 0, left), (base + 3 * block, left, features - left)]
    tags = []
    for group in (near, partner):
        tags += [piece[:, features:] for piece in group[:3]] + [group[4][:, features - left :]]
    parts = jnp.concatenate(tags, axis=0)[:, : 3 * ep_size].astype(jnp.float32)
    parts = parts.reshape(-1, 3, ep_size)
    here = (experts == lax.axis_index("ep"))[None, None, :]
    parts = jnp.sum(jnp.where(here, parts, 0.0), axis=2)
    weight = (parts[:, 0] + parts[:, 1] + parts[:, 2])[:, None]
    keep, send = expert_call(
        weight, near + partner, tuple(places), w_gate[0], w_up[0], w_down[0]
    )
    got = pull(send, "ep", 1, 2, 1)
    yield None
    keep = keep + got.astype(jnp.float32)
    own, by_x, by_y, both = (keep[n * block : (n + 1) * block] for n in range(4))
    got_a = pull(both[:, :left].astype(jnp.bfloat16), "ep", 2, 2, 1)
    got_b = pull(both[:, left:].astype(jnp.bfloat16), "dp", 1, 2, 1)
    yield None
    by_x = jnp.concatenate([by_x[:, :left] + got_a.astype(jnp.float32), by_x[:, left:]], axis=1)
    by_y = jnp.concatenate([by_y[:, :left], by_y[:, left:] + got_b.astype(jnp.float32)], axis=1)
    got_x = pull(by_x.astype(jnp.bfloat16), "dp", 1, 2, 1)
    got_y = pull(by_y.astype(jnp.bfloat16), "ep", 2, 2, 1)
    yield None
    own = own + got_x.astype(jnp.float32) + got_y.astype(jnp.float32)
    got = []
    for shift in range(1, outer):
        piece = own[shift * tokens : (shift + 1) * tokens].astype(jnp.bfloat16)
        got.append(push(piece, "ep", 4, outer, shift))
    yield None
    total = own[:tokens]
    for piece in got:
        total = total + piece.astype(jnp.float32)
    yield total.astype(jnp.bfloat16)


def on_device(
    queries,
    suffix_latent,
    page_pool,
    page_owner,
    page_slot,
    prefix_len,
    moe_input,
    expert_ids,
    gate_weights,
    w_gate,
    w_up,
    w_down,
):
    pieces, bias = fetch_pages(page_pool, page_owner, page_slot, prefix_len[0])
    pieces = pieces + [suffix_latent]
    moe_args = (moe_input, expert_ids, gate_weights, w_gate, w_up, w_down)
    head_count = queries.shape[1] // KEY
    if not can_square(moe_input.shape[0], w_gate.shape[2]):
        moe_output = experts_staged(*moe_args)
        return (attend(queries, pieces, bias, 0, head_count, 2), moe_output)
    stages = experts_square(*moe_args)
    heads = 4
    steps = head_count // heads
    cuts = [0, steps // 8, 3 * steps // 8, 6 * steps // 8, steps]
    attn_context = None
    for n in range(4):
        next(stages)
        start, count = cuts[n] * heads, (cuts[n + 1] - cuts[n]) * heads
        if count:
            attn_context = attend(
                queries, pieces, bias, start, count, heads, attn_context
            )
    moe_output = next(stages)
    return (attn_context, moe_output)


def solution(mesh):
    return jax.shard_map(
        on_device,
        mesh=mesh,
        in_specs=(
            P("ep", "dp"),
            P("ep", None),
            P("ep", None),
            P("ep", None),
            P("ep", None),
            P("ep"),
            P(("dp", "ep"), None),
            P(("dp", "ep"), None),
            P(("dp", "ep"), None),
            P("ep", None, "dp"),
            P("ep", None, "dp"),
            P("ep", "dp", None),
        ),
        out_specs=(P("ep", "dp"), P(("dp", "ep"), None)),
        check_vma=False,
    )
```

profile of v0, /device:TPU:0, one launch (start us, length us, event | category | flops | bytes accessed | tf_op | source)
XLA Modules:
  0.0 234.3 jit_solution(13631268652815782597)
XLA Ops:
  3.3 5.1 %collective-permute-start.31 = (bf16[16,3712]{1,0:T(8,128)(2,1)S(1)}, bf16[16,3712]{1,0:T(8,128)(2,1)S(1)}, u32[]{:S(2)}, u32[]{:S(2)}) collective-permute-start(bf16[16,3712]{1,0:T(8,128)(2,1)S(1)} %pad_maximum_fusion.3), channel_id=1, source_target_pairs={{4,0},{5,1},{6,2},{7,3},{8,4},{9,5},{10,6},{11,7},{12,8},{13,9},{1... | collective-permute-start | bytes 356360 | tf_op jit(solution)/shard_map/ppermute | solution.py:28
  9.4 2.6 %collective-permute-done.31 = bf16[16,3712]{1,0:T(8,128)(2,1)S(1)} collective-permute-done((bf16[16,3712]{1,0:T(8,128)(2,1)S(1)}, bf16[16,3712]{1,0:T(8,128)(2,1)S(1)}, u32[]{:S(2)}, u32[]{:S(2)}) %collective-permute-start.31) | collective-permute-done | bytes 118816 | tf_op jit(solution)/shard_map/ppermute | solution.py:28
  12.0 6.7 %collective-permute-done.32 = bf16[16,3712]{1,0:T(8,128)(2,1)S(1)} collective-permute-done((bf16[16,3712]{1,0:T(8,128)(2,1)S(1)}, bf16[16,3712]{1,0:T(8,128)(2,1)S(1)}, u32[]{:S(2)}, u32[]{:S(2)}) %collective-permute-start.32) | collective-permute-done | bytes 118816 | tf_op jit(solution)/shard_map/ppermute | solution.py:28
  19.6 1.6 collective-permute-start.35
  22.7 9.2 %collective-permute-done.35.refs_2_ = bf16[64,3712]{1,0:T(8,128)(2,1)S(1)} collective-permute-done((bf16[64,3712]{1,0:T(8,128)(2,1)S(1)}, bf16[64,3712]{1,0:T(8,128)(2,1)S(1)}, u32[]{:S(2)}, u32[]{:S(2)}) %collective-permute-start.35) | collective-permute-done | bytes 475168 | tf_op jit(solution)/shard_map/ppermute | solution.py:28
  31.9 1.6 collective-permute-start.36
  33.5 1.6 collective-permute-start.41
  35.6 4.1 %collective-permute-done.41.refs_3_ = bf16[64,1792]{1,0:T(8,128)(2,1)} collective-permute-done((bf16[64,1792]{1,0:T(8,128)(2,1)S(1)}, bf16[64,1792]{1,0:T(8,128)(2,1)}, u32[]{:S(2)}, u32[]{:S(2)}) %collective-permute-start.41) | collective-permute-done | bytes 229408 | tf_op jit(solution)/shard_map/ppermute | solution.py:28
  43.7 15.3 %expert.1 = (f32[256,3584]{1,0:T(8,128)}, bf16[256,3584]{1,0:T(8,128)(2,1)}) custom-call(f32[512,1]{1,0:T(8,128)} %copy.75.weight_ref, bf16[64,3712]{1,0:T(8,128)(2,1)} %copy-done, bf16[64,3712]{1,0:T(8,128)(2,1)} %copy-done.34, bf16[64,3712]{1,0:T(8,128)(2,1)} %copy-done.33, bf16[64,1792]{1,0:T(8,128)(2,1)} %collective-permute-done.41.refs_3_, ...), custom_call_target="tpu_custom_call" | custom-call | tf_op jit(solution)/shard_map/expert/pallas_call | solution.py:305
  60.0 4.7 %all-to-all-start = ((s32[16,1,2]{2,1,0:T(1,128)}), s32[16,1,2]{2,1,0:T(1,128)S(1)}, u32[]{:S(2)}, u32[]{:S(2)}) async-start(s32[16,1,2]{2,1,0:T(1,128)} %copy.65), calls=%async_computation | async-start | bytes 16384 | tf_op jit(solution)/shard_map/all_to_all | solution.py:154
  65.1 4.6 %fusion.32 = (bf16[256,3584]{1,0:T(8,128)(2,1)S(1)}, f32[256,3584]{1,0:T(8,128)}) fusion(f32[256,3584]{1,0:T(8,128)} %get-tuple-element.36, bf16[256,3584]{1,0:T(8,128)(2,1)S(1)} %collective-permute-done.43), kind=kLoop, calls=%fused_computation.100 | loop fusion | flops 2752512 | bytes 11010048 | tf_op jit(solution)/shard_map/convert.11
  69.7 2.0 collective-permute-start.44
  72.3 1.6 reshape.435.pool_ref
  75.2 41.7 %pick.1 = (bf16[64,576]{1,0:T(8,128)(2,1)}, bf16[64,576]{1,0:T(8,128)(2,1)}, bf16[64,576]{1,0:T(8,128)(2,1)}, bf16[64,576]{1,0:T(8,128)(2,1)}, bf16[64,576]{1,0:...) custom-call(s32[16,1]{1,0:T(8,128)} %constant_dynamic-slice_fusion.s, ...), custom_call_target="tpu_custom_call" | custom-call | tf_op jit(solution)/shard_map/pick/pallas_call | solution.py:201
  118.3 3.3 %collective-permute-start.3 = (bf16[64,576]{1,0:T(8,128)(2,1)}, bf16[64,576]{1,0:T(8,128)(2,1)S(1)}, u32[]{:S(2)}, u32[]{:S(2)}) collective-permute-start(bf16[64,576]{1,0:T(8,128)(2,1)} %get-tuple-element.24), channel_id=1, source_target_pairs={{4,0},{5,1},{6,2},{7,3},{8,4},{9,5},{10,6},{11,7},{12,8},{13,9},{1... | collective-permute-start | bytes 221192 | tf_op jit(solution)/shard_map/ppermute | solution.py:133
  126.1 2.4 %collective-permute-start.7 = (bf16[64,576]{1,0:T(8,128)(2,1)S(1)}, bf16[64,576]{1,0:T(8,128)(2,1)S(1)}, u32[]{:S(2)}, u32[]{:S(2)}) collective-permute-start(bf16[64,576]{1,0:T(8,128)(2,1)S(1)} %copy-done.51), channel_id=1, source_target_pairs={{8,0},{9,1},{10,2},{11,3},{12,4},{13,5},{14,6},{15,7},{0,8},{1,9},... | collective-permute-start | bytes 221192 | tf_op jit(solution)/shard_map/ppermute | solution.py:133
  128.6 2.0 collective-permute-start.8
  130.6 2.4 %collective-permute-start.9 = (bf16[64,576]{1,0:T(8,128)(2,1)S(1)}, bf16[64,576]{1,0:T(8,128)(2,1)S(1)}, u32[]{:S(2)}, u32[]{:S(2)}) collective-permute-start(bf16[64,576]{1,0:T(8,128)(2,1)S(1)} %copy-done.49), channel_id=1, source_target_pairs={{10,0},{11,1},{8,2},{9,3},{14,4},{15,5},{12,6},{13,7},{2,8},{3,9},... | collective-permute-start | bytes 221192 | tf_op jit(solution)/shard_map/ppermute | solution.py:133
  133.1 1.5 collective-permute-start.45
  135.5 3.9 %collective-permute-done.7.refs_8_ = bf16[64,576]{1,0:T(8,128)(2,1)S(1)} collective-permute-done((bf16[64,576]{1,0:T(8,128)(2,1)S(1)}, bf16[64,576]{1,0:T(8,128)(2,1)S(1)}, u32[]{:S(2)}, u32[]{:S(2)}) %collective-permute-start.7) | collective-permute-done | bytes 73760 | tf_op jit(solution)/shard_map/ppermute | solution.py:133
  141.4 4.0 %collective-permute-done.9.refs_10_ = bf16[64,576]{1,0:T(8,128)(2,1)S(1)} collective-permute-done((bf16[64,576]{1,0:T(8,128)(2,1)S(1)}, bf16[64,576]{1,0:T(8,128)(2,1)S(1)}, u32[]{:S(2)}, u32[]{:S(2)}) %collective-permute-start.9) | collective-permute-done | bytes 73760 | tf_op jit(solution)/shard_map/ppermute | solution.py:133
  147.4 4.4 %collective-permute-done.12.refs_13_ = bf16[64,576]{1,0:T(8,128)(2,1)S(1)} collective-permute-done((bf16[64,576]{1,0:T(8,128)(2,1)S(1)}, bf16[64,576]{1,0:T(8,128)(2,1)S(1)}, u32[]{:S(2)}, u32[]{:S(2)}) %collective-permute-start.12) | collective-permute-done | bytes 73760 | tf_op jit(solution)/shard_map/ppermute | solution.py:133
  151.7 1.5 collective-permute-start.15
  156.0 1.5 collective-permute-start.17
  177.8 1.8 collective-permute-done.27.refs_28_
  179.6 1.7 collective-permute-done.28.refs_29_
  182.8 1.7 copy.71.refs_32_
  185.8 7.8 %attend.4.refs_33_ = bf16[128,16384]{1,0:T(8,128)(2,1)} custom-call(f32[1,2048]{1,0:T(1,128)} %select_n.204.bias_ref, bf16[128,18432]{1,0:T(8,128)(2,1)} %q_ref.7, bf16[64,576]{1,0:T(8,128)(2,1)} %get-tuple-element.20.refs_0_, bf16[64,576]{1,0:T(8,128)(2,1)} %copy-done.2, bf16[64,576]{1,0:T(8,128)(2,1)} %copy-done.3, bf16[64,576]{1,0:T(8,128)(2,1)} %copy-done.4, ...), custom_call_target="tpu_custom_call" | custom-call | tf_op jit(solution)/shard_map/attend/pallas_call | solution.py:104
  193.6 11.7 %attend.5.refs_33_ = bf16[128,16384]{1,0:T(8,128)(2,1)} custom-call(f32[1,2048]{1,0:T(1,128)} %select_n.204.bias_ref, bf16[128,18432]{1,0:T(8,128)(2,1)} %q_ref.7, bf16[64,576]{1,0:T(8,128)(2,1)} %get-tuple-element.20.refs_0_, bf16[64,576]{1,0:T(8,128)(2,1)} %copy-done.2, bf16[64,576]{1,0:T(8,128)(2,1)} %copy-done.3, ...), custom_call_target="tpu_custom_call", output_to_operand_aliasing={{}: (35, {})} | custom-call | tf_op jit(solution)/shard_map/attend/pallas_call | solution.py:104
  205.3 15.5 %attend.6.refs_33_ = bf16[128,16384]{1,0:T(8,128)(2,1)} custom-call(f32[1,2048]{1,0:T(1,128)} %select_n.204.bias_ref, bf16[128,18432]{1,0:T(8,128)(2,1)} %q_ref.7, bf16[64,576]{1,0:T(8,128)(2,1)} %get-tuple-element.20.refs_0_, bf16[64,576]{1,0:T(8,128)(2,1)} %copy-done.2, bf16[64,576]{1,0:T(8,128)(2,1)} %copy-done.3, ...), custom_call_target="tpu_custom_call", output_to_operand_aliasing={{}: (35, {})} | custom-call | tf_op jit(solution)/shard_map/attend/pallas_call | solution.py:104
  220.8 11.7 %attend.7 = bf16[128,16384]{1,0:T(8,128)(2,1)} custom-call(f32[1,2048]{1,0:T(1,128)} %select_n.204.bias_ref, bf16[128,18432]{1,0:T(8,128)(2,1)} %q_ref.7, bf16[64,576]{1,0:T(8,128)(2,1)} %get-tuple-element.20.refs_0_, bf16[64,576]{1,0:T(8,128)(2,1)} %copy-done.2, bf16[64,576]{1,0:T(8,128)(2,1)} %copy-done.3, ...), custom_call_target="tpu_custom_call", output_to_operand_aliasing={{}: (35, {})} | custom-call | tf_op jit(solution)/shard_map/attend/pallas_call | solution.py:104
  232.5 1.7 fusion.5
  (238 shorter events, 49.3 us)
Async XLA Ops:
  3.3 8.7 %collective-permute-start.31 = (bf16[16,3712]{1,0:T(8,128)(2,1)S(1)}, bf16[16,3712]{1,0:T(8,128)(2,1)S(1)}, u32[]{:S(2)}, u32[]{:S(2)}) collective-permute-start(bf16[16,3712]{1,0:T(8,128)(2,1)S(1)} %pad_maximum_fusion.3), channel_id=1, source_target_pairs={{4,0},{5,1},{6,2},{7,3},{8,4},{9,5},{10,6},{11,7},{12,8},{13,9},{1... | collective-permute-start | bytes 356360 | tf_op jit(solution)/shard_map/ppermute | solution.py:28
  8.4 10.3 %collective-permute-start.32 = (bf16[16,3712]{1,0:T(8,128)(2,1)S(1)}, bf16[16,3712]{1,0:T(8,128)(2,1)S(1)}, u32[]{:S(2)}, u32[]{:S(2)}) collective-permute-start(bf16[16,3712]{1,0:T(8,128)(2,1)S(1)} %pad_maximum_fusion.3), channel_id=1, source_target_pairs={{8,0},{9,1},{10,2},{11,3},{12,4},{13,5},{14,6},{15,7},{0,8},{1,9},... | collective-permute-start | bytes 356360 | tf_op jit(solution)/shard_map/ppermute | solution.py:28
  8.4 10.3 %collective-permute-start.33 = (bf16[16,3712]{1,0:T(8,128)(2,1)S(1)}, bf16[16,3712]{1,0:T(8,128)(2,1)S(1)}, u32[]{:S(2)}, u32[]{:S(2)}) collective-permute-start(bf16[16,3712]{1,0:T(8,128)(2,1)S(1)} %pad_maximum_fusion.3), channel_id=1, source_target_pairs={{12,0},{13,1},{14,2},{15,3},{0,4},{1,5},{2,6},{3,7},{4,8},{5,9},{6... | collective-permute-start | bytes 356360 | tf_op jit(solution)/shard_map/ppermute | solution.py:28
  19.6 12.2 %collective-permute-start.35 = (bf16[64,3712]{1,0:T(8,128)(2,1)S(1)}, bf16[64,3712]{1,0:T(8,128)(2,1)S(1)}, u32[]{:S(2)}, u32[]{:S(2)}) collective-permute-start(bf16[64,3712]{1,0:T(8,128)(2,1)S(1)} %pad_maximum_fusion.refs_0_), channel_id=1, source_target_pairs={{2,0},{3,1},{0,2},{1,3},{6,4},{7,5},{4,6},{5,7},{10,8},{11,9},{8,1... | collective-permute-start | bytes 1425416 | tf_op jit(solution)/shard_map/ppermute | solution.py:28
  21.2 12.2 %collective-permute-start.34 = (bf16[64,3712]{1,0:T(8,128)(2,1)S(1)}, bf16[64,3712]{1,0:T(8,128)(2,1)S(1)}, u32[]{:S(2)}, u32[]{:S(2)}) collective-permute-start(bf16[64,3712]{1,0:T(8,128)(2,1)S(1)} %pad_maximum_fusion.refs_0_), channel_id=1, source_target_pairs={{16,0},{0,16},{17,1},{1,17},{18,2},{2,18},{19,3},{3,19},{20,4},{4,... | collective-permute-start | bytes 1425416 | tf_op jit(solution)/shard_map/ppermute | solution.py:28
  22.7 17.5 %collective-permute-start.37 = (bf16[64,3712]{1,0:T(8,128)(2,1)S(1)}, bf16[64,3712]{1,0:T(8,128)(2,1)S(1)}, u32[]{:S(2)}, u32[]{:S(2)}) collective-permute-start(bf16[64,3712]{1,0:T(8,128)(2,1)S(1)} %pad_maximum_fusion.refs_0_), channel_id=1, source_target_pairs={{1,0},{0,1},{3,2},{2,3},{5,4},{4,5},{7,6},{6,7},{9,8},{8,9},{11,10... | collective-permute-start | bytes 1425416 | tf_op jit(solution)/shard_map/ppermute | solution.py:28
  60.0 13.9 %all-to-all-start = ((s32[16,1,2]{2,1,0:T(1,128)}), s32[16,1,2]{2,1,0:T(1,128)S(1)}, u32[]{:S(2)}, u32[]{:S(2)}) async-start(s32[16,1,2]{2,1,0:T(1,128)} %copy.65), calls=%async_computation | async-start | bytes 16384 | tf_op jit(solution)/shard_map/all_to_all | solution.py:154
  69.7 48.5 %collective-permute-start.44 = (bf16[64,1792]{1,0:T(8,128)(2,1)S(1)}, bf16[64,1792]{1,0:T(8,128)(2,1)S(1)}, u32[]{:S(2)}, u32[]{:S(2)}) collective-permute-start(bf16[64,1792]{1,0:T(8,128)(2,1)S(1)} %get-tuple-element.46), channel_id=1, source_target_pairs={{2,0},{3,1},{0,2},{1,3},{6,4},{7,5},{4,6},{5,7},{10,8},{11,9},{8,1... | collective-permute-start | bytes 688136 | tf_op jit(solution)/shard_map/ppermute | solution.py:28
  71.7 49.8 %collective-permute-start.46 = (bf16[64,1792]{1,0:T(8,128)(2,1)S(1)}, bf16[64,1792]{1,0:T(8,128)(2,1)S(1)}, u32[]{:S(2)}, u32[]{:S(2)}) collective-permute-start(bf16[64,1792]{1,0:T(8,128)(2,1)S(1)} %get-tuple-element.47), channel_id=1, source_target_pairs={{16,0},{0,16},{17,1},{1,17},{18,2},{2,18},{19,3},{3,19},{20,4},{4,... | collective-permute-start | bytes 688136 | tf_op jit(solution)/shard_map/ppermute | solution.py:28
  117.1 8.2 %collective-permute-start.1 = (bf16[64,576]{1,0:T(8,128)(2,1)}, bf16[64,576]{1,0:T(8,128)(2,1)S(1)}, u32[]{:S(2)}, u32[]{:S(2)}) collective-permute-start(bf16[64,576]{1,0:T(8,128)(2,1)} %get-tuple-element.22), channel_id=1, source_target_pairs={{2,0},{3,1},{0,2},{1,3},{6,4},{7,5},{4,6},{5,7},{10,8},{11,9},{8,1... | collective-permute-start | bytes 221192 | tf_op jit(solution)/shard_map/ppermute | solution.py:133
  118.3 7.8 %collective-permute-start.2 = (bf16[64,576]{1,0:T(8,128)(2,1)}, bf16[64,576]{1,0:T(8,128)(2,1)S(1)}, u32[]{:S(2)}, u32[]{:S(2)}) collective-permute-start(bf16[64,576]{1,0:T(8,128)(2,1)} %get-tuple-element.23), channel_id=1, source_target_pairs={{3,0},{0,1},{1,2},{2,3},{7,4},{4,5},{5,6},{6,7},{11,8},{8,9},{9,10... | collective-permute-start | bytes 221192 | tf_op jit(solution)/shard_map/ppermute | solution.py:133
  118.3 10.3 %collective-permute-start.3 = (bf16[64,576]{1,0:T(8,128)(2,1)}, bf16[64,576]{1,0:T(8,128)(2,1)S(1)}, u32[]{:S(2)}, u32[]{:S(2)}) collective-permute-start(bf16[64,576]{1,0:T(8,128)(2,1)} %get-tuple-element.24), channel_id=1, source_target_pairs={{4,0},{5,1},{6,2},{7,3},{8,4},{9,5},{10,6},{11,7},{12,8},{13,9},{1... | collective-permute-start | bytes 221192 | tf_op jit(solution)/shard_map/ppermute | solution.py:133
  121.6 9.1 %collective-permute-start.4 = (bf16[64,576]{1,0:T(8,128)(2,1)}, bf16[64,576]{1,0:T(8,128)(2,1)S(1)}, u32[]{:S(2)}, u32[]{:S(2)}) collective-permute-start(bf16[64,576]{1,0:T(8,128)(2,1)} %get-tuple-element.25), channel_id=1, source_target_pairs={{5,0},{6,1},{7,2},{4,3},{9,4},{10,5},{11,6},{8,7},{13,8},{14,9},{1... | collective-permute-start | bytes 221192 | tf_op jit(solution)/shard_map/ppermute | solution.py:133
  124.3 8.7 %collective-permute-start.5 = (bf16[64,576]{1,0:T(8,128)(2,1)}, bf16[64,576]{1,0:T(8,128)(2,1)S(1)}, u32[]{:S(2)}, u32[]{:S(2)}) collective-permute-start(bf16[64,576]{1,0:T(8,128)(2,1)} %get-tuple-element.26), channel_id=1, source_target_pairs={{6,0},{7,1},{4,2},{5,3},{10,4},{11,5},{8,6},{9,7},{14,8},{15,9},{1... | collective-permute-start | bytes 221192 | tf_op jit(solution)/shard_map/ppermute | solution.py:133
  125.3 9.2 %collective-permute-start.6 = (bf16[64,576]{1,0:T(8,128)(2,1)}, bf16[64,576]{1,0:T(8,128)(2,1)S(1)}, u32[]{:S(2)}, u32[]{:S(2)}) collective-permute-start(bf16[64,576]{1,0:T(8,128)(2,1)} %get-tuple-element.27), channel_id=1, source_target_pairs={{7,0},{4,1},{5,2},{6,3},{11,4},{8,5},{9,6},{10,7},{15,8},{12,9},{1... | collective-permute-start | bytes 221192 | tf_op jit(solution)/shard_map/ppermute | solution.py:133
  126.1 13.3 %collective-permute-start.7 = (bf16[64,576]{1,0:T(8,128)(2,1)S(1)}, bf16[64,576]{1,0:T(8,128)(2,1)S(1)}, u32[]{:S(2)}, u32[]{:S(2)}) collective-permute-start(bf16[64,576]{1,0:T(8,128)(2,1)S(1)} %copy-done.51), channel_id=1, source_target_pairs={{8,0},{9,1},{10,2},{11,3},{12,4},{13,5},{14,6},{15,7},{0,8},{1,9},... | collective-permute-start | bytes 221192 | tf_op jit(solution)/shard_map/ppermute | solution.py:133
  128.6 11.9 %collective-permute-start.8 = (bf16[64,576]{1,0:T(8,128)(2,1)S(1)}, bf16[64,576]{1,0:T(8,128)(2,1)S(1)}, u32[]{:S(2)}, u32[]{:S(2)}) collective-permute-start(bf16[64,576]{1,0:T(8,128)(2,1)S(1)} %copy-done.50), channel_id=1, source_target_pairs={{9,0},{10,1},{11,2},{8,3},{13,4},{14,5},{15,6},{12,7},{1,8},{2,9},... | collective-permute-start | bytes 221192 | tf_op jit(solution)/shard_map/ppermute | solution.py:133
  130.6 14.8 %collective-permute-start.9 = (bf16[64,576]{1,0:T(8,128)(2,1)S(1)}, bf16[64,576]{1,0:T(8,128)(2,1)S(1)}, u32[]{:S(2)}, u32[]{:S(2)}) collective-permute-start(bf16[64,576]{1,0:T(8,128)(2,1)S(1)} %copy-done.49), channel_id=1, source_target_pairs={{10,0},{11,1},{8,2},{9,3},{14,4},{15,5},{12,6},{13,7},{2,8},{3,9},... | collective-permute-start | bytes 221192 | tf_op jit(solution)/shard_map/ppermute | solution.py:133
  133.1 31.5 %collective-permute-start.45 = (bf16[64,3584]{1,0:T(8,128)(2,1)S(1)}, bf16[64,3584]{1,0:T(8,128)(2,1)S(1)}, u32[]{:S(2)}, u32[]{:S(2)}) collective-permute-start(bf16[64,3584]{1,0:T(8,128)(2,1)S(1)} %pad_maximum_fusion.1), channel_id=1, source_target_pairs={{16,0},{0,16},{17,1},{1,17},{18,2},{2,18},{19,3},{3,19},{20,4},{4,... | collective-permute-start | bytes 1376264 | tf_op jit(solution)/shard_map/ppermute | solution.py:28
  134.6 30.6 %collective-permute-start.47 = (bf16[64,3584]{1,0:T(8,128)(2,1)}, bf16[64,3584]{1,0:T(8,128)(2,1)S(1)}, u32[]{:S(2)}, u32[]{:S(2)}) collective-permute-start(bf16[64,3584]{1,0:T(8,128)(2,1)} %pad_maximum_fusion.2), channel_id=1, source_target_pairs={{2,0},{3,1},{0,2},{1,3},{6,4},{7,5},{4,6},{5,7},{10,8},{11,9},{8,1... | collective-permute-start | bytes 1376264 | tf_op jit(solution)/shard_map/ppermute | solution.py:28
  146.2 8.2 %collective-permute-start.13 = (bf16[64,576]{1,0:T(8,128)(2,1)S(1)}, bf16[64,576]{1,0:T(8,128)(2,1)S(1)}, u32[]{:S(2)}, u32[]{:S(2)}) collective-permute-start(bf16[64,576]{1,0:T(8,128)(2,1)S(1)} %copy-done.45), channel_id=1, source_target_pairs={{14,0},{15,1},{12,2},{13,3},{2,4},{3,5},{0,6},{1,7},{6,8},{7,9},{4... | collective-permute-start | bytes 221192 | tf_op jit(solution)/shard_map/ppermute | solution.py:133
  147.4 8.6 %collective-permute-start.14 = (bf16[64,576]{1,0:T(8,128)(2,1)S(1)}, bf16[64,576]{1,0:T(8,128)(2,1)S(1)}, u32[]{:S(2)}, u32[]{:S(2)}) collective-permute-start(bf16[64,576]{1,0:T(8,128)(2,1)S(1)} %copy-done.44), channel_id=1, source_target_pairs={{15,0},{12,1},{13,2},{14,3},{3,4},{0,5},{1,6},{2,7},{7,8},{4,9},{5... | collective-permute-start | bytes 221192 | tf_op jit(solution)/shard_map/ppermute | solution.py:133
  159.6 9.3 %collective-permute-start.19 = (bf16[64,576]{1,0:T(8,128)(2,1)S(1)}, bf16[64,576]{1,0:T(8,128)(2,1)S(1)}, u32[]{:S(2)}, u32[]{:S(2)}) collective-permute-start(bf16[64,576]{1,0:T(8,128)(2,1)S(1)} %collective-permute-done.3.refs_4_), channel_id=1, source_target_pairs={{16,0},{0,16},{17,1},{1,17},{18,2},{2,18},{19,3},{3,19},{20,4},{4,... | collective-permute-start | bytes 221192 | tf_op jit(solution)/shard_map/ppermute | solution.py:28
  161.3 8.2 %collective-permute-start.20 = (bf16[64,576]{1,0:T(8,128)(2,1)S(1)}, bf16[64,576]{1,0:T(8,128)(2,1)S(1)}, u32[]{:S(2)}, u32[]{:S(2)}) collective-permute-start(bf16[64,576]{1,0:T(8,128)(2,1)S(1)} %collective-permute-done.4.refs_5_), channel_id=1, source_target_pairs={{16,0},{0,16},{17,1},{1,17},{18,2},{2,18},{19,3},{3,19},{20,4},{4,... | collective-permute-start | bytes 221192 | tf_op jit(solution)/shard_map/ppermute | solution.py:28
  163.1 7.9 %collective-permute-start.21 = (bf16[64,576]{1,0:T(8,128)(2,1)S(1)}, bf16[64,576]{1,0:T(8,128)(2,1)S(1)}, u32[]{:S(2)}, u32[]{:S(2)}) collective-permute-start(bf16[64,576]{1,0:T(8,128)(2,1)S(1)} %collective-permute-done.5.refs_6_), channel_id=1, source_target_pairs={{16,0},{0,16},{17,1},{1,17},{18,2},{2,18},{19,3},{3,19},{20,4},{4,... | collective-permute-start | bytes 221192 | tf_op jit(solution)/shard_map/ppermute | solution.py:28
  171.5 8.0 %collective-permute-start.27 = (bf16[64,576]{1,0:T(8,128)(2,1)S(1)}, bf16[64,576]{1,0:T(8,128)(2,1)S(1)}, u32[]{:S(2)}, u32[]{:S(2)}) collective-permute-start(bf16[64,576]{1,0:T(8,128)(2,1)S(1)} %collective-permute-done.11.refs_12_), channel_id=1, source_target_pairs={{16,0},{0,16},{17,1},{1,17},{18,2},{2,18},{19,3},{3,19},{20,4},{4,... | collective-permute-start | bytes 221192 | tf_op jit(solution)/shard_map/ppermute | solution.py:28
  173.0 8.3 %collective-permute-start.28 = (bf16[64,576]{1,0:T(8,128)(2,1)S(1)}, bf16[64,576]{1,0:T(8,128)(2,1)S(1)}, u32[]{:S(2)}, u32[]{:S(2)}) collective-permute-start(bf16[64,576]{1,0:T(8,128)(2,1)S(1)} %collective-permute-done.12.refs_13_), channel_id=1, source_target_pairs={{16,0},{0,16},{17,1},{1,17},{18,2},{2,18},{19,3},{3,19},{20,4},{4,... | collective-permute-start | bytes 221192 | tf_op jit(solution)/shard_map/ppermute | solution.py:28
  174.3 10.2 %collective-permute-start.29 = (bf16[64,576]{1,0:T(8,128)(2,1)S(1)}, bf16[64,576]{1,0:T(8,128)(2,1)S(1)}, u32[]{:S(2)}, u32[]{:S(2)}) collective-permute-start(bf16[64,576]{1,0:T(8,128)(2,1)S(1)} %collective-permute-done.13.refs_14_), channel_id=1, source_target_pairs={{16,0},{0,16},{17,1},{1,17},{18,2},{2,18},{19,3},{3,19},{20,4},{4,... | collective-permute-start | bytes 221192 | tf_op jit(solution)/shard_map/ppermute | solution.py:28
  176.0 8.6 %collective-permute-start.30 = (bf16[64,576]{1,0:T(8,128)(2,1)S(1)}, bf16[64,576]{1,0:T(8,128)(2,1)S(1)}, u32[]{:S(2)}, u32[]{:S(2)}) collective-permute-start(bf16[64,576]{1,0:T(8,128)(2,1)S(1)} %collective-permute-done.14.refs_15_), channel_id=1, source_target_pairs={{16,0},{0,16},{17,1},{1,17},{18,2},{2,18},{19,3},{3,19},{20,4},{4,... | collective-permute-start | bytes 221192 | tf_op jit(solution)/shard_map/ppermute | solution.py:28
  177.8 54.8 %collective-permute-start.48 = (bf16[16,3584]{1,0:T(8,128)(2,1)}, bf16[16,3584]{1,0:T(8,128)(2,1)}, u32[]{:S(2)}, u32[]{:S(2)}) collective-permute-start(bf16[16,3584]{1,0:T(8,128)(2,1)} %get-tuple-element.50), channel_id=1, source_target_pairs={{12,0},{13,1},{14,2},{15,3},{0,4},{1,5},{2,6},{3,7},{4,8},{5,9},{6... | collective-permute-start | bytes 344072 | tf_op jit(solution)/shard_map/ppermute | solution.py:28
  179.5 53.0 %collective-permute-start.49 = (bf16[16,3584]{1,0:T(8,128)(2,1)}, bf16[16,3584]{1,0:T(8,128)(2,1)}, u32[]{:S(2)}, u32[]{:S(2)}) collective-permute-start(bf16[16,3584]{1,0:T(8,128)(2,1)} %get-tuple-element.52), channel_id=1, source_target_pairs={{8,0},{9,1},{10,2},{11,3},{12,4},{13,5},{14,6},{15,7},{0,8},{1,9},... | collective-permute-start | bytes 344072 | tf_op jit(solution)/shard_map/ppermute | solution.py:28
  181.3 51.3 %collective-permute-start.50 = (bf16[16,3584]{1,0:T(8,128)(2,1)}, bf16[16,3584]{1,0:T(8,128)(2,1)}, u32[]{:S(2)}, u32[]{:S(2)}) collective-permute-start(bf16[16,3584]{1,0:T(8,128)(2,1)} %get-tuple-element.51), channel_id=1, source_target_pairs={{4,0},{5,1},{6,2},{7,3},{8,4},{9,5},{10,6},{11,7},{12,8},{13,9},{1... | collective-permute-start | bytes 344072 | tf_op jit(solution)/shard_map/ppermute | solution.py:28
  (72 other events, 1310.6 us)
where the time goes:
time: 235 us; the launch traced here: 234 us
  Pallas kernels  104 us (44%)
  starting transfers between devices  56 us (24%)
  waiting for transfers between devices  46.5 us (20%)
  local copies, waits for them, and re-layouts  13.5 us (6%)
  other arithmetic  12.5 us (5%)
    pallas_call x4, Pallas kernels, attend(): pl.pallas_call(functools.partial(attention_body, heads=heads, together=to...  46.7 us
    pallas_call x1, Pallas kernels, pick_pages(): pl.pallas_call(functools.partial(pick_body, count=count), in_specs=[pl.Bl...  41.7 us
    ppermute x36, starting transfers between devices, pull(): return lax.ppermute(values, axis, pairs)  36.5 us
    ppermute x36, waiting for transfers between devices, pull(): return lax.ppermute(values, axis, pairs)  30.5 us
    ppermute x15, waiting for transfers between devices, pull_block(): return lax.ppermute(values, 'ep', pairs)  16 us
    pallas_call x1, Pallas kernels, expert_call(): pl.pallas_call(functools.partial(expert_body, places=places, hidden_steps...  15.3 us
    ppermute x15, starting transfers between devices, pull_block(): return lax.ppermute(values, 'ep', pairs)  14.8 us
    another operation x3, other arithmetic  7.31 us
  transfers between devices with their start and end apart: 52, of which 19 were waited for; matrix products, arithmetic and copies ran while one was open for 8% of the time, Pallas kernels for 38%

commit v1 on v0

--- a/solution.py
+++ b/solution.py
@@ -18,18 +18,22 @@
 neg_large = -1e30
 
 
-def pull(values, axis, stride, size, shift):
+def partner(pos, shift, size):
+    return pos ^ shift if size & (size - 1) == 0 else (pos + shift) % size
+
+
+def pull(values, axis, stride, size, shift, back=False):
     total = lax.axis_size(axis)
     pairs = []
     for dst in range(total):
         pos = (dst // stride) % size
-        src = dst + (((pos + shift) % size) - pos) * stride
-        pairs.append((src, dst))
+        src = dst + (partner(pos, shift, size) - pos) * stride
+        pairs.append((dst, src) if back else (src, dst))
     return lax.ppermute(values, axis, pairs)
 
 
 def push(values, axis, stride, size, shift):
-    return pull(values, axis, stride, size, size - shift)
+    return pull(values, axis, stride, size, shift, back=True)
 
 
 def gather_stages():
@@ -46,9 +50,11 @@
     return [stage for stage in stages if stage[2] > 1]
 
 
-def attention_body(bias_ref, q_ref, *refs, heads, together, pieces, aliased):
+def attention_body(
+    number_ref, length_ref, q_ref, *refs, heads, together, pieces, aliased
+):
     piece_refs = refs[:pieces]
-    o_ref, k_ref, sem = refs[pieces + aliased :]
+    o_ref, k_ref, bias_ref, sem = refs[pieces + aliased :]
     tokens = q_ref.shape[0]
     keys = k_ref.shape[0]
     prefix = bias_ref.shape[1]
@@ -64,6 +70,13 @@
             copy.start()
             copies.append(copy)
             start += rows
+        lane = lax.broadcasted_iota(jnp.int32, (1, 2 * PAGE), 1)
+        for pair in range(prefix // (2 * PAGE)):
+            low = number_ref[2 * pair] * PAGE
+            high = number_ref[2 * pair + 1] * PAGE - PAGE
+            position = lane + jnp.where(lane < PAGE, low, high)
+            seen = jnp.where(position < length_ref[0], 0.0, neg_large)
+            bias_ref[:, 2 * PAGE * pair : 2 * PAGE * (pair + 1)] = seen.astype(jnp.float32)
         for copy in copies:
             copy.wait()
 
@@ -92,10 +105,12 @@
             o_ref[:, h * LATENT : (h + 1) * LATENT] = part.astype(jnp.bfloat16)
 
 
-def attend(queries, pieces, bias, start, count, heads, so_far=None):
+def attend(queries, pieces, numbers, length, start, count, heads, so_far=None):
     tokens = queries.shape[0]
     head_count = queries.shape[1] // KEY
     keys = sum(piece.shape[0] for piece in pieces)
+    prefix = numbers.shape[0] * PAGE
+    scalars = pl.BlockSpec(memory_space=pltpu.SMEM)
     together = 4 if heads % 4 == 0 and keys <= 2304 else 2
     offset = start // heads
     aliased = 0 if so_far is None else 1
@@ -107,7 +122,8 @@
         ),
         grid=(count // heads,),
         in_specs=[
-            pl.BlockSpec(bias.shape, lambda i: (0, 0)),
+            scalars,
+            scalars,
             pl.BlockSpec((tokens, heads * KEY), lambda i: (0, i + offset)),
             *[anywhere] * (len(pieces) + aliased),
         ],
@@ -115,12 +131,13 @@
         out_shape=jax.ShapeDtypeStruct((tokens, head_count * LATENT), jnp.bfloat16),
         scratch_shapes=[
             pltpu.VMEM((keys, KEY), jnp.bfloat16),
+            pltpu.VMEM((1, prefix), jnp.float32),
             pltpu.SemaphoreType.DMA((len(pieces),)),
         ],
-        input_output_aliases={2 + len(pieces): 0} if aliased else {},
+        input_output_aliases={3 + len(pieces): 0} if aliased else {},
         compiler_params=pltpu.CompilerParams(vmem_limit_bytes=56 << 20),
         name="attend",
-    )(bias, queries, *pieces, *extra)
+    )(numbers, length, queries, *pieces, *extra)
 
 
 def pull_block(values, a, b, inner):
@@ -128,12 +145,12 @@
     outer = total // inner
     pairs = []
     for dst in range(total):
-        src = (dst // inner + a) % outer * inner + (dst % inner + b) % inner
+        src = partner(dst // inner, a, outer) * inner + partner(dst % inner, b, inner)
         pairs.append((src, dst))
     return lax.ppermute(values, "ep", pairs)
 
 
-def fetch_pages(page_pool, page_owner, page_slot, length):
+def fetch_pages(page_pool, page_owner, page_slot):
     ep_size = lax.axis_size("ep")
     dp_size = lax.axis_size("dp")
     me = lax.axis_index("ep")
@@ -152,60 +169,85 @@
     )
     wanted = jnp.sum(jnp.where(match, page_slot[0][None, None, :], 0), axis=2)
     asked = lax.all_to_all(wanted, "ep", split_axis=0, concat_axis=0, tiled=True)
+    first = (plane * own_ranks) % ranks if planes > 1 else 0
+    pool = page_pool.reshape(page_pool.shape[0], PAGE, KEY)
+    where = jnp.stack([me, jnp.asarray(first, jnp.int32)]).astype(jnp.int32)
+    chosen = pick_pages(where, asked, pool, inner, own_ranks)
+    groups = []
+    for a in range(outer):
+        pieces = []
+        for b in range(inner):
+            step = a * inner + b
+            pieces.append(pull_block(chosen[step], a, b, inner) if step else chosen[0])
+        groups.append(pack_pages(pieces))
+    blocks = list(groups)
+    for shift in range(1, planes):
+        for a in range(outer):
+            blocks.append(pull(groups[a], "dp", 1, dp_size, shift))
     steps = jnp.arange(ep_size, dtype=jnp.int32)
-    serve = (me // inner - steps // inner) % outer * inner + (me % inner - steps % inner) % inner
-    hear = (me // inner + steps // inner) % outer * inner + (me % inner + steps % inner) % inner
-    slots = asked[serve]
-    first = (plane * own_ranks) % ranks if planes > 1 else 0
-    mine = lax.dynamic_slice_in_dim(slots, first, own_ranks, axis=1)
-    pool = page_pool.reshape(page_pool.shape[0], PAGE, KEY)
-    chosen = pick_pages(pool, mine, ep_size, own_ranks)
-    pieces = []
-    for step in range(ep_size):
-        a, b = step // inner, step % inner
-        pieces.append(pull_block(chosen[step], a, b, inner) if step else chosen[step])
-    blocks = list(pieces)
-    for shift in range(1, planes):
-        for step in range(ep_size):
-            blocks.append(pull(pieces[step], "dp", 1, dp_size, shift))
-    number = jnp.sum(jnp.where(match, page_id[None, None, :], 0), axis=2)
-    number = jnp.where(jnp.any(match, axis=2), number, pages)[hear]
-    by_plane = number.reshape(ep_size, planes, own_ranks).transpose(1, 0, 2)
-    if planes > 1:
-        by_plane = by_plane[(plane + jnp.arange(planes, dtype=jnp.int32)) % planes]
-    position = by_plane.reshape(-1)[:, None] * PAGE + jnp.arange(PAGE, dtype=jnp.int32)[None, :]
-    seen = (position < length) & (position < pages * PAGE)
-    bias = jnp.where(seen, 0.0, neg_large).astype(jnp.float32).reshape(1, -1)
-    return blocks, bias
-
-
-def pick_body(slots_ref, pool_ref, *refs, count):
-    outs = refs[:-1]
-    sem = refs[-1]
-    copies = []
+    group, place = me // inner, me % inner
+    hear = partner(group, steps // inner, outer) * inner + partner(place, steps % inner, inner)
+    turn = partner(plane, jnp.arange(planes, dtype=jnp.int32), planes) if planes > 1 else 0
+    order = turn * own_ranks + jnp.arange(own_ranks, dtype=jnp.int32)[:, None]
+    order = order.T.reshape(planes, 1, own_ranks)
+    seat = page_owner[0] + page_id // ep_size * ep_size
+    place_of = (hear[None, :, None] + order * ep_size).reshape(-1, 1)
+    hit = place_of == seat[None, :]
+    numbers = pages + jnp.sum(jnp.where(hit, page_id[None, :] - pages, 0), axis=1)
+    return blocks, numbers
+
+
+def pack_body(*refs):
+    start = 0
+    for piece in refs[:-1]:
+        rows = piece.shape[0]
+        refs[-1][start : start + rows] = piece[...]
+        start += rows
+
+
+def pack_pages(pieces):
+    if len(pieces) == 1:
+        return pieces[0]
+    rows = sum(piece.shape[0] for piece in pieces)
+    whole = pl.BlockSpec(memory_space=pltpu.VMEM)
+    return pl.pallas_call(
+        pack_body,
+        in_specs=[whole] * len(pieces),
+        out_specs=whole,
+        out_shape=jax.ShapeDtypeStruct((rows, pieces[0].shape[1]), pieces[0].dtype),
+        name="pack",
+    )(*pieces)
+
+
+def pick_body(where_ref, asked_ref, pool_ref, *outs, inner, count):
+    steps = len(outs)
+    me = where_ref[0]
     for n, out in enumerate(outs):
+        low, high = n % inner, n // inner
+        if inner & (inner - 1) == 0:
+            place = (me % inner) ^ low
+        else:
+            place = (me % inner + inner - low) % inner
+        outer = steps // inner
+        if outer & (outer - 1) == 0:
+            group = (me // inner) ^ high
+        else:
+            group = (me // inner + outer - high) % outer
         for r in range(count):
-            copies.append(
-                pltpu.make_async_copy(
-                    pool_ref.at[slots_ref[n, r]], out.at[pl.ds(r * PAGE, PAGE)], sem.at[n, r]
-                )
-            )
-    for copy in copies:
-        copy.start()
-    for copy in copies:
-        copy.wait()
-
-
-def pick_pages(pool, slots, steps, count):
-    anywhere = pl.BlockSpec(memory_space=pl.ANY)
+            slot = asked_ref[group * inner + place, where_ref[1] + r]
+            out[r * PAGE : (r + 1) * PAGE] = pool_ref[slot]
+
+
+def pick_pages(where, asked, pool, inner, count):
+    steps = asked.shape[0]
+    scalars = pl.BlockSpec(memory_space=pltpu.SMEM)
     return pl.pallas_call(
-        functools.partial(pick_body, count=count),
-        in_specs=[pl.BlockSpec(memory_space=pltpu.SMEM), anywhere],
-        out_specs=[anywhere] * steps,
+        functools.partial(pick_body, inner=inner, count=count),
+        in_specs=[scalars, scalars, pl.BlockSpec(memory_space=pltpu.VMEM)],
+        out_specs=[pl.BlockSpec(memory_space=pltpu.VMEM)] * steps,
         out_shape=[jax.ShapeDtypeStruct((count * PAGE, KEY), pool.dtype)] * steps,
-        scratch_shapes=[pltpu.SemaphoreType.DMA((steps, count))],
         name="pick",
-    )(slots, pool)
+    )(where, asked, pool)
 
 
 def split_exact(values):
@@ -253,81 +295,84 @@
     return kept.astype(jnp.bfloat16)
 
 
-def expert_body(weight_ref, *refs, places, hidden_steps):
+def expert_body(me_ref, *refs, places, hidden_steps, experts, features):
     pieces = refs[: len(places)]
-    gate_ref, up_ref, down_ref, keep_ref, send_ref, x_ref, acc_ref, sem = refs[len(places) :]
+    gate_ref, up_ref, down_ref, keep_ref, send_ref, x_ref, h_ref, w_ref, sem = refs[len(places) :]
     step = pl.program_id(0)
 
     @pl.when(step == 0)
     def load_rows():
         copies = []
-        for n, (piece, (row, lane, lanes)) in enumerate(zip(pieces, places, strict=True)):
-            rows = piece.shape[0]
+        for n, (piece, (row, lane)) in enumerate(zip(pieces, places, strict=True)):
+            rows, lanes = piece.shape
             copies.append(
                 pltpu.make_async_copy(
-                    piece.at[:, pl.ds(0, lanes)],
-                    x_ref.at[pl.ds(row, rows), pl.ds(lane, lanes)],
-                    sem.at[n],
+                    piece, x_ref.at[pl.ds(row, rows), pl.ds(lane, lanes)], sem.at[n]
                 )
             )
         for copy in copies:
             copy.start()
         for copy in copies:
             copy.wait()
-
-    x = x_ref[...]
-    gate = jnp.dot(x, gate_ref[...], preferred_element_type=jnp.float32)
-    up = jnp.dot(x, up_ref[...], preferred_element_type=jnp.float32)
-    hidden = (gate / (1.0 + jnp.exp(-gate)) * up).astype(jnp.bfloat16)
-    part = jnp.dot(hidden, down_ref[...], preferred_element_type=jnp.float32)
-
-    @pl.when(step == 0)
-    def begin():
-        acc_ref[...] = part
-
-    @pl.when((step > 0) & (step < hidden_steps - 1))
-    def add():
-        acc_ref[...] += part
-
-    @pl.when(step == hidden_steps - 1)
-    def finish():
-        total = (acc_ref[...] + part) * weight_ref[...]
+        tags = x_ref[:, features:].astype(jnp.float32)
+        lane = lax.broadcasted_iota(jnp.int32, tags.shape, 1)
+        mine = (lane % experts == me_ref[0]) & (lane < 3 * experts)
+        w_ref[...] = jnp.sum(jnp.where(mine, tags, 0.0), axis=1, keepdims=True)
+
+    block = gate_ref.shape[1]
+    for n in range(hidden_steps):
+
+        @pl.when(step == n)
+        def first_layer(n=n):
+            x = x_ref[:, :features]
+            gate = jnp.dot(x, gate_ref[...], preferred_element_type=jnp.float32)
+            up = jnp.dot(x, up_ref[...], preferred_element_type=jnp.float32)
+            hidden = gate / (1.0 + jnp.exp(-gate)) * up
+            h_ref[:, n * block : (n + 1) * block] = hidden.astype(jnp.bfloat16)
+
+    @pl.when(step >= hidden_steps)
+    def second_layer():
+        part = jnp.dot(h_ref[...], down_ref[...], preferred_element_type=jnp.float32)
+        total = part * w_ref[...]
         half = keep_ref.shape[0]
         keep_ref[...] = total[:half]
         send_ref[...] = total[half:].astype(jnp.bfloat16)
 
 
-def expert_call(weight, pieces, places, w_gate, w_up, w_down):
-    rows = weight.shape[0]
+def expert_call(me, pieces, places, rows, experts, w_gate, w_up, w_down):
     features, hidden = w_gate.shape
+    width = pieces[0].shape[1]
     block = 256
+    wide = 512 if features % 512 == 0 else 128
+    steps = hidden // block
     anywhere = pl.BlockSpec(memory_space=pl.ANY)
+    outs = pl.BlockSpec((rows // 2, wide), lambda i: (0, jnp.maximum(i - steps, 0)))
     return pl.pallas_call(
-        functools.partial(expert_body, places=places, hidden_steps=hidden // block),
-        grid=(hidden // block,),
+        functools.partial(
+            expert_body, places=places, hidden_steps=steps, experts=experts, features=features
+        ),
+        grid=(steps + features // wide,),
         in_specs=[
-            pl.BlockSpec((rows, 1), lambda i: (0, 0)),
+            pl.BlockSpec(memory_space=pltpu.SMEM),
             *[anywhere] * len(pieces),
-            pl.BlockSpec((features, block), lambda i: (0, i)),
-            pl.BlockSpec((features, block), lambda i: (0, i)),
-            pl.BlockSpec((block, features), lambda i: (i, 0)),
+            pl.BlockSpec((features, block), lambda i: (0, jnp.minimum(i, steps - 1))),
+            pl.BlockSpec((features, block), lambda i: (0, jnp.minimum(i, steps - 1))),
+            pl.BlockSpec((hidden, wide), lambda i: (0, jnp.maximum(i - steps, 0))),
         ],
-        out_specs=[
-            pl.BlockSpec((rows // 2, features), lambda i: (0, 0)),
-            pl.BlockSpec((rows // 2, features), lambda i: (0, 0)),
-        ],
+        out_specs=[outs, outs],
         out_shape=[
             jax.ShapeDtypeStruct((rows // 2, features), jnp.float32),
             jax.ShapeDtypeStruct((rows // 2, features), jnp.bfloat16),
         ],
         scratch_shapes=[
-            pltpu.VMEM((rows, features), jnp.bfloat16),
-            pltpu.VMEM((rows, features), jnp.float32),
+            pltpu.VMEM((rows, width), jnp.bfloat16),
+            pltpu.VMEM((rows, hidden), jnp.bfloat16),
+            pltpu.VMEM((rows, 1), jnp.float32),
             pltpu.SemaphoreType.DMA((len(pieces),)),
         ],
         compiler_params=pltpu.CompilerParams(vmem_limit_bytes=58 << 20),
         name="expert",
-    )(weight, *pieces, w_gate, w_up, w_down)
+    )(me, *pieces, w_gate, w_up, w_down)
 
 
 def can_square(tokens, hidden):
@@ -357,24 +402,17 @@
     both_a = pull(by_x[:, :left], "ep", 2, 2, 1)
     both_b = pull(by_y[:, left:], "dp", 1, 2, 1)
     near = [own, by_x, by_y, both_a, both_b]
-    partner = []
+    across = []
     for piece in near:
-        partner.append(pull(piece, "ep", 1, 2, 1))
+        across.append(pull(piece, "ep", 1, 2, 1))
     block = own.shape[0]
     places = []
     for base in (0, 4 * block):
-        places += [(base + n * block, 0, features) for n in range(3)]
-        places += [(base + 3 * block, 0, left), (base + 3 * block, left, features - left)]
-    tags = []
-    for group in (near, partner):
-        tags += [piece[:, features:] for piece in group[:3]] + [group[4][:, features - left :]]
-    parts = jnp.concatenate(tags, axis=0)[:, : 3 * ep_size].astype(jnp.float32)
-    parts = parts.reshape(-1, 3, ep_size)
-    here = (experts == lax.axis_index("ep"))[None, None, :]
-    parts = jnp.sum(jnp.where(here, parts, 0.0), axis=2)
-    weight = (parts[:, 0] + parts[:, 1] + parts[:, 2])[:, None]
+        places += [(base + n * block, 0) for n in range(3)]
+        places += [(base + 3 * block, 0), (base + 3 * block, left)]
+    me = lax.axis_index("ep").astype(jnp.int32).reshape(1)
     keep, send = expert_call(
-        weight, near + partner, tuple(places), w_gate[0], w_up[0], w_down[0]
+        me, near + across, tuple(places), 8 * block, ep_size, w_gate[0], w_up[0], w_down[0]
     )
     got = pull(send, "ep", 1, 2, 1)
     yield None
@@ -414,13 +452,13 @@
     w_up,
     w_down,
 ):
-    pieces, bias = fetch_pages(page_pool, page_owner, page_slot, prefix_len[0])
+    pieces, numbers = fetch_pages(page_pool, page_owner, page_slot)
     pieces = pieces + [suffix_latent]
     moe_args = (moe_input, expert_ids, gate_weights, w_gate, w_up, w_down)
     head_count = queries.shape[1] // KEY
     if not can_square(moe_input.shape[0], w_gate.shape[2]):
         moe_output = experts_staged(*moe_args)
-        return (attend(queries, pieces, bias, 0, head_count, 2), moe_output)
+        return (attend(queries, pieces, numbers, prefix_len, 0, head_count, 2), moe_output)
     stages = experts_square(*moe_args)
     heads = 4
     steps = head_count // heads
@@ -431,7 +469,7 @@
         start, count = cuts[n] * heads, (cuts[n + 1] - cuts[n]) * heads
         if count:
             attn_context = attend(
-                queries, pieces, bias, start, count, heads, attn_context
+                queries, pieces, numbers, prefix_len, start, count, heads, attn_context
             )
     moe_output = next(stages)
     return (attn_context, moe_output)

time: 235 us -> 210 us (0.89)
  the two profiles are of different devices: /device:TPU:0 before, /device:TPU:15 now
where the time goes in v1:
time: 210 us; the launch traced here: 206 us
  Pallas kernels  71.1 us (34%)
  waiting for transfers between devices  65.7 us (31%)
  starting transfers between devices  48.5 us (23%)
  other arithmetic  11.4 us (5%)
  local copies, waits for them, and re-layouts  7.52 us (4%)
    ppermute x24, waiting for transfers between devices, pull(): return lax.ppermute(values, axis, pairs)  48.7 us
    pallas_call x4, Pallas kernels, attend(): pl.pallas_call(functools.partial(attention_body, heads=heads, together=to...  46.1 us
    ppermute x24, starting transfers between devices, pull(): return lax.ppermute(values, axis, pairs)  22 us
    ppermute x15, starting transfers between devices, pull_block(): return lax.ppermute(values, 'ep', pairs)  20.3 us
    pallas_call x1, Pallas kernels, expert_call(): pl.pallas_call(functools.partial(expert_body, places=places, hidden_steps...  15.7 us
    ppermute x15, waiting for transfers between devices, pull_block(): return lax.ppermute(values, 'ep', pairs)  15.5 us
    another operation x3, other arithmetic  7.14 us
    pallas_call x4, Pallas kernels, pack_pages(): pl.pallas_call(pack_body, in_specs=[whole] * len(pieces), out_specs=whole...  7.06 us
  transfers between devices with their start and end apart: 40, of which 18 were waited for; matrix products, arithmetic and copies ran while one was open for 4% of the time, Pallas kernels for 27%

profile of v1, /device:TPU:15, one launch (start us, length us, event | category | flops | bytes accessed | tf_op | source)
XLA Modules:
  0.0 206.0 jit_solution(15445718159946974825)
XLA Ops:
  3.5 2.3 %collective-permute-start.20 = (bf16[16,3712]{1,0:T(8,128)(2,1)S(1)}, bf16[16,3712]{1,0:T(8,128)(2,1)S(1)}, u32[]{:S(2)}, u32[]{:S(2)}) collective-permute-start(bf16[16,3712]{1,0:T(8,128)(2,1)S(1)} %pad_maximum_fusion.3), channel_id=1, source_target_pairs={{8,0},{9,1},{10,2},{11,3},{12,4},{13,5},{14,6},{15,7},{0,8},{1,9},... | collective-permute-start | bytes 356360 | tf_op jit(solution)/shard_map/ppermute | solution.py:32
  7.4 3.6 %collective-permute-done.20 = bf16[16,3712]{1,0:T(8,128)(2,1)S(1)} collective-permute-done((bf16[16,3712]{1,0:T(8,128)(2,1)S(1)}, bf16[16,3712]{1,0:T(8,128)(2,1)S(1)}, u32[]{:S(2)}, u32[]{:S(2)}) %collective-permute-start.20) | collective-permute-done | bytes 118816 | tf_op jit(solution)/shard_map/ppermute | solution.py:32
  11.0 4.9 %collective-permute-done.21 = bf16[16,3712]{1,0:T(8,128)(2,1)S(1)} collective-permute-done((bf16[16,3712]{1,0:T(8,128)(2,1)S(1)}, bf16[16,3712]{1,0:T(8,128)(2,1)S(1)}, u32[]{:S(2)}, u32[]{:S(2)}) %collective-permute-start.21) | collective-permute-done | bytes 118816 | tf_op jit(solution)/shard_map/ppermute | solution.py:32
  17.4 10.0 %collective-permute-done.23.refs_2_ = bf16[64,3712]{1,0:T(8,128)(2,1)S(1)} collective-permute-done((bf16[64,3712]{1,0:T(8,128)(2,1)S(1)}, bf16[64,3712]{1,0:T(8,128)(2,1)S(1)}, u32[]{:S(2)}, u32[]{:S(2)}) %collective-permute-start.23) | collective-permute-done | bytes 475168 | tf_op jit(solution)/shard_map/ppermute | solution.py:32
  27.7 3.1 %collective-permute-start.26 = (bf16[64,3712]{1,0:T(8,128)(2,1)S(1)}, bf16[64,3712]{1,0:T(8,128)(2,1)S(1)}, u32[]{:S(2)}, u32[]{:S(2)}) collective-permute-start(bf16[64,3712]{1,0:T(8,128)(2,1)S(1)} %pad_maximum_fusion.refs_0_), channel_id=1, source_target_pairs={{1,0},{0,1},{3,2},{2,3},{5,4},{4,5},{7,6},{6,7},{9,8},{8,9},{11,10... | collective-permute-start | bytes 1425416 | tf_op jit(solution)/shard_map/ppermute | solution.py:32
  32.6 3.9 %collective-permute-start.30 = (bf16[64,1920]{1,0:T(8,128)(2,1)S(1)}, bf16[64,1920]{1,0:T(8,128)(2,1)S(1)}, u32[]{:S(2)}, u32[]{:S(2)}) collective-permute-start(bf16[64,1920]{1,0:T(8,128)(2,1)S(1)} %collective-permute-done.25.refs_4_), channel_id=1, source_target_pairs={{1,0},{0,1},{3,2},{2,3},{5,4},{4,5},{7,6},{6,7},{9,8},{8,9},{11,10... | collective-permute-start | bytes 737288 | tf_op jit(solution)/shard_map/ppermute | solution.py:32
  36.5 2.1 %collective-permute-done.24.refs_3_ = bf16[64,1792]{1,0:T(8,128)(2,1)} collective-permute-done((bf16[64,1792]{1,0:T(8,128)(2,1)S(1)}, bf16[64,1792]{1,0:T(8,128)(2,1)}, u32[]{:S(2)}, u32[]{:S(2)}) %collective-permute-start.24) | collective-permute-done | bytes 229408 | tf_op jit(solution)/shard_map/ppermute | solution.py:32
  42.1 15.7 %expert.1 = (f32[256,3584]{1,0:T(8,128)}, bf16[256,3584]{1,0:T(8,128)(2,1)}) custom-call(s32[1]{0:T(128)} %bitcast.1.me_ref, bf16[64,3712]{1,0:T(8,128)(2,1)} %copy-done.4, bf16[64,3712]{1,0:T(8,128)(2,1)} %copy-done.6, bf16[64,3712]{1,0:T(8,128)(2,1)} %copy-done.5, bf16[64,1792]{1,0:T(8,128)(2,1)} %collective-permute-done.24.refs_3_, ...), custom_call_target="tpu_custom_call" | custom-call | tf_op jit(solution)/shard_map/expert/pallas_call | solution.py:350
  58.2 3.6 %collective-permute-done.31 = bf16[256,3584]{1,0:T(8,128)(2,1)S(1)} collective-permute-done((bf16[256,3584]{1,0:T(8,128)(2,1)}, bf16[256,3584]{1,0:T(8,128)(2,1)S(1)}, u32[]{:S(2)}, u32[]{:S(2)}) %collective-permute-start.31) | collective-permute-done | bytes 1835040 | tf_op jit(solution)/shard_map/ppermute | solution.py:32
  61.8 4.6 %fusion.21 = (bf16[256,3584]{1,0:T(8,128)(2,1)S(1)}, f32[256,3584]{1,0:T(8,128)}) fusion(f32[256,3584]{1,0:T(8,128)} %get-tuple-element.36, bf16[256,3584]{1,0:T(8,128)(2,1)S(1)} %collective-permute-done.31), kind=kLoop, calls=%fused_computation.55 | loop fusion | flops 2752512 | bytes 11010048 | tf_op jit(solution)/shard_map/convert.10
  68.8 6.2 %all-to-all-start = ((s32[16,1,2]{2,1,0:T(1,128)}), s32[16,1,2]{2,1,0:T(1,128)S(1)}, u32[]{:S(2)}, u32[]{:S(2)}) async-start(s32[16,1,2]{2,1,0:T(1,128)} %copy.33), calls=%async_computation | async-start | bytes 16384 | tf_op jit(solution)/shard_map/all_to_all | solution.py:171
  79.4 2.3 %pick.1 = (bf16[64,576]{1,0:T(8,128)(2,1)}, bf16[64,576]{1,0:T(8,128)(2,1)}, bf16[64,576]{1,0:T(8,128)(2,1)}, bf16[64,576]{1,0:T(8,128)(2,1)}, bf16[64,576]{1,0:...) custom-call(s32[2]{0:T(128)} %pad_add_fusion.where_ref, ...), custom_call_target="tpu_custom_call" | custom-call | tf_op jit(solution)/shard_map/pick/pallas_call | solution.py:244
  82.1 2.0 collective-permute-start.12
  87.8 5.5 %collective-permute-start.14 = (bf16[64,576]{1,0:T(8,128)(2,1)S(1)}, bf16[64,576]{1,0:T(8,128)(2,1)S(1)}, u32[]{:S(2)}, u32[]{:S(2)}) collective-permute-start(bf16[64,576]{1,0:T(8,128)(2,1)S(1)} %copy-done.42), channel_id=1, source_target_pairs={{15,0},{14,1},{13,2},{12,3},{11,4},{10,5},{9,6},{8,7},{7,8},{6,9},... | collective-permute-start | bytes 221192 | tf_op jit(solution)/shard_map/ppermute | solution.py:150
  96.7 7.4 %collective-permute-done.14.refs_3_ = bf16[64,576]{1,0:T(8,128)(2,1)S(1)} collective-permute-done((bf16[64,576]{1,0:T(8,128)(2,1)S(1)}, bf16[64,576]{1,0:T(8,128)(2,1)S(1)}, u32[]{:S(2)}, u32[]{:S(2)}) %collective-permute-start.14) | collective-permute-done | bytes 73760 | tf_op jit(solution)/shard_map/ppermute | solution.py:150
  104.1 1.7 collective-permute-start.8
  110.4 2.4 %collective-permute-start.4 = (bf16[64,576]{1,0:T(8,128)(2,1)}, bf16[64,576]{1,0:T(8,128)(2,1)S(1)}, u32[]{:S(2)}, u32[]{:S(2)}) collective-permute-start(bf16[64,576]{1,0:T(8,128)(2,1)} %get-tuple-element.25), channel_id=1, source_target_pairs={{5,0},{4,1},{7,2},{6,3},{1,4},{0,5},{3,6},{2,7},{13,8},{12,9},{15,... | collective-permute-start | bytes 221192 | tf_op jit(solution)/shard_map/ppermute | solution.py:150
  112.8 2.7 %collective-permute-start.5 = (bf16[64,576]{1,0:T(8,128)(2,1)S(1)}, bf16[64,576]{1,0:T(8,128)(2,1)S(1)}, u32[]{:S(2)}, u32[]{:S(2)}) collective-permute-start(bf16[64,576]{1,0:T(8,128)(2,1)S(1)} %copy-done.36), channel_id=1, source_target_pairs={{6,0},{7,1},{4,2},{5,3},{2,4},{3,5},{0,6},{1,7},{14,8},{15,9},{12,... | collective-permute-start | bytes 221192 | tf_op jit(solution)/shard_map/ppermute | solution.py:150
  116.5 2.7 %collective-permute-done.5.refs_2_ = bf16[64,576]{1,0:T(8,128)(2,1)S(1)} collective-permute-done((bf16[64,576]{1,0:T(8,128)(2,1)S(1)}, bf16[64,576]{1,0:T(8,128)(2,1)S(1)}, u32[]{:S(2)}, u32[]{:S(2)}) %collective-permute-start.5) | collective-permute-done | bytes 73760 | tf_op jit(solution)/shard_map/ppermute | solution.py:150
  119.2 1.8 collective-permute-done.6.refs_3_
  122.2 1.8 pack.7.refs_3_
  124.0 1.8 pack.6.refs_2_
  125.8 1.8 pack.5.refs_1_
  129.8 1.8 pack.4.refs_0_
  134.9 2.7 %collective-permute-done.18.refs_7_ = bf16[256,576]{1,0:T(8,128)(2,1)S(1)} collective-permute-done((bf16[256,576]{1,0:T(8,128)(2,1)}, bf16[256,576]{1,0:T(8,128)(2,1)S(1)}, u32[]{:S(2)}, u32[]{:S(2)}) %collective-permute-start.18) | collective-permute-done | bytes 294944 | tf_op jit(solution)/shard_map/ppermute | solution.py:32
  138.7 5.9 %collective-permute-done.17.refs_6_ = bf16[256,576]{1,0:T(8,128)(2,1)S(1)} collective-permute-done((bf16[256,576]{1,0:T(8,128)(2,1)}, bf16[256,576]{1,0:T(8,128)(2,1)S(1)}, u32[]{:S(2)}, u32[]{:S(2)}) %collective-permute-start.17) | collective-permute-done | bytes 294944 | tf_op jit(solution)/shard_map/ppermute | solution.py:32
  145.3 6.2 %collective-permute-done.16.refs_5_ = bf16[256,576]{1,0:T(8,128)(2,1)S(1)} collective-permute-done((bf16[256,576]{1,0:T(8,128)(2,1)}, bf16[256,576]{1,0:T(8,128)(2,1)S(1)}, u32[]{:S(2)}, u32[]{:S(2)}) %collective-permute-start.16) | collective-permute-done | bytes 294944 | tf_op jit(solution)/shard_map/ppermute | solution.py:32
  151.6 6.8 %collective-permute-done.15.refs_4_ = bf16[256,576]{1,0:T(8,128)(2,1)S(1)} collective-permute-done((bf16[256,576]{1,0:T(8,128)(2,1)}, bf16[256,576]{1,0:T(8,128)(2,1)S(1)}, u32[]{:S(2)}, u32[]{:S(2)}) %collective-permute-start.15) | collective-permute-done | bytes 294944 | tf_op jit(solution)/shard_map/ppermute | solution.py:32
  159.1 7.5 %attend.4.refs_9_ = bf16[128,16384]{1,0:T(8,128)(2,1)} custom-call(s32[32]{0:T(128)} %broadcast_add_fusion.number_ref, s32[1]{0:T(128)S(6)} %copy.46.length_ref, bf16[128,18432]{1,0:T(8,128)(2,1)} %q_ref.7, bf16[256,576]{1,0:T(8,128)(2,1)} %pack.4.refs_0_, bf16[256,576]{1,0:T(8,128)(2,1)} %pack.5.refs_1_, bf16[256,576]{1,0:T(8,128)(2,1)} %pack.6.refs_2_, ...), custom_call_target="tpu_custom_call" | custom-call | tf_op jit(solution)/shard_map/attend/pallas_call | solution.py:119
  166.7 11.5 %attend.5.refs_9_ = bf16[128,16384]{1,0:T(8,128)(2,1)} custom-call(s32[32]{0:T(128)} %broadcast_add_fusion.number_ref, s32[1]{0:T(128)S(6)} %copy.46.length_ref, bf16[128,18432]{1,0:T(8,128)(2,1)} %q_ref.7, bf16[256,576]{1,0:T(8,128)(2,1)} %pack.4.refs_0_, bf16[256,576]{1,0:T(8,128)(2,1)} %pack.5.refs_1_, ...), custom_call_target="tpu_custom_call", output_to_operand_aliasing={{}: (12, {})} | custom-call | tf_op jit(solution)/shard_map/attend/pallas_call | solution.py:119
  178.2 15.6 %attend.6.refs_9_ = bf16[128,16384]{1,0:T(8,128)(2,1)} custom-call(s32[32]{0:T(128)} %broadcast_add_fusion.number_ref, s32[1]{0:T(128)S(6)} %copy.46.length_ref, bf16[128,18432]{1,0:T(8,128)(2,1)} %q_ref.7, bf16[256,576]{1,0:T(8,128)(2,1)} %pack.4.refs_0_, bf16[256,576]{1,0:T(8,128)(2,1)} %pack.5.refs_1_, ...), custom_call_target="tpu_custom_call", output_to_operand_aliasing={{}: (12, {})} | custom-call | tf_op jit(solution)/shard_map/attend/pallas_call | solution.py:119
  193.8 11.5 %attend.7 = bf16[128,16384]{1,0:T(8,128)(2,1)} custom-call(s32[32]{0:T(128)} %broadcast_add_fusion.number_ref, s32[1]{0:T(128)S(6)} %copy.46.length_ref, bf16[128,18432]{1,0:T(8,128)(2,1)} %q_ref.7, bf16[256,576]{1,0:T(8,128)(2,1)} %pack.4.refs_0_, bf16[256,576]{1,0:T(8,128)(2,1)} %pack.5.refs_1_, ...), custom_call_target="tpu_custom_call", output_to_operand_aliasing={{}: (12, {})} | custom-call | tf_op jit(solution)/shard_map/attend/pallas_call | solution.py:119
  (180 shorter events, 41.2 us)
Async XLA Ops:
  3.5 7.5 %collective-permute-start.20 = (bf16[16,3712]{1,0:T(8,128)(2,1)S(1)}, bf16[16,3712]{1,0:T(8,128)(2,1)S(1)}, u32[]{:S(2)}, u32[]{:S(2)}) collective-permute-start(bf16[16,3712]{1,0:T(8,128)(2,1)S(1)} %pad_maximum_fusion.3), channel_id=1, source_target_pairs={{8,0},{9,1},{10,2},{11,3},{12,4},{13,5},{14,6},{15,7},{0,8},{1,9},... | collective-permute-start | bytes 356360 | tf_op jit(solution)/shard_map/ppermute | solution.py:32
  5.8 10.1 %collective-permute-start.21 = (bf16[16,3712]{1,0:T(8,128)(2,1)S(1)}, bf16[16,3712]{1,0:T(8,128)(2,1)S(1)}, u32[]{:S(2)}, u32[]{:S(2)}) collective-permute-start(bf16[16,3712]{1,0:T(8,128)(2,1)S(1)} %pad_maximum_fusion.3), channel_id=1, source_target_pairs={{12,0},{13,1},{14,2},{15,3},{8,4},{9,5},{10,6},{11,7},{4,8},{5,9},... | collective-permute-start | bytes 356360 | tf_op jit(solution)/shard_map/ppermute | solution.py:32
  16.8 10.5 %collective-permute-start.23 = (bf16[64,3712]{1,0:T(8,128)(2,1)S(1)}, bf16[64,3712]{1,0:T(8,128)(2,1)S(1)}, u32[]{:S(2)}, u32[]{:S(2)}) collective-permute-start(bf16[64,3712]{1,0:T(8,128)(2,1)S(1)} %pad_maximum_fusion.refs_0_), channel_id=1, source_target_pairs={{2,0},{3,1},{0,2},{1,3},{6,4},{7,5},{4,6},{5,7},{10,8},{11,9},{8,1... | collective-permute-start | bytes 1425416 | tf_op jit(solution)/shard_map/ppermute | solution.py:32
  17.1 13.7 %collective-permute-start.22 = (bf16[64,3712]{1,0:T(8,128)(2,1)S(1)}, bf16[64,3712]{1,0:T(8,128)(2,1)S(1)}, u32[]{:S(2)}, u32[]{:S(2)}) collective-permute-start(bf16[64,3712]{1,0:T(8,128)(2,1)S(1)} %pad_maximum_fusion.refs_0_), channel_id=1, source_target_pairs={{16,0},{0,16},{17,1},{1,17},{18,2},{2,18},{19,3},{3,19},{20,4},{4,... | collective-permute-start | bytes 1425416 | tf_op jit(solution)/shard_map/ppermute | solution.py:32
  27.7 11.8 %collective-permute-start.26 = (bf16[64,3712]{1,0:T(8,128)(2,1)S(1)}, bf16[64,3712]{1,0:T(8,128)(2,1)S(1)}, u32[]{:S(2)}, u32[]{:S(2)}) collective-permute-start(bf16[64,3712]{1,0:T(8,128)(2,1)S(1)} %pad_maximum_fusion.refs_0_), channel_id=1, source_target_pairs={{1,0},{0,1},{3,2},{2,3},{5,4},{4,5},{7,6},{6,7},{9,8},{8,9},{11,10... | collective-permute-start | bytes 1425416 | tf_op jit(solution)/shard_map/ppermute | solution.py:32
  30.8 10.2 %collective-permute-start.27 = (bf16[64,3712]{1,0:T(8,128)(2,1)S(1)}, bf16[64,3712]{1,0:T(8,128)(2,1)S(1)}, u32[]{:S(2)}, u32[]{:S(2)}) collective-permute-start(bf16[64,3712]{1,0:T(8,128)(2,1)S(1)} %collective-permute-done.22.refs_1_), channel_id=1, source_target_pairs={{1,0},{0,1},{3,2},{2,3},{5,4},{4,5},{7,6},{6,7},{9,8},{8,9},{11,10... | collective-permute-start | bytes 1425416 | tf_op jit(solution)/shard_map/ppermute | solution.py:32
  30.9 10.1 %collective-permute-start.28 = (bf16[64,3712]{1,0:T(8,128)(2,1)S(1)}, bf16[64,3712]{1,0:T(8,128)(2,1)S(1)}, u32[]{:S(2)}, u32[]{:S(2)}) collective-permute-start(bf16[64,3712]{1,0:T(8,128)(2,1)S(1)} %collective-permute-done.23.refs_2_), channel_id=1, source_target_pairs={{1,0},{0,1},{3,2},{2,3},{5,4},{4,5},{7,6},{6,7},{9,8},{8,9},{11,10... | collective-permute-start | bytes 1425416 | tf_op jit(solution)/shard_map/ppermute | solution.py:32
  31.3 7.3 %collective-permute-start.24 = (bf16[64,1792]{1,0:T(8,128)(2,1)S(1)}, bf16[64,1792]{1,0:T(8,128)(2,1)}, u32[]{:S(2)}, u32[]{:S(2)}) collective-permute-start(bf16[64,1792]{1,0:T(8,128)(2,1)S(1)} %slice.68), channel_id=1, source_target_pairs={{2,0},{3,1},{0,2},{1,3},{6,4},{7,5},{4,6},{5,7},{10,8},{11,9},{8,1... | collective-permute-start | bytes 688136 | tf_op jit(solution)/shard_map/ppermute | solution.py:32
  32.6 8.4 %collective-permute-start.30 = (bf16[64,1920]{1,0:T(8,128)(2,1)S(1)}, bf16[64,1920]{1,0:T(8,128)(2,1)S(1)}, u32[]{:S(2)}, u32[]{:S(2)}) collective-permute-start(bf16[64,1920]{1,0:T(8,128)(2,1)S(1)} %collective-permute-done.25.refs_4_), channel_id=1, source_target_pairs={{1,0},{0,1},{3,2},{2,3},{5,4},{4,5},{7,6},{6,7},{9,8},{8,9},{11,10... | collective-permute-start | bytes 737288 | tf_op jit(solution)/shard_map/ppermute | solution.py:32
  66.5 18.8 %collective-permute-start.32 = (bf16[64,1792]{1,0:T(8,128)(2,1)S(1)}, bf16[64,1792]{1,0:T(8,128)(2,1)S(1)}, u32[]{:S(2)}, u32[]{:S(2)}) collective-permute-start(bf16[64,1792]{1,0:T(8,128)(2,1)S(1)} %get-tuple-element.44), channel_id=1, source_target_pairs={{2,0},{3,1},{0,2},{1,3},{6,4},{7,5},{4,6},{5,7},{10,8},{11,9},{8,1... | collective-permute-start | bytes 688136 | tf_op jit(solution)/shard_map/ppermute | solution.py:32
  67.8 17.6 %collective-permute-start.34 = (bf16[64,1792]{1,0:T(8,128)(2,1)S(1)}, bf16[64,1792]{1,0:T(8,128)(2,1)S(1)}, u32[]{:S(2)}, u32[]{:S(2)}) collective-permute-start(bf16[64,1792]{1,0:T(8,128)(2,1)S(1)} %get-tuple-element.45), channel_id=1, source_target_pairs={{16,0},{0,16},{17,1},{1,17},{18,2},{2,18},{19,3},{3,19},{20,4},{4,... | collective-permute-start | bytes 688136 | tf_op jit(solution)/shard_map/ppermute | solution.py:32
  68.8 10.0 %all-to-all-start = ((s32[16,1,2]{2,1,0:T(1,128)}), s32[16,1,2]{2,1,0:T(1,128)S(1)}, u32[]{:S(2)}, u32[]{:S(2)}) async-start(s32[16,1,2]{2,1,0:T(1,128)} %copy.33), calls=%async_computation | async-start | bytes 16384 | tf_op jit(solution)/shard_map/all_to_all | solution.py:171
  82.1 12.5 %collective-permute-start.12 = (bf16[64,576]{1,0:T(8,128)(2,1)}, bf16[64,576]{1,0:T(8,128)(2,1)S(1)}, u32[]{:S(2)}, u32[]{:S(2)}) collective-permute-start(bf16[64,576]{1,0:T(8,128)(2,1)} %get-tuple-element.33), channel_id=1, source_target_pairs={{13,0},{12,1},{15,2},{14,3},{9,4},{8,5},{11,6},{10,7},{5,8},{4,9},... | collective-permute-start | bytes 221192 | tf_op jit(solution)/shard_map/ppermute | solution.py:150
  84.1 11.1 %collective-permute-start.13 = (bf16[64,576]{1,0:T(8,128)(2,1)}, bf16[64,576]{1,0:T(8,128)(2,1)S(1)}, u32[]{:S(2)}, u32[]{:S(2)}) collective-permute-start(bf16[64,576]{1,0:T(8,128)(2,1)} %get-tuple-element.34), channel_id=1, source_target_pairs={{14,0},{15,1},{12,2},{13,3},{10,4},{11,5},{8,6},{9,7},{6,8},{7,9},... | collective-permute-start | bytes 221192 | tf_op jit(solution)/shard_map/ppermute | solution.py:150
  86.6 45.0 %collective-permute-start.33 = (bf16[64,3584]{1,0:T(8,128)(2,1)S(1)}, bf16[64,3584]{1,0:T(8,128)(2,1)S(1)}, u32[]{:S(2)}, u32[]{:S(2)}) collective-permute-start(bf16[64,3584]{1,0:T(8,128)(2,1)S(1)} %pad_maximum_fusion.1), channel_id=1, source_target_pairs={{16,0},{0,16},{17,1},{1,17},{18,2},{2,18},{19,3},{3,19},{20,4},{4,... | collective-permute-start | bytes 1376264 | tf_op jit(solution)/shard_map/ppermute | solution.py:32
  87.5 44.8 %collective-permute-start.35 = (bf16[64,3584]{1,0:T(8,128)(2,1)S(1)}, bf16[64,3584]{1,0:T(8,128)(2,1)S(1)}, u32[]{:S(2)}, u32[]{:S(2)}) collective-permute-start(bf16[64,3584]{1,0:T(8,128)(2,1)S(1)} %pad_maximum_fusion.2), channel_id=1, source_target_pairs={{2,0},{3,1},{0,2},{1,3},{6,4},{7,5},{4,6},{5,7},{10,8},{11,9},{8,1... | collective-permute-start | bytes 1376264 | tf_op jit(solution)/shard_map/ppermute | solution.py:32
  87.8 16.2 %collective-permute-start.14 = (bf16[64,576]{1,0:T(8,128)(2,1)S(1)}, bf16[64,576]{1,0:T(8,128)(2,1)S(1)}, u32[]{:S(2)}, u32[]{:S(2)}) collective-permute-start(bf16[64,576]{1,0:T(8,128)(2,1)S(1)} %copy-done.42), channel_id=1, source_target_pairs={{15,0},{14,1},{13,2},{12,3},{11,4},{10,5},{9,6},{8,7},{7,8},{6,9},... | collective-permute-start | bytes 221192 | tf_op jit(solution)/shard_map/ppermute | solution.py:150
  94.7 11.2 %collective-permute-start.10 = (bf16[64,576]{1,0:T(8,128)(2,1)S(1)}, bf16[64,576]{1,0:T(8,128)(2,1)S(1)}, u32[]{:S(2)}, u32[]{:S(2)}) collective-permute-start(bf16[64,576]{1,0:T(8,128)(2,1)S(1)} %copy-done.41), channel_id=1, source_target_pairs={{11,0},{10,1},{9,2},{8,3},{15,4},{14,5},{13,6},{12,7},{3,8},{2,9},... | collective-permute-start | bytes 221192 | tf_op jit(solution)/shard_map/ppermute | solution.py:150
  95.3 11.2 %collective-permute-start.7 = (bf16[64,576]{1,0:T(8,128)(2,1)S(1)}, bf16[64,576]{1,0:T(8,128)(2,1)S(1)}, u32[]{:S(2)}, u32[]{:S(2)}) collective-permute-start(bf16[64,576]{1,0:T(8,128)(2,1)S(1)} %copy-done.40), channel_id=1, source_target_pairs={{8,0},{9,1},{10,2},{11,3},{12,4},{13,5},{14,6},{15,7},{0,8},{1,9},... | collective-permute-start | bytes 221192 | tf_op jit(solution)/shard_map/ppermute | solution.py:150
  105.8 7.0 %collective-permute-start.9 = (bf16[64,576]{1,0:T(8,128)(2,1)S(1)}, bf16[64,576]{1,0:T(8,128)(2,1)S(1)}, u32[]{:S(2)}, u32[]{:S(2)}) collective-permute-start(bf16[64,576]{1,0:T(8,128)(2,1)S(1)} %copy-done.38), channel_id=1, source_target_pairs={{10,0},{11,1},{8,2},{9,3},{14,4},{15,5},{12,6},{13,7},{2,8},{3,9},... | collective-permute-start | bytes 221192 | tf_op jit(solution)/shard_map/ppermute | solution.py:150
  106.4 9.1 %collective-permute-start.3 = (bf16[64,576]{1,0:T(8,128)(2,1)S(1)}, bf16[64,576]{1,0:T(8,128)(2,1)S(1)}, u32[]{:S(2)}, u32[]{:S(2)}) collective-permute-start(bf16[64,576]{1,0:T(8,128)(2,1)S(1)} %copy-done.37), channel_id=1, source_target_pairs={{4,0},{5,1},{6,2},{7,3},{0,4},{1,5},{2,6},{3,7},{12,8},{13,9},{14,... | collective-permute-start | bytes 221192 | tf_op jit(solution)/shard_map/ppermute | solution.py:150
  112.8 6.4 %collective-permute-start.5 = (bf16[64,576]{1,0:T(8,128)(2,1)S(1)}, bf16[64,576]{1,0:T(8,128)(2,1)S(1)}, u32[]{:S(2)}, u32[]{:S(2)}) collective-permute-start(bf16[64,576]{1,0:T(8,128)(2,1)S(1)} %copy-done.36), channel_id=1, source_target_pairs={{6,0},{7,1},{4,2},{5,3},{2,4},{3,5},{0,6},{1,7},{14,8},{15,9},{12,... | collective-permute-start | bytes 221192 | tf_op jit(solution)/shard_map/ppermute | solution.py:150
  116.4 11.2 %collective-permute-start = (bf16[64,576]{1,0:T(8,128)(2,1)S(1)}, bf16[64,576]{1,0:T(8,128)(2,1)S(1)}, u32[]{:S(2)}, u32[]{:S(2)}) collective-permute-start(bf16[64,576]{1,0:T(8,128)(2,1)S(1)} %copy-done.34), channel_id=1, source_target_pairs={{1,0},{0,1},{3,2},{2,3},{5,4},{4,5},{7,6},{6,7},{9,8},{8,9},{11,10... | collective-permute-start | bytes 221192 | tf_op jit(solution)/shard_map/ppermute | solution.py:150
  119.2 9.1 %collective-permute-start.1 = (bf16[64,576]{1,0:T(8,128)(2,1)S(1)}, bf16[64,576]{1,0:T(8,128)(2,1)S(1)}, u32[]{:S(2)}, u32[]{:S(2)}) collective-permute-start(bf16[64,576]{1,0:T(8,128)(2,1)S(1)} %copy-done.33), channel_id=1, source_target_pairs={{2,0},{3,1},{0,2},{1,3},{6,4},{7,5},{4,6},{5,7},{10,8},{11,9},{8,1... | collective-permute-start | bytes 221192 | tf_op jit(solution)/shard_map/ppermute | solution.py:150
  121.0 8.0 %collective-permute-start.2 = (bf16[64,576]{1,0:T(8,128)(2,1)S(1)}, bf16[64,576]{1,0:T(8,128)(2,1)S(1)}, u32[]{:S(2)}, u32[]{:S(2)}) collective-permute-start(bf16[64,576]{1,0:T(8,128)(2,1)S(1)} %copy-done.32), channel_id=1, source_target_pairs={{3,0},{2,1},{1,2},{0,3},{7,4},{6,5},{5,6},{4,7},{11,8},{10,9},{9,1... | collective-permute-start | bytes 221192 | tf_op jit(solution)/shard_map/ppermute | solution.py:150
  127.6 9.9 %collective-permute-start.18 = (bf16[256,576]{1,0:T(8,128)(2,1)}, bf16[256,576]{1,0:T(8,128)(2,1)S(1)}, u32[]{:S(2)}, u32[]{:S(2)}) collective-permute-start(bf16[256,576]{1,0:T(8,128)(2,1)} %pack.7.refs_3_), channel_id=1, source_target_pairs={{16,0},{0,16},{17,1},{1,17},{18,2},{2,18},{19,3},{3,19},{20,4},{4,... | collective-permute-start | bytes 884744 | tf_op jit(solution)/shard_map/ppermute | solution.py:32
  128.3 16.2 %collective-permute-start.17 = (bf16[256,576]{1,0:T(8,128)(2,1)}, bf16[256,576]{1,0:T(8,128)(2,1)S(1)}, u32[]{:S(2)}, u32[]{:S(2)}) collective-permute-start(bf16[256,576]{1,0:T(8,128)(2,1)} %pack.6.refs_2_), channel_id=1, source_target_pairs={{16,0},{0,16},{17,1},{1,17},{18,2},{2,18},{19,3},{3,19},{20,4},{4,... | collective-permute-start | bytes 884744 | tf_op jit(solution)/shard_map/ppermute | solution.py:32
  129.1 22.5 %collective-permute-start.16 = (bf16[256,576]{1,0:T(8,128)(2,1)}, bf16[256,576]{1,0:T(8,128)(2,1)S(1)}, u32[]{:S(2)}, u32[]{:S(2)}) collective-permute-start(bf16[256,576]{1,0:T(8,128)(2,1)} %pack.5.refs_1_), channel_id=1, source_target_pairs={{16,0},{0,16},{17,1},{1,17},{18,2},{2,18},{19,3},{3,19},{20,4},{4,... | collective-permute-start | bytes 884744 | tf_op jit(solution)/shard_map/ppermute | solution.py:32
  131.6 26.8 %collective-permute-start.15 = (bf16[256,576]{1,0:T(8,128)(2,1)}, bf16[256,576]{1,0:T(8,128)(2,1)S(1)}, u32[]{:S(2)}, u32[]{:S(2)}) collective-permute-start(bf16[256,576]{1,0:T(8,128)(2,1)} %pack.4.refs_0_), channel_id=1, source_target_pairs={{16,0},{0,16},{17,1},{1,17},{18,2},{2,18},{19,3},{3,19},{20,4},{4,... | collective-permute-start | bytes 884744 | tf_op jit(solution)/shard_map/ppermute | solution.py:32
  133.6 71.6 %collective-permute-start.36 = (bf16[16,3584]{1,0:T(8,128)(2,1)S(1)}, bf16[16,3584]{1,0:T(8,128)(2,1)S(1)}, u32[]{:S(2)}, u32[]{:S(2)}) collective-permute-start(bf16[16,3584]{1,0:T(8,128)(2,1)S(1)} %get-tuple-element.48), channel_id=1, source_target_pairs={{0,4},{1,5},{2,6},{3,7},{4,0},{5,1},{6,2},{7,3},{8,12},{9,13},{10,... | collective-permute-start | bytes 344072 | tf_op jit(solution)/shard_map/ppermute | solution.py:32
  137.5 67.8 %collective-permute-start.37 = (bf16[16,3584]{1,0:T(8,128)(2,1)S(1)}, bf16[16,3584]{1,0:T(8,128)(2,1)S(1)}, u32[]{:S(2)}, u32[]{:S(2)}) collective-permute-start(bf16[16,3584]{1,0:T(8,128)(2,1)S(1)} %get-tuple-element.50), channel_id=1, source_target_pairs={{0,8},{1,9},{2,10},{3,11},{4,12},{5,13},{6,14},{7,15},{8,0},{9,1},... | collective-permute-start | bytes 344072 | tf_op jit(solution)/shard_map/ppermute | solution.py:32
  144.5 60.8 %collective-permute-start.38 = (bf16[16,3584]{1,0:T(8,128)(2,1)S(1)}, bf16[16,3584]{1,0:T(8,128)(2,1)S(1)}, u32[]{:S(2)}, u32[]{:S(2)}) collective-permute-start(bf16[16,3584]{1,0:T(8,128)(2,1)S(1)} %get-tuple-element.49), channel_id=1, source_target_pairs={{0,12},{1,13},{2,14},{3,15},{4,8},{5,9},{6,10},{7,11},{8,4},{9,5},... | collective-permute-start | bytes 344072 | tf_op jit(solution)/shard_map/ppermute | solution.py:32
  (51 other events, 703.6 us)

commit v2 on v1

--- a/solution.py
+++ b/solution.py
@@ -13,6 +13,7 @@
 ROPE = 64
 KEY = LATENT + ROPE
 PAGE = 64
+LANES = 128
 
 score_scale = 0.07216878364870322
 neg_large = -1e30
@@ -51,25 +52,31 @@
 
 
 def attention_body(
-    number_ref, length_ref, q_ref, *refs, heads, together, pieces, aliased
+    number_ref, length_ref, q_ref, packed_ref, suffix_ref, *refs, heads, together, aliased
 ):
-    piece_refs = refs[:pieces]
-    o_ref, k_ref, bias_ref, sem = refs[pieces + aliased :]
+    o_ref, k_ref, tail_ref, rotary_ref, bias_ref, sem = refs[aliased:]
     tokens = q_ref.shape[0]
-    keys = k_ref.shape[0]
-    prefix = bias_ref.shape[1]
+    steps, rows, _ = k_ref.shape
+    prefix = steps * rows
+    slabs = LATENT // LANES
     factor = score_scale * math.log2(math.e)
 
     @pl.when(pl.program_id(0) == 0)
     def load_keys():
         copies = []
-        start = 0
-        for n, piece in enumerate(piece_refs):
-            rows = piece.shape[0]
-            copy = pltpu.make_async_copy(piece, k_ref.at[pl.ds(start, rows)], sem.at[n])
+        for t in range(slabs):
+            copies.append(
+                pltpu.make_async_copy(
+                    packed_ref.at[:, pl.ds(t * rows, rows)],
+                    k_ref.at[:, :, pl.ds(t * LANES, LANES)],
+                    sem.at[t],
+                )
+            )
+        last = packed_ref.at[:, pl.ds(slabs * rows, rows // 2)]
+        copies.append(pltpu.make_async_copy(last, rotary_ref, sem.at[slabs]))
+        copies.append(pltpu.make_async_copy(suffix_ref, tail_ref, sem.at[slabs + 1]))
+        for copy in copies:
             copy.start()
-            copies.append(copy)
-            start += rows
         lane = lax.broadcasted_iota(jnp.int32, (1, 2 * PAGE), 1)
         for pair in range(prefix // (2 * PAGE)):
             low = number_ref[2 * pair] * PAGE
@@ -79,17 +86,23 @@
             bias_ref[:, 2 * PAGE * pair : 2 * PAGE * (pair + 1)] = seen.astype(jnp.float32)
         for copy in copies:
             copy.wait()
+        for n in range(steps):
+            both = rotary_ref[n]
+            k_ref[n, : rows // 2, LATENT:] = both[:, : LANES - ROPE]
+            k_ref[n, rows // 2 :, LATENT:] = both[:, LANES - ROPE :]
 
     bias = bias_ref[...]
-    row = lax.broadcasted_iota(jnp.int32, (tokens, keys - prefix), 0)
-    col = lax.broadcasted_iota(jnp.int32, (tokens, keys - prefix), 1)
+    suffix = tail_ref.shape[0]
+    row = lax.broadcasted_iota(jnp.int32, (tokens, suffix), 0)
+    col = lax.broadcasted_iota(jnp.int32, (tokens, suffix), 1)
     causal = jnp.where(col <= row, 0.0, neg_large).astype(jnp.float32)
     causal = jnp.concatenate([causal] * together, axis=0)
+    keys = jnp.concatenate([k_ref[...].reshape(prefix, KEY), tail_ref[...]], axis=0)
     for first in range(0, heads, together):
         group = range(first, first + together)
         q = jnp.concatenate([q_ref[:, h * KEY : (h + 1) * KEY] for h in group], axis=0)
         s = lax.dot_general(
-            q, k_ref[...], (((1,), (1,)), ((), ())), preferred_element_type=jnp.float32
+            q, keys, (((1,), (1,)), ((), ())), preferred_element_type=jnp.float32
         )
         sp = s[:, :prefix] + bias
         ss = s[:, prefix:] + causal
@@ -99,68 +112,52 @@
         ps = jnp.exp2(ss * factor - shift)
         total = jnp.sum(pp, axis=1, keepdims=True) + jnp.sum(ps, axis=1, keepdims=True)
         p = jnp.concatenate([pp.astype(jnp.bfloat16), ps.astype(jnp.bfloat16)], axis=1)
-        acc = jnp.dot(p, k_ref[:, :LATENT], preferred_element_type=jnp.float32) / total
+        acc = jnp.dot(p, keys[:, :LATENT], preferred_element_type=jnp.float32) / total
         for n, h in enumerate(group):
             part = acc[n * tokens : (n + 1) * tokens]
             o_ref[:, h * LATENT : (h + 1) * LATENT] = part.astype(jnp.bfloat16)
 
 
-def attend(queries, pieces, numbers, length, start, count, heads, so_far=None):
+def attend(queries, packed, suffix, numbers, length, start, count, heads, so_far=None):
     tokens = queries.shape[0]
     head_count = queries.shape[1] // KEY
-    keys = sum(piece.shape[0] for piece in pieces)
     prefix = numbers.shape[0] * PAGE
+    steps = packed.shape[0]
+    rows = prefix // steps
     scalars = pl.BlockSpec(memory_space=pltpu.SMEM)
-    together = 4 if heads % 4 == 0 and keys <= 2304 else 2
+    together = 4 if heads % 4 == 0 and prefix <= 2048 else 2
     offset = start // heads
     aliased = 0 if so_far is None else 1
     anywhere = pl.BlockSpec(memory_space=pl.ANY)
     extra = [so_far] if aliased else []
     return pl.pallas_call(
-        functools.partial(
-            attention_body, heads=heads, together=together, pieces=len(pieces), aliased=aliased
-        ),
+        functools.partial(attention_body, heads=heads, together=together, aliased=aliased),
         grid=(count // heads,),
         in_specs=[
             scalars,
             scalars,
             pl.BlockSpec((tokens, heads * KEY), lambda i: (0, i + offset)),
-            *[anywhere] * (len(pieces) + aliased),
+            *[anywhere] * (2 + aliased),
         ],
         out_specs=pl.BlockSpec((tokens, heads * LATENT), lambda i: (0, i + offset)),
         out_shape=jax.ShapeDtypeStruct((tokens, head_count * LATENT), jnp.bfloat16),
         scratch_shapes=[
-            pltpu.VMEM((keys, KEY), jnp.bfloat16),
+            pltpu.VMEM((steps, rows, KEY), jnp.bfloat16),
+            pltpu.VMEM(suffix.shape, jnp.bfloat16),
+            pltpu.VMEM((steps, rows // 2, LANES), jnp.bfloat16),
             pltpu.VMEM((1, prefix), jnp.float32),
-            pltpu.SemaphoreType.DMA((len(pieces),)),
+            pltpu.SemaphoreType.DMA((LATENT // LANES + 2,)),
         ],
-        input_output_aliases={3 + len(pieces): 0} if aliased else {},
-        compiler_params=pltpu.CompilerParams(vmem_limit_bytes=56 << 20),
+        input_output_aliases={5: 0} if aliased else {},
+        compiler_params=pltpu.CompilerParams(vmem_limit_bytes=58 << 20),
         name="attend",
-    )(numbers, length, queries, *pieces, *extra)
-
-
-def pull_block(values, a, b, inner):
-    total = lax.axis_size("ep")
-    outer = total // inner
-    pairs = []
-    for dst in range(total):
-        src = partner(dst // inner, a, outer) * inner + partner(dst % inner, b, inner)
-        pairs.append((src, dst))
-    return lax.ppermute(values, "ep", pairs)
+    )(numbers, length, queries, packed, suffix, *extra)
 
 
 def fetch_pages(page_pool, page_owner, page_slot):
     ep_size = lax.axis_size("ep")
-    dp_size = lax.axis_size("dp")
-    me = lax.axis_index("ep")
-    plane = lax.axis_index("dp")
     pages = page_owner.shape[1]
     ranks = (pages + ep_size - 1) // ep_size
-    planes = dp_size if ranks % dp_size == 0 else 1
-    own_ranks = ranks // planes
-    inner = 4 if ep_size % 4 == 0 else 1
-    outer = ep_size // inner
     page_id = jnp.arange(pages, dtype=jnp.int32)
     owners = jnp.arange(ep_size, dtype=jnp.int32)
     rank_id = jnp.arange(ranks, dtype=jnp.int32)
@@ -168,86 +165,44 @@
         page_id[None, None, :] // ep_size == rank_id[None, :, None]
     )
     wanted = jnp.sum(jnp.where(match, page_slot[0][None, None, :], 0), axis=2)
+    place = jnp.arange(ep_size * ranks, dtype=jnp.int32)
+    seat = page_owner[0] * ranks + page_id // ep_size
+    hit = place[:, None] == seat[None, :]
+    numbers = pages + jnp.sum(jnp.where(hit, page_id[None, :] - pages, 0), axis=1)
     asked = lax.all_to_all(wanted, "ep", split_axis=0, concat_axis=0, tiled=True)
-    first = (plane * own_ranks) % ranks if planes > 1 else 0
     pool = page_pool.reshape(page_pool.shape[0], PAGE, KEY)
-    where = jnp.stack([me, jnp.asarray(first, jnp.int32)]).astype(jnp.int32)
-    chosen = pick_pages(where, asked, pool, inner, own_ranks)
-    groups = []
-    for a in range(outer):
-        pieces = []
-        for b in range(inner):
-            step = a * inner + b
-            pieces.append(pull_block(chosen[step], a, b, inner) if step else chosen[0])
-        groups.append(pack_pages(pieces))
-    blocks = list(groups)
-    for shift in range(1, planes):
-        for a in range(outer):
-            blocks.append(pull(groups[a], "dp", 1, dp_size, shift))
-    steps = jnp.arange(ep_size, dtype=jnp.int32)
-    group, place = me // inner, me % inner
-    hear = partner(group, steps // inner, outer) * inner + partner(place, steps % inner, inner)
-    turn = partner(plane, jnp.arange(planes, dtype=jnp.int32), planes) if planes > 1 else 0
-    order = turn * own_ranks + jnp.arange(own_ranks, dtype=jnp.int32)[:, None]
-    order = order.T.reshape(planes, 1, own_ranks)
-    seat = page_owner[0] + page_id // ep_size * ep_size
-    place_of = (hear[None, :, None] + order * ep_size).reshape(-1, 1)
-    hit = place_of == seat[None, :]
-    numbers = pages + jnp.sum(jnp.where(hit, page_id[None, :] - pages, 0), axis=1)
-    return blocks, numbers
-
-
-def pack_body(*refs):
-    start = 0
-    for piece in refs[:-1]:
-        rows = piece.shape[0]
-        refs[-1][start : start + rows] = piece[...]
-        start += rows
-
-
-def pack_pages(pieces):
-    if len(pieces) == 1:
-        return pieces[0]
-    rows = sum(piece.shape[0] for piece in pieces)
+    chosen = pick_pages(asked, pool)
+    fetched = lax.all_to_all(chosen, "ep", split_axis=0, concat_axis=0, tiled=True)
+    return fetched, numbers
+
+
+def pick_body(asked_ref, pool_ref, out_ref):
+    steps, ranks = asked_ref.shape
+    rows = ranks * PAGE
+    slabs = LATENT // LANES
+    for n in range(steps):
+        rotary = []
+        for r in range(ranks):
+            page = pool_ref[asked_ref[n, r]]
+            for t in range(slabs):
+                start = t * rows + r * PAGE
+                out_ref[n, start : start + PAGE] = page[:, t * LANES : (t + 1) * LANES]
+            rotary.append(page[:, LATENT:])
+        rotary = jnp.concatenate(rotary, axis=0)
+        low, high = rotary[: rows // 2], rotary[rows // 2 :]
+        out_ref[n, slabs * rows :] = jnp.concatenate([low, high], axis=1)
+
+
+def pick_pages(asked, pool):
+    steps, ranks = asked.shape
     whole = pl.BlockSpec(memory_space=pltpu.VMEM)
     return pl.pallas_call(
-        pack_body,
-        in_specs=[whole] * len(pieces),
+        pick_body,
+        in_specs=[pl.BlockSpec(memory_space=pltpu.SMEM), whole],
         out_specs=whole,
-        out_shape=jax.ShapeDtypeStruct((rows, pieces[0].shape[1]), pieces[0].dtype),
-        name="pack",
-    )(*pieces)
-
-
-def pick_body(where_ref, asked_ref, pool_ref, *outs, inner, count):
-    steps = len(outs)
-    me = where_ref[0]
-    for n, out in enumerate(outs):
-        low, high = n % inner, n // inner
-        if inner & (inner - 1) == 0:
-            place = (me % inner) ^ low
-        else:
-            place = (me % inner + inner - low) % inner
-        outer = steps // inner
-        if outer & (outer - 1) == 0:
-            group = (me // inner) ^ high
-        else:
-            group = (me // inner + outer - high) % outer
-        for r in range(count):
-            slot = asked_ref[group * inner + place, where_ref[1] + r]
-            out[r * PAGE : (r + 1) * PAGE] = pool_ref[slot]
-
-
-def pick_pages(where, asked, pool, inner, count):
-    steps = asked.shape[0]
-    scalars = pl.BlockSpec(memory_space=pltpu.SMEM)
-    return pl.pallas_call(
-        functools.partial(pick_body, inner=inner, count=count),
-        in_specs=[scalars, scalars, pl.BlockSpec(memory_space=pltpu.VMEM)],
-        out_specs=[pl.BlockSpec(memory_space=pltpu.VMEM)] * steps,
-        out_shape=[jax.ShapeDtypeStruct((count * PAGE, KEY), pool.dtype)] * steps,
+        out_shape=jax.ShapeDtypeStruct((steps, ranks * PAGE * KEY // LANES, LANES), pool.dtype),
         name="pick",
-    )(where, asked, pool)
+    )(asked, pool)
 
 
 def split_exact(values):
@@ -452,25 +407,24 @@
     w_up,
     w_down,
 ):
-    pieces, numbers = fetch_pages(page_pool, page_owner, page_slot)
-    pieces = pieces + [suffix_latent]
+    packed, numbers = fetch_pages(page_pool, page_owner, page_slot)
+    source = (queries, packed, suffix_latent, numbers, prefix_len)
     moe_args = (moe_input, expert_ids, gate_weights, w_gate, w_up, w_down)
     head_count = queries.shape[1] // KEY
     if not can_square(moe_input.shape[0], w_gate.shape[2]):
         moe_output = experts_staged(*moe_args)
-        return (attend(queries, pieces, numbers, prefix_len, 0, head_count, 2), moe_output)
+        return (attend(*source, 0, head_count, 2), moe_output)
     stages = experts_square(*moe_args)
     heads = 4
     steps = head_count // heads
-    cuts = [0, steps // 8, 3 * steps // 8, 6 * steps // 8, steps]
+    next(stages)
+    cuts = [0, steps // 4, 5 * steps // 8, steps]
     attn_context = None
-    for n in range(4):
+    for n in range(3):
         next(stages)
         start, count = cuts[n] * heads, (cuts[n + 1] - cuts[n]) * heads
         if count:
-            attn_context = attend(
-                queries, pieces, numbers, prefix_len, start, count, heads, attn_context
-            )
+            attn_context = attend(*source, start, count, heads, attn_context)
     moe_output = next(stages)
     return (attn_context, moe_output)
 

time: 210 us -> 198 us (0.943)
  starting transfers between devices: 48.5 us -> 36.9 us
  Pallas kernels: 71.1 us -> 61 us
  waiting for transfers between devices: 65.7 us -> 75.2 us
    ppermute x24 -> x20, waiting for transfers between devices: 48.7 us -> 73.1 us  [pull(): return lax.ppermute(values, axis, pairs)]
    ppermute x15 -> x0, starting transfers between devices: 20.3 us -> none  [pull_block(): return lax.ppermute(values, 'ep', pairs)]
    ppermute x15 -> x0, waiting for transfers between devices: 15.5 us -> none  [pull_block(): return lax.ppermute(values, 'ep', pairs)]
    pallas_call x5 -> x1, Pallas kernels: 9.32 us -> 2.84 us  [pick_pages(): pl.pallas_call(pick_body, in_specs=[pl.BlockSpec(memory_space=pltpu.SMEM)...]
    all_to_all x0 -> x1, starting transfers between devices: none -> 6.22 us  [fetch_pages(): lax.all_to_all(chosen, 'ep', split_axis=0, concat_axis=0, tiled=True)]
    pallas_call x4 -> x3, Pallas kernels: 46.1 us -> 42.5 us  [attend(): pl.pallas_call(functools.partial(attention_body, heads=heads, together=to...]
    ppermute x24 -> x20, starting transfers between devices: 22 us -> 24.5 us  [pull(): return lax.ppermute(values, axis, pairs)]
    unnamed x89 -> x29, local copies, waits for them, and re-layouts: 4.79 us -> 6.25 us
  transfers between devices with their start and end apart: 40 -> 22, of which waited for: 18 -> 13; matrix products, arithmetic and copies ran while one was open for 4% -> 5% of each run, Pallas kernels for 27% -> 1%
where the time goes in v2:
time: 198 us; the launch traced here: 196 us
  waiting for transfers between devices  75.2 us (38%)
  Pallas kernels  61 us (31%)
  starting transfers between devices  36.9 us (19%)
  other arithmetic  12.4 us (6%)
  local copies, waits for them, and re-layouts  8.69 us (4%)
    ppermute x20, waiting for transfers between devices, pull(): return lax.ppermute(values, axis, pairs)  73.1 us
    pallas_call x3, Pallas kernels, attend(): pl.pallas_call(functools.partial(attention_body, heads=heads, together=to...  42.5 us
    ppermute x20, starting transfers between devices, pull(): return lax.ppermute(values, axis, pairs)  24.5 us
    pallas_call x1, Pallas kernels, expert_call(): pl.pallas_call(functools.partial(expert_body, places=places, hidden_steps...  15.7 us
    another operation x3, other arithmetic  7.2 us
    unnamed x29, local copies, waits for them, and re-layouts  6.25 us
    all_to_all x1, starting transfers between devices, fetch_pages(): lax.all_to_all(chosen, 'ep', split_axis=0, concat_axis=0, tiled=True)  6.22 us
    all_to_all x1, starting transfers between devices, fetch_pages(): lax.all_to_all(wanted, 'ep', split_axis=0, concat_axis=0, tiled=True)  6.21 us
  transfers between devices with their start and end apart: 22, of which 13 were waited for; matrix products, arithmetic and copies ran while one was open for 5% of the time, Pallas kernels for 1%

profile of v2, /device:TPU:15, one launch (start us, length us, event | category | flops | bytes accessed | tf_op | source)
XLA Modules:
  0.0 195.9 jit_solution(18368056004418558458)
XLA Ops:
  3.5 2.3 %collective-permute-start.1 = (bf16[16,3712]{1,0:T(8,128)(2,1)S(1)}, bf16[16,3712]{1,0:T(8,128)(2,1)S(1)}, u32[]{:S(2)}, u32[]{:S(2)}) collective-permute-start(bf16[16,3712]{1,0:T(8,128)(2,1)S(1)} %pad_maximum_fusion.3), channel_id=1, source_target_pairs={{8,0},{9,1},{10,2},{11,3},{12,4},{13,5},{14,6},{15,7},{0,8},{1,9},... | collective-permute-start | bytes 356360 | tf_op jit(solution)/shard_map/ppermute | solution.py:33
  6.0 1.5 collective-permute-done
  7.4 3.6 %collective-permute-done.1 = bf16[16,3712]{1,0:T(8,128)(2,1)S(1)} collective-permute-done((bf16[16,3712]{1,0:T(8,128)(2,1)S(1)}, bf16[16,3712]{1,0:T(8,128)(2,1)S(1)}, u32[]{:S(2)}, u32[]{:S(2)}) %collective-permute-start.1) | collective-permute-done | bytes 118816 | tf_op jit(solution)/shard_map/ppermute | solution.py:33
  11.0 4.9 %collective-permute-done.2 = bf16[16,3712]{1,0:T(8,128)(2,1)S(1)} collective-permute-done((bf16[16,3712]{1,0:T(8,128)(2,1)S(1)}, bf16[16,3712]{1,0:T(8,128)(2,1)S(1)}, u32[]{:S(2)}, u32[]{:S(2)}) %collective-permute-start.2) | collective-permute-done | bytes 118816 | tf_op jit(solution)/shard_map/ppermute | solution.py:33
  17.4 10.0 %collective-permute-done.4.refs_2_ = bf16[64,3712]{1,0:T(8,128)(2,1)S(1)} collective-permute-done((bf16[64,3712]{1,0:T(8,128)(2,1)S(1)}, bf16[64,3712]{1,0:T(8,128)(2,1)S(1)}, u32[]{:S(2)}, u32[]{:S(2)}) %collective-permute-start.4) | collective-permute-done | bytes 475168 | tf_op jit(solution)/shard_map/ppermute | solution.py:33
  27.7 3.1 %collective-permute-start.7 = (bf16[64,3712]{1,0:T(8,128)(2,1)S(1)}, bf16[64,3712]{1,0:T(8,128)(2,1)S(1)}, u32[]{:S(2)}, u32[]{:S(2)}) collective-permute-start(bf16[64,3712]{1,0:T(8,128)(2,1)S(1)} %pad_maximum_fusion.refs_0_), channel_id=1, source_target_pairs={{1,0},{0,1},{3,2},{2,3},{5,4},{4,5},{7,6},{6,7},{9,8},{8,9},{11,10... | collective-permute-start | bytes 1425416 | tf_op jit(solution)/shard_map/ppermute | solution.py:33
  32.6 3.9 %collective-permute-start.11 = (bf16[64,1920]{1,0:T(8,128)(2,1)S(1)}, bf16[64,1920]{1,0:T(8,128)(2,1)S(1)}, u32[]{:S(2)}, u32[]{:S(2)}) collective-permute-start(bf16[64,1920]{1,0:T(8,128)(2,1)S(1)} %collective-permute-done.6.refs_4_), channel_id=1, source_target_pairs={{1,0},{0,1},{3,2},{2,3},{5,4},{4,5},{7,6},{6,7},{9,8},{8,9},{11,10... | collective-permute-start | bytes 737288 | tf_op jit(solution)/shard_map/ppermute | solution.py:33
  36.5 2.1 %collective-permute-done.5.refs_3_ = bf16[64,1792]{1,0:T(8,128)(2,1)} collective-permute-done((bf16[64,1792]{1,0:T(8,128)(2,1)S(1)}, bf16[64,1792]{1,0:T(8,128)(2,1)}, u32[]{:S(2)}, u32[]{:S(2)}) %collective-permute-start.5) | collective-permute-done | bytes 229408 | tf_op jit(solution)/shard_map/ppermute | solution.py:33
  39.5 1.5 collective-permute-done.10.refs_8_
  42.0 15.7 %expert.1 = (f32[256,3584]{1,0:T(8,128)}, bf16[256,3584]{1,0:T(8,128)(2,1)}) custom-call(s32[1]{0:T(128)} %bitcast.5.me_ref, bf16[64,3712]{1,0:T(8,128)(2,1)} %copy-done.1, bf16[64,3712]{1,0:T(8,128)(2,1)} %copy-done.3, bf16[64,3712]{1,0:T(8,128)(2,1)} %copy-done.2, bf16[64,1792]{1,0:T(8,128)(2,1)} %collective-permute-done.5.refs_3_, ...), custom_call_target="tpu_custom_call" | custom-call | tf_op jit(solution)/shard_map/expert/pallas_call | solution.py:305
  58.2 3.6 %collective-permute-done.12 = bf16[256,3584]{1,0:T(8,128)(2,1)S(1)} collective-permute-done((bf16[256,3584]{1,0:T(8,128)(2,1)}, bf16[256,3584]{1,0:T(8,128)(2,1)S(1)}, u32[]{:S(2)}, u32[]{:S(2)}) %collective-permute-start.12) | collective-permute-done | bytes 1835040 | tf_op jit(solution)/shard_map/ppermute | solution.py:33
  61.8 4.6 %fusion.16 = (bf16[256,3584]{1,0:T(8,128)(2,1)S(1)}, f32[256,3584]{1,0:T(8,128)}) fusion(f32[256,3584]{1,0:T(8,128)} %get-tuple-element.4, bf16[256,3584]{1,0:T(8,128)(2,1)S(1)} %collective-permute-done.12), kind=kLoop, calls=%fused_computation.44 | loop fusion | flops 2752512 | bytes 11010048 | tf_op jit(solution)/shard_map/convert.10
  66.5 1.3 collective-permute-start.13
  68.8 6.2 %all-to-all-start = ((s32[16,1,2]{2,1,0:T(1,128)}), s32[16,1,2]{2,1,0:T(1,128)S(1)}, u32[]{:S(2)}, u32[]{:S(2)}) async-start(s32[16,1,2]{2,1,0:T(1,128)} %copy.30), calls=%async_computation | async-start | bytes 16384 | tf_op jit(solution)/shard_map/all_to_all | solution.py:172
  75.0 1.6 reshape.138.pool_ref
  76.7 2.1 %all-to-all-done = s32[16,1,2]{2,1,0:T(1,128)S(1)} async-done(((s32[16,1,2]{2,1,0:T(1,128)}), s32[16,1,2]{2,1,0:T(1,128)S(1)}, u32[]{:S(2)}, u32[]{:S(2)}) %all-to-all-start) | async-done | bytes 160 | tf_op jit(solution)/shard_map/all_to_all | solution.py:172
  79.4 2.8 %pick.1 = bf16[16,576,128]{2,1,0:T(8,128)(2,1)} custom-call(s32[16,2]{1,0:T(8,128)} %bitcast.13, bf16[8,64,576]{2,1,0:T(8,128)(2,1)} %reshape.138.pool_ref), custom_call_target="tpu_custom_call" | custom-call | tf_op jit(solution)/shard_map/pick/pallas_call | solution.py:199
  82.3 6.2 %all-to-all-start.1 = ((bf16[16,576,128]{2,1,0:T(8,128)(2,1)}), bf16[16,576,128]{2,1,0:T(8,128)(2,1)S(1)}, u32[]{:S(2)}, u32[]{:S(2)}) async-start(bf16[16,576,128]{2,1,0:T(8,128)(2,1)} %pick.1), calls=%async_computation.1 | async-start | bytes 4718592 | tf_op jit(solution)/shard_map/all_to_all | solution.py:175
  88.5 1.3 fusion.2
  92.5 1.7 copy.35.suffix_ref
  95.0 7.6 %collective-permute-done.14 = bf16[64,3584]{1,0:T(8,128)(2,1)S(1)} collective-permute-done((bf16[64,3584]{1,0:T(8,128)(2,1)}, bf16[64,3584]{1,0:T(8,128)(2,1)S(1)}, u32[]{:S(2)}, u32[]{:S(2)}) %collective-permute-start.14) | collective-permute-done | bytes 458784 | tf_op jit(solution)/shard_map/ppermute | solution.py:33
  102.5 9.8 %collective-permute-done.16 = bf16[64,3584]{1,0:T(8,128)(2,1)S(1)} collective-permute-done((bf16[64,3584]{1,0:T(8,128)(2,1)}, bf16[64,3584]{1,0:T(8,128)(2,1)S(1)}, u32[]{:S(2)}, u32[]{:S(2)}) %collective-permute-start.16) | collective-permute-done | bytes 458784 | tf_op jit(solution)/shard_map/ppermute | solution.py:33
  112.4 1.3 fusion.14
  113.7 5.5 %collective-permute-start.17 = (bf16[16,3584]{1,0:T(8,128)(2,1)S(1)}, bf16[16,3584]{1,0:T(8,128)(2,1)S(1)}, u32[]{:S(2)}, u32[]{:S(2)}) collective-permute-start(bf16[16,3584]{1,0:T(8,128)(2,1)S(1)} %get-tuple-element.16), channel_id=1, source_target_pairs={{0,4},{1,5},{2,6},{3,7},{4,0},{5,1},{6,2},{7,3},{8,12},{9,13},{10,... | collective-permute-start | bytes 344072 | tf_op jit(solution)/shard_map/ppermute | solution.py:33
  119.2 2.6 %collective-permute-start.18 = (bf16[16,3584]{1,0:T(8,128)(2,1)S(1)}, bf16[16,3584]{1,0:T(8,128)(2,1)S(1)}, u32[]{:S(2)}, u32[]{:S(2)}) collective-permute-start(bf16[16,3584]{1,0:T(8,128)(2,1)S(1)} %get-tuple-element.18), channel_id=1, source_target_pairs={{0,8},{1,9},{2,10},{3,11},{4,12},{5,13},{6,14},{7,15},{8,0},{9,1},... | collective-permute-start | bytes 344072 | tf_op jit(solution)/shard_map/ppermute | solution.py:33
  122.5 8.3 %collective-permute-done.17 = bf16[16,3584]{1,0:T(8,128)(2,1)S(1)} collective-permute-done((bf16[16,3584]{1,0:T(8,128)(2,1)S(1)}, bf16[16,3584]{1,0:T(8,128)(2,1)S(1)}, u32[]{:S(2)}, u32[]{:S(2)}) %collective-permute-start.17) | collective-permute-done | bytes 114720 | tf_op jit(solution)/shard_map/ppermute | solution.py:33
  130.8 15.8 %collective-permute-done.18 = bf16[16,3584]{1,0:T(8,128)(2,1)S(1)} collective-permute-done((bf16[16,3584]{1,0:T(8,128)(2,1)S(1)}, bf16[16,3584]{1,0:T(8,128)(2,1)S(1)}, u32[]{:S(2)}, u32[]{:S(2)}) %collective-permute-start.18) | collective-permute-done | bytes 114720 | tf_op jit(solution)/shard_map/ppermute | solution.py:33
  146.6 4.5 %collective-permute-done.19 = bf16[16,3584]{1,0:T(8,128)(2,1)S(1)} collective-permute-done((bf16[16,3584]{1,0:T(8,128)(2,1)S(1)}, bf16[16,3584]{1,0:T(8,128)(2,1)S(1)}, u32[]{:S(2)}, u32[]{:S(2)}) %collective-permute-start.19) | collective-permute-done | bytes 114720 | tf_op jit(solution)/shard_map/ppermute | solution.py:33
  151.8 1.4 copy-done
  153.2 11.5 %attend.3.refs_0_ = bf16[128,16384]{1,0:T(8,128)(2,1)} custom-call(s32[32]{0:T(128)} %broadcast_add_fusion.number_ref, s32[1]{0:T(128)S(6)} %copy.41.length_ref, bf16[128,18432]{1,0:T(8,128)(2,1)} %q_ref.5, bf16[16,576,128]{2,1,0:T(8,128)(2,1)} %copy-done, bf16[128,576]{1,0:T(8,128)(2,1)} %copy.35.suffix_ref), custom_call_target="tpu_custom_call" | custom-call | tf_op jit(solution)/shard_map/attend/pallas_call | solution.py:133
  164.8 15.5 %attend.4.refs_0_ = bf16[128,16384]{1,0:T(8,128)(2,1)} custom-call(s32[32]{0:T(128)} %broadcast_add_fusion.number_ref, s32[1]{0:T(128)S(6)} %copy.41.length_ref, bf16[128,18432]{1,0:T(8,128)(2,1)} %q_ref.5, bf16[16,576,128]{2,1,0:T(8,128)(2,1)} %copy-done, bf16[128,576]{1,0:T(8,128)(2,1)} %copy.35.suffix_ref, ...), custom_call_target="tpu_custom_call", output_to_operand_aliasing={{}: (5, {})} | custom-call | tf_op jit(solution)/shard_map/attend/pallas_call | solution.py:133
  180.2 15.5 %attend.5 = bf16[128,16384]{1,0:T(8,128)(2,1)} custom-call(s32[32]{0:T(128)} %broadcast_add_fusion.number_ref, s32[1]{0:T(128)S(6)} %copy.41.length_ref, bf16[128,18432]{1,0:T(8,128)(2,1)} %q_ref.5, bf16[16,576,128]{2,1,0:T(8,128)(2,1)} %copy-done, bf16[128,576]{1,0:T(8,128)(2,1)} %copy.35.suffix_ref, ...), custom_call_target="tpu_custom_call", output_to_operand_aliasing={{}: (5, {})} | custom-call | tf_op jit(solution)/shard_map/attend/pallas_call | solution.py:133
  (71 shorter events, 15.0 us)
Async XLA Ops:
  3.3 4.2 %collective-permute-start = (bf16[16,3712]{1,0:T(8,128)(2,1)S(1)}, bf16[16,3712]{1,0:T(8,128)(2,1)S(1)}, u32[]{:S(2)}, u32[]{:S(2)}) collective-permute-start(bf16[16,3712]{1,0:T(8,128)(2,1)S(1)} %pad_maximum_fusion.3), channel_id=1, source_target_pairs={{4,0},{5,1},{6,2},{7,3},{0,4},{1,5},{2,6},{3,7},{12,8},{13,9},{14,... | collective-permute-start | bytes 356360 | tf_op jit(solution)/shard_map/ppermute | solution.py:33
  3.5 7.5 %collective-permute-start.1 = (bf16[16,3712]{1,0:T(8,128)(2,1)S(1)}, bf16[16,3712]{1,0:T(8,128)(2,1)S(1)}, u32[]{:S(2)}, u32[]{:S(2)}) collective-permute-start(bf16[16,3712]{1,0:T(8,128)(2,1)S(1)} %pad_maximum_fusion.3), channel_id=1, source_target_pairs={{8,0},{9,1},{10,2},{11,3},{12,4},{13,5},{14,6},{15,7},{0,8},{1,9},... | collective-permute-start | bytes 356360 | tf_op jit(solution)/shard_map/ppermute | solution.py:33
  5.8 10.1 %collective-permute-start.2 = (bf16[16,3712]{1,0:T(8,128)(2,1)S(1)}, bf16[16,3712]{1,0:T(8,128)(2,1)S(1)}, u32[]{:S(2)}, u32[]{:S(2)}) collective-permute-start(bf16[16,3712]{1,0:T(8,128)(2,1)S(1)} %pad_maximum_fusion.3), channel_id=1, source_target_pairs={{12,0},{13,1},{14,2},{15,3},{8,4},{9,5},{10,6},{11,7},{4,8},{5,9},... | collective-permute-start | bytes 356360 | tf_op jit(solution)/shard_map/ppermute | solution.py:33
  16.8 24.2 %copy-start.1 = (bf16[64,3712]{1,0:T(8,128)(2,1)}, bf16[64,3712]{1,0:T(8,128)(2,1)S(1)}, u32[]{:S(2)}) copy-start(bf16[64,3712]{1,0:T(8,128)(2,1)S(1)} %pad_maximum_fusion.refs_0_) | copy-start | bytes 1425412
  16.8 10.5 %collective-permute-start.4 = (bf16[64,3712]{1,0:T(8,128)(2,1)S(1)}, bf16[64,3712]{1,0:T(8,128)(2,1)S(1)}, u32[]{:S(2)}, u32[]{:S(2)}) collective-permute-start(bf16[64,3712]{1,0:T(8,128)(2,1)S(1)} %pad_maximum_fusion.refs_0_), channel_id=1, source_target_pairs={{2,0},{3,1},{0,2},{1,3},{6,4},{7,5},{4,6},{5,7},{10,8},{11,9},{8,1... | collective-permute-start | bytes 1425416 | tf_op jit(solution)/shard_map/ppermute | solution.py:33
  17.1 13.7 %collective-permute-start.3 = (bf16[64,3712]{1,0:T(8,128)(2,1)S(1)}, bf16[64,3712]{1,0:T(8,128)(2,1)S(1)}, u32[]{:S(2)}, u32[]{:S(2)}) collective-permute-start(bf16[64,3712]{1,0:T(8,128)(2,1)S(1)} %pad_maximum_fusion.refs_0_), channel_id=1, source_target_pairs={{16,0},{0,16},{17,1},{1,17},{18,2},{2,18},{19,3},{3,19},{20,4},{4,... | collective-permute-start | bytes 1425416 | tf_op jit(solution)/shard_map/ppermute | solution.py:33
  27.3 13.7 %copy-start.2 = (bf16[64,3712]{1,0:T(8,128)(2,1)}, bf16[64,3712]{1,0:T(8,128)(2,1)S(1)}, u32[]{:S(2)}) copy-start(bf16[64,3712]{1,0:T(8,128)(2,1)S(1)} %collective-permute-done.4.refs_2_) | copy-start | bytes 1425412
  27.4 5.2 %collective-permute-start.6 = (bf16[64,1920]{1,0:T(8,128)(2,1)S(1)}, bf16[64,1920]{1,0:T(8,128)(2,1)S(1)}, u32[]{:S(2)}, u32[]{:S(2)}) collective-permute-start(bf16[64,1920]{1,0:T(8,128)(2,1)S(1)} %slice.69), channel_id=1, source_target_pairs={{16,0},{0,16},{17,1},{1,17},{18,2},{2,18},{19,3},{3,19},{20,4},{4,... | collective-permute-start | bytes 737288 | tf_op jit(solution)/shard_map/ppermute | solution.py:33
  27.7 11.8 %collective-permute-start.7 = (bf16[64,3712]{1,0:T(8,128)(2,1)S(1)}, bf16[64,3712]{1,0:T(8,128)(2,1)S(1)}, u32[]{:S(2)}, u32[]{:S(2)}) collective-permute-start(bf16[64,3712]{1,0:T(8,128)(2,1)S(1)} %pad_maximum_fusion.refs_0_), channel_id=1, source_target_pairs={{1,0},{0,1},{3,2},{2,3},{5,4},{4,5},{7,6},{6,7},{9,8},{8,9},{11,10... | collective-permute-start | bytes 1425416 | tf_op jit(solution)/shard_map/ppermute | solution.py:33
  30.8 10.2 %copy-start.3 = (bf16[64,3712]{1,0:T(8,128)(2,1)}, bf16[64,3712]{1,0:T(8,128)(2,1)S(1)}, u32[]{:S(2)}) copy-start(bf16[64,3712]{1,0:T(8,128)(2,1)S(1)} %collective-permute-done.3.refs_1_) | copy-start | bytes 1425412
  30.8 10.2 %collective-permute-start.8 = (bf16[64,3712]{1,0:T(8,128)(2,1)S(1)}, bf16[64,3712]{1,0:T(8,128)(2,1)S(1)}, u32[]{:S(2)}, u32[]{:S(2)}) collective-permute-start(bf16[64,3712]{1,0:T(8,128)(2,1)S(1)} %collective-permute-done.3.refs_1_), channel_id=1, source_target_pairs={{1,0},{0,1},{3,2},{2,3},{5,4},{4,5},{7,6},{6,7},{9,8},{8,9},{11,10... | collective-permute-start | bytes 1425416 | tf_op jit(solution)/shard_map/ppermute | solution.py:33
  30.9 10.1 %collective-permute-start.9 = (bf16[64,3712]{1,0:T(8,128)(2,1)S(1)}, bf16[64,3712]{1,0:T(8,128)(2,1)S(1)}, u32[]{:S(2)}, u32[]{:S(2)}) collective-permute-start(bf16[64,3712]{1,0:T(8,128)(2,1)S(1)} %collective-permute-done.4.refs_2_), channel_id=1, source_target_pairs={{1,0},{0,1},{3,2},{2,3},{5,4},{4,5},{7,6},{6,7},{9,8},{8,9},{11,10... | collective-permute-start | bytes 1425416 | tf_op jit(solution)/shard_map/ppermute | solution.py:33
  31.3 7.3 %collective-permute-start.5 = (bf16[64,1792]{1,0:T(8,128)(2,1)S(1)}, bf16[64,1792]{1,0:T(8,128)(2,1)}, u32[]{:S(2)}, u32[]{:S(2)}) collective-permute-start(bf16[64,1792]{1,0:T(8,128)(2,1)S(1)} %slice.68), channel_id=1, source_target_pairs={{2,0},{3,1},{0,2},{1,3},{6,4},{7,5},{4,6},{5,7},{10,8},{11,9},{8,1... | collective-permute-start | bytes 688136 | tf_op jit(solution)/shard_map/ppermute | solution.py:33
  32.6 8.4 %copy-start.8 = (bf16[64,1920]{1,0:T(8,128)(2,1)}, bf16[64,1920]{1,0:T(8,128)(2,1)S(1)}, u32[]{:S(2)}) copy-start(bf16[64,1920]{1,0:T(8,128)(2,1)S(1)} %collective-permute-done.6.refs_4_) | copy-start | bytes 737284
  32.6 8.4 %collective-permute-start.11 = (bf16[64,1920]{1,0:T(8,128)(2,1)S(1)}, bf16[64,1920]{1,0:T(8,128)(2,1)S(1)}, u32[]{:S(2)}, u32[]{:S(2)}) collective-permute-start(bf16[64,1920]{1,0:T(8,128)(2,1)S(1)} %collective-permute-done.6.refs_4_), channel_id=1, source_target_pairs={{1,0},{0,1},{3,2},{2,3},{5,4},{4,5},{7,6},{6,7},{9,8},{8,9},{11,10... | collective-permute-start | bytes 737288 | tf_op jit(solution)/shard_map/ppermute | solution.py:33
  38.6 2.4 %collective-permute-start.10 = (bf16[64,1792]{1,0:T(8,128)(2,1)}, bf16[64,1792]{1,0:T(8,128)(2,1)}, u32[]{:S(2)}, u32[]{:S(2)}) collective-permute-start(bf16[64,1792]{1,0:T(8,128)(2,1)} %collective-permute-done.5.refs_3_), channel_id=1, source_target_pairs={{1,0},{0,1},{3,2},{2,3},{5,4},{4,5},{7,6},{6,7},{9,8},{8,9},{11,10... | collective-permute-start | bytes 688136 | tf_op jit(solution)/shard_map/ppermute | solution.py:33
  39.5 1.5 copy-start.5
  41.0 1.0 copy-start.9
  42.0 16.2 %copy-start.11 = (s32[1,32]{1,0:T(1,128)S(1)}, s32[1,32]{1,0:T(1,128)}, u32[]{:S(2)}) copy-start(s32[1,32]{1,0:T(1,128)} %param.15) | copy-start | bytes 388
  57.8 4.1 %collective-permute-start.12 = (bf16[256,3584]{1,0:T(8,128)(2,1)}, bf16[256,3584]{1,0:T(8,128)(2,1)S(1)}, u32[]{:S(2)}, u32[]{:S(2)}) collective-permute-start(bf16[256,3584]{1,0:T(8,128)(2,1)} %get-tuple-element.5), channel_id=1, source_target_pairs={{1,0},{0,1},{3,2},{2,3},{5,4},{4,5},{7,6},{6,7},{9,8},{8,9},{11,10... | collective-permute-start | bytes 5505032 | tf_op jit(solution)/shard_map/ppermute | solution.py:33
  61.8 6.2 %copy-start.12 = (s32[1,32]{1,0:T(1,128)S(1)}, s32[1,32]{1,0:T(1,128)}, u32[]{:S(2)}) copy-start(s32[1,32]{1,0:T(1,128)} %param.16) | copy-start | bytes 388
  61.8 13.2 %copy-start.4 = (bf16[8,36864]{1,0:T(8,128)(2,1)S(1)}, bf16[8,36864]{1,0:T(8,128)(2,1)}, u32[]{:S(2)}) copy-start(bf16[8,36864]{1,0:T(8,128)(2,1)} %param.14) | copy-start | bytes 1769476
  66.5 22.0 %collective-permute-start.13 = (bf16[64,1792]{1,0:T(8,128)(2,1)S(1)}, bf16[64,1792]{1,0:T(8,128)(2,1)S(1)}, u32[]{:S(2)}, u32[]{:S(2)}) collective-permute-start(bf16[64,1792]{1,0:T(8,128)(2,1)S(1)} %get-tuple-element.12), channel_id=1, source_target_pairs={{2,0},{3,1},{0,2},{1,3},{6,4},{7,5},{4,6},{5,7},{10,8},{11,9},{8,1... | collective-permute-start | bytes 688136 | tf_op jit(solution)/shard_map/ppermute | solution.py:33
  67.7 20.8 %collective-permute-start.15 = (bf16[64,1792]{1,0:T(8,128)(2,1)S(1)}, bf16[64,1792]{1,0:T(8,128)(2,1)}, u32[]{:S(2)}, u32[]{:S(2)}) collective-permute-start(bf16[64,1792]{1,0:T(8,128)(2,1)S(1)} %get-tuple-element.13), channel_id=1, source_target_pairs={{16,0},{0,16},{17,1},{1,17},{18,2},{2,18},{19,3},{3,19},{20,4},{4,... | collective-permute-start | bytes 688136 | tf_op jit(solution)/shard_map/ppermute | solution.py:33
  68.8 10.0 %all-to-all-start = ((s32[16,1,2]{2,1,0:T(1,128)}), s32[16,1,2]{2,1,0:T(1,128)S(1)}, u32[]{:S(2)}, u32[]{:S(2)}) async-start(s32[16,1,2]{2,1,0:T(1,128)} %copy.30), calls=%async_computation | async-start | bytes 16384 | tf_op jit(solution)/shard_map/all_to_all | solution.py:172
  82.3 69.5 %all-to-all-start.1 = ((bf16[16,576,128]{2,1,0:T(8,128)(2,1)}), bf16[16,576,128]{2,1,0:T(8,128)(2,1)S(1)}, u32[]{:S(2)}, u32[]{:S(2)}) async-start(bf16[16,576,128]{2,1,0:T(8,128)(2,1)} %pick.1), calls=%async_computation.1 | async-start | bytes 4718592 | tf_op jit(solution)/shard_map/all_to_all | solution.py:175
  90.6 11.9 %collective-permute-start.14 = (bf16[64,3584]{1,0:T(8,128)(2,1)}, bf16[64,3584]{1,0:T(8,128)(2,1)S(1)}, u32[]{:S(2)}, u32[]{:S(2)}) collective-permute-start(bf16[64,3584]{1,0:T(8,128)(2,1)} %pad_maximum_fusion.1), channel_id=1, source_target_pairs={{16,0},{0,16},{17,1},{1,17},{18,2},{2,18},{19,3},{3,19},{20,4},{4,... | collective-permute-start | bytes 1376264 | tf_op jit(solution)/shard_map/ppermute | solution.py:33
  92.2 20.2 %collective-permute-start.16 = (bf16[64,3584]{1,0:T(8,128)(2,1)}, bf16[64,3584]{1,0:T(8,128)(2,1)S(1)}, u32[]{:S(2)}, u32[]{:S(2)}) collective-permute-start(bf16[64,3584]{1,0:T(8,128)(2,1)} %pad_maximum_fusion.2), channel_id=1, source_target_pairs={{2,0},{3,1},{0,2},{1,3},{6,4},{7,5},{4,6},{5,7},{10,8},{11,9},{8,1... | collective-permute-start | bytes 1376264 | tf_op jit(solution)/shard_map/ppermute | solution.py:33
  113.7 17.0 %collective-permute-start.17 = (bf16[16,3584]{1,0:T(8,128)(2,1)S(1)}, bf16[16,3584]{1,0:T(8,128)(2,1)S(1)}, u32[]{:S(2)}, u32[]{:S(2)}) collective-permute-start(bf16[16,3584]{1,0:T(8,128)(2,1)S(1)} %get-tuple-element.16), channel_id=1, source_target_pairs={{0,4},{1,5},{2,6},{3,7},{4,0},{5,1},{6,2},{7,3},{8,12},{9,13},{10,... | collective-permute-start | bytes 344072 | tf_op jit(solution)/shard_map/ppermute | solution.py:33
  119.2 27.4 %collective-permute-start.18 = (bf16[16,3584]{1,0:T(8,128)(2,1)S(1)}, bf16[16,3584]{1,0:T(8,128)(2,1)S(1)}, u32[]{:S(2)}, u32[]{:S(2)}) collective-permute-start(bf16[16,3584]{1,0:T(8,128)(2,1)S(1)} %get-tuple-element.18), channel_id=1, source_target_pairs={{0,8},{1,9},{2,10},{3,11},{4,12},{5,13},{6,14},{7,15},{8,0},{9,1},... | collective-permute-start | bytes 344072 | tf_op jit(solution)/shard_map/ppermute | solution.py:33
  121.8 29.3 %collective-permute-start.19 = (bf16[16,3584]{1,0:T(8,128)(2,1)S(1)}, bf16[16,3584]{1,0:T(8,128)(2,1)S(1)}, u32[]{:S(2)}, u32[]{:S(2)}) collective-permute-start(bf16[16,3584]{1,0:T(8,128)(2,1)S(1)} %get-tuple-element.17), channel_id=1, source_target_pairs={{0,12},{1,13},{2,14},{3,15},{4,8},{5,9},{6,10},{7,11},{8,4},{9,5},... | collective-permute-start | bytes 344072 | tf_op jit(solution)/shard_map/ppermute | solution.py:33
  151.8 1.4 copy-start
  (3 other events, 2.3 us)

commit v3 on v2

--- a/solution.py
+++ b/solution.py
@@ -13,7 +13,6 @@
 ROPE = 64
 KEY = LATENT + ROPE
 PAGE = 64
-LANES = 128
 
 score_scale = 0.07216878364870322
 neg_large = -1e30
@@ -52,29 +51,24 @@
 
 
 def attention_body(
-    number_ref, length_ref, q_ref, packed_ref, suffix_ref, *refs, heads, together, aliased
+    number_ref, length_ref, q_ref, *refs, heads, together, count, aliased
 ):
-    o_ref, k_ref, tail_ref, rotary_ref, bias_ref, sem = refs[aliased:]
+    pieces = refs[:count]
+    o_ref, k_ref, bias_ref, sem = refs[count + aliased :]
     tokens = q_ref.shape[0]
-    steps, rows, _ = k_ref.shape
-    prefix = steps * rows
-    slabs = LATENT // LANES
+    prefix = bias_ref.shape[1]
     factor = score_scale * math.log2(math.e)
 
     @pl.when(pl.program_id(0) == 0)
     def load_keys():
         copies = []
-        for t in range(slabs):
+        start = 0
+        for n, piece in enumerate(pieces):
+            rows = piece.shape[0]
             copies.append(
-                pltpu.make_async_copy(
-                    packed_ref.at[:, pl.ds(t * rows, rows)],
-                    k_ref.at[:, :, pl.ds(t * LANES, LANES)],
-                    sem.at[t],
-                )
+                pltpu.make_async_copy(piece, k_ref.at[pl.ds(start, rows)], sem.at[n])
             )
-        last = packed_ref.at[:, pl.ds(slabs * rows, rows // 2)]
-        copies.append(pltpu.make_async_copy(last, rotary_ref, sem.at[slabs]))
-        copies.append(pltpu.make_async_copy(suffix_ref, tail_ref, sem.at[slabs + 1]))
+            start += rows
         for copy in copies:
             copy.start()
         lane = lax.broadcasted_iota(jnp.int32, (1, 2 * PAGE), 1)
@@ -86,23 +80,18 @@
             bias_ref[:, 2 * PAGE * pair : 2 * PAGE * (pair + 1)] = seen.astype(jnp.float32)
         for copy in copies:
             copy.wait()
-        for n in range(steps):
-            both = rotary_ref[n]
-            k_ref[n, : rows // 2, LATENT:] = both[:, : LANES - ROPE]
-            k_ref[n, rows // 2 :, LATENT:] = both[:, LANES - ROPE :]
 
     bias = bias_ref[...]
-    suffix = tail_ref.shape[0]
+    suffix = k_ref.shape[0] - prefix
     row = lax.broadcasted_iota(jnp.int32, (tokens, suffix), 0)
     col = lax.broadcasted_iota(jnp.int32, (tokens, suffix), 1)
     causal = jnp.where(col <= row, 0.0, neg_large).astype(jnp.float32)
     causal = jnp.concatenate([causal] * together, axis=0)
-    keys = jnp.concatenate([k_ref[...].reshape(prefix, KEY), tail_ref[...]], axis=0)
     for first in range(0, heads, together):
         group = range(first, first + together)
         q = jnp.concatenate([q_ref[:, h * KEY : (h + 1) * KEY] for h in group], axis=0)
         s = lax.dot_general(
-            q, keys, (((1,), (1,)), ((), ())), preferred_element_type=jnp.float32
+            q, k_ref[...], (((1,), (1,)), ((), ())), preferred_element_type=jnp.float32
         )
         sp = s[:, :prefix] + bias
         ss = s[:, prefix:] + causal
@@ -112,18 +101,17 @@
         ps = jnp.exp2(ss * factor - shift)
         total = jnp.sum(pp, axis=1, keepdims=True) + jnp.sum(ps, axis=1, keepdims=True)
         p = jnp.concatenate([pp.astype(jnp.bfloat16), ps.astype(jnp.bfloat16)], axis=1)
-        acc = jnp.dot(p, keys[:, :LATENT], preferred_element_type=jnp.float32) / total
+        acc = jnp.dot(p, k_ref[:, :LATENT], preferred_element_type=jnp.float32) / total
         for n, h in enumerate(group):
             part = acc[n * tokens : (n + 1) * tokens]
             o_ref[:, h * LATENT : (h + 1) * LATENT] = part.astype(jnp.bfloat16)
 
 
-def attend(queries, packed, suffix, numbers, length, start, count, heads, so_far=None):
+def attend(queries, pieces, numbers, length, start, count, heads, so_far=None):
     tokens = queries.shape[0]
     head_count = queries.shape[1] // KEY
     prefix = numbers.shape[0] * PAGE
-    steps = packed.shape[0]
-    rows = prefix // steps
+    keys = sum(piece.shape[0] for piece in pieces)
     scalars = pl.BlockSpec(memory_space=pltpu.SMEM)
     together = 4 if heads % 4 == 0 and prefix <= 2048 else 2
     offset = start // heads
@@ -131,78 +119,99 @@
     anywhere = pl.BlockSpec(memory_space=pl.ANY)
     extra = [so_far] if aliased else []
     return pl.pallas_call(
-        functools.partial(attention_body, heads=heads, together=together, aliased=aliased),
+        functools.partial(
+            attention_body, heads=heads, together=together, count=len(pieces), aliased=aliased
+        ),
         grid=(count // heads,),
         in_specs=[
             scalars,
             scalars,
             pl.BlockSpec((tokens, heads * KEY), lambda i: (0, i + offset)),
-            *[anywhere] * (2 + aliased),
+            *[anywhere] * (len(pieces) + aliased),
         ],
         out_specs=pl.BlockSpec((tokens, heads * LATENT), lambda i: (0, i + offset)),
         out_shape=jax.ShapeDtypeStruct((tokens, head_count * LATENT), jnp.bfloat16),
         scratch_shapes=[
-            pltpu.VMEM((steps, rows, KEY), jnp.bfloat16),
-            pltpu.VMEM(suffix.shape, jnp.bfloat16),
-            pltpu.VMEM((steps, rows // 2, LANES), jnp.bfloat16),
+            pltpu.VMEM((keys, KEY), jnp.bfloat16),
             pltpu.VMEM((1, prefix), jnp.float32),
-            pltpu.SemaphoreType.DMA((LATENT // LANES + 2,)),
+            pltpu.SemaphoreType.DMA((len(pieces),)),
         ],
-        input_output_aliases={5: 0} if aliased else {},
+        input_output_aliases={3 + len(pieces): 0} if aliased else {},
         compiler_params=pltpu.CompilerParams(vmem_limit_bytes=58 << 20),
         name="attend",
-    )(numbers, length, queries, packed, suffix, *extra)
+    )(numbers, length, queries, *pieces, *extra)
 
 
 def fetch_pages(page_pool, page_owner, page_slot):
     ep_size = lax.axis_size("ep")
+    me = lax.axis_index("ep").astype(jnp.int32)
     pages = page_owner.shape[1]
     ranks = (pages + ep_size - 1) // ep_size
+    inner = 4 if ep_size % 4 == 0 else 1
+    outer = ep_size // inner
+    pool = page_pool.reshape(page_pool.shape[0], PAGE, KEY)
+    pools = [pool]
+    for a in range(1, outer):
+        pools.append(pull(pool, "ep", inner, outer, a))
+    table = jnp.concatenate([page_owner, page_slot], axis=0)
+    tables = [table]
+    for b in range(1, inner):
+        tables.append(push(table, "ep", 1, inner, b))
+    cuts = sorted({0, outer // 2, outer})
+    pieces = []
+    group, place = me // inner, me % inner
+    owners = []
+    for low, high in zip(cuts, cuts[1:]):
+        hosts = [partner(group, jnp.int32(a), outer) * inner + place for a in range(low, high)]
+        parts = pick_pages(jnp.stack(hosts), tables, pools[low:high], ep_size, ranks)
+        for b in range(inner):
+            pieces.append(pull(parts[b], "ep", 1, inner, b) if b else parts[b])
+            owners += [(a, b) for a in range(low, high)]
+    across = jnp.array([a for a, _ in owners], jnp.int32)
+    beside = jnp.array([b for _, b in owners], jnp.int32)
+    hear = partner(group, across, outer) * inner + partner(place, beside, inner)
     page_id = jnp.arange(pages, dtype=jnp.int32)
-    owners = jnp.arange(ep_size, dtype=jnp.int32)
-    rank_id = jnp.arange(ranks, dtype=jnp.int32)
-    match = (page_owner[0][None, None, :] == owners[:, None, None]) & (
-        page_id[None, None, :] // ep_size == rank_id[None, :, None]
-    )
-    wanted = jnp.sum(jnp.where(match, page_slot[0][None, None, :], 0), axis=2)
-    place = jnp.arange(ep_size * ranks, dtype=jnp.int32)
     seat = page_owner[0] * ranks + page_id // ep_size
-    hit = place[:, None] == seat[None, :]
+    place_of = hear[:, None] * ranks + jnp.arange(ranks, dtype=jnp.int32)[None, :]
+    hit = place_of.reshape(-1, 1) == seat[None, :]
     numbers = pages + jnp.sum(jnp.where(hit, page_id[None, :] - pages, 0), axis=1)
-    asked = lax.all_to_all(wanted, "ep", split_axis=0, concat_axis=0, tiled=True)
-    pool = page_pool.reshape(page_pool.shape[0], PAGE, KEY)
-    chosen = pick_pages(asked, pool)
-    fetched = lax.all_to_all(chosen, "ep", split_axis=0, concat_axis=0, tiled=True)
-    return fetched, numbers
-
-
-def pick_body(asked_ref, pool_ref, out_ref):
-    steps, ranks = asked_ref.shape
-    rows = ranks * PAGE
-    slabs = LATENT // LANES
-    for n in range(steps):
-        rotary = []
-        for r in range(ranks):
-            page = pool_ref[asked_ref[n, r]]
-            for t in range(slabs):
-                start = t * rows + r * PAGE
-                out_ref[n, start : start + PAGE] = page[:, t * LANES : (t + 1) * LANES]
-            rotary.append(page[:, LATENT:])
-        rotary = jnp.concatenate(rotary, axis=0)
-        low, high = rotary[: rows // 2], rotary[rows // 2 :]
-        out_ref[n, slabs * rows :] = jnp.concatenate([low, high], axis=1)
-
-
-def pick_pages(asked, pool):
-    steps, ranks = asked.shape
+    return pieces, numbers
+
+
+def pick_body(host_ref, *refs, count, total, ep_size, ranks):
+    inner = (len(refs) - 1 - count) // 2
+    tables = refs[:inner]
+    pools = refs[inner : inner + count]
+    outs = refs[inner + count : -1]
+    slot_ref = refs[-1]
+    for b, table in enumerate(tables):
+        if total != ep_size * ranks:
+            for n in range(ep_size * ranks):
+                slot_ref[b, n] = 0
+        for k in range(table.shape[1]):
+            slot_ref[b, table[0, k] * ranks + k // ep_size] = table[1, k]
+        for n, pool in enumerate(pools):
+            for r in range(ranks):
+                slot = slot_ref[b, host_ref[n] * ranks + r]
+                start = (n * ranks + r) * PAGE
+                outs[b][start : start + PAGE] = pool[slot]
+
+
+def pick_pages(hosts, tables, pools, ep_size, ranks):
+    rows = len(pools) * ranks * PAGE
+    scalars = pl.BlockSpec(memory_space=pltpu.SMEM)
     whole = pl.BlockSpec(memory_space=pltpu.VMEM)
+    total = tables[0].shape[1]
     return pl.pallas_call(
-        pick_body,
-        in_specs=[pl.BlockSpec(memory_space=pltpu.SMEM), whole],
-        out_specs=whole,
-        out_shape=jax.ShapeDtypeStruct((steps, ranks * PAGE * KEY // LANES, LANES), pool.dtype),
+        functools.partial(
+            pick_body, count=len(pools), total=total, ep_size=ep_size, ranks=ranks
+        ),
+        in_specs=[scalars] * (1 + len(tables)) + [whole] * len(pools),
+        out_specs=[whole] * len(tables),
+        out_shape=[jax.ShapeDtypeStruct((rows, KEY), pools[0].dtype)] * len(tables),
+        scratch_shapes=[pltpu.SMEM((len(tables), ep_size * ranks), jnp.int32)],
         name="pick",
-    )(asked, pool)
+    )(hosts, *tables, *pools)
 
 
 def split_exact(values):
@@ -339,8 +348,7 @@
 def experts_square(moe_input, expert_ids, gate_weights, w_gate, w_up, w_down):
     ep_size = lax.axis_size("ep")
     outer = ep_size // 4
-    tokens, features = moe_input.shape
-    left = features // 256 * 128
+    tokens, _ = moe_input.shape
     experts = jnp.arange(ep_size, dtype=jnp.int32)
     named = expert_ids[:, :, None] == experts[None, None, :]
     dense = jnp.sum(jnp.where(named, gate_weights[:, :, None], 0.0), axis=1)
@@ -354,17 +362,13 @@
     own = jnp.concatenate([rows] + far, axis=0)
     by_x = pull(own, "dp", 1, 2, 1)
     by_y = pull(own, "ep", 2, 2, 1)
-    both_a = pull(by_x[:, :left], "ep", 2, 2, 1)
-    both_b = pull(by_y[:, left:], "dp", 1, 2, 1)
-    near = [own, by_x, by_y, both_a, both_b]
+    both = pull(by_y, "dp", 1, 2, 1)
+    near = [own, by_x, by_y, both]
     across = []
     for piece in near:
         across.append(pull(piece, "ep", 1, 2, 1))
     block = own.shape[0]
-    places = []
-    for base in (0, 4 * block):
-        places += [(base + n * block, 0) for n in range(3)]
-        places += [(base + 3 * block, 0), (base + 3 * block, left)]
+    places = [(n * block, 0) for n in range(8)]
     me = lax.axis_index("ep").astype(jnp.int32).reshape(1)
     keep, send = expert_call(
         me, near + across, tuple(places), 8 * block, ep_size, w_gate[0], w_up[0], w_down[0]
@@ -373,12 +377,10 @@
     yield None
     keep = keep + got.astype(jnp.float32)
     own, by_x, by_y, both = (keep[n * block : (n + 1) * block] for n in range(4))
-    got_a = pull(both[:, :left].astype(jnp.bfloat16), "ep", 2, 2, 1)
-    got_b = pull(both[:, left:].astype(jnp.bfloat16), "dp", 1, 2, 1)
+    got_both = pull(both.astype(jnp.bfloat16), "dp", 1, 2, 1)
+    got_x = pull(by_x.astype(jnp.bfloat16), "dp", 1, 2, 1)
     yield None
-    by_x = jnp.concatenate([by_x[:, :left] + got_a.astype(jnp.float32), by_x[:, left:]], axis=1)
-    by_y = jnp.concatenate([by_y[:, :left], by_y[:, left:] + got_b.astype(jnp.float32)], axis=1)
-    got_x = pull(by_x.astype(jnp.bfloat16), "dp", 1, 2, 1)
+    by_y = by_y + got_both.astype(jnp.float32)
     got_y = pull(by_y.astype(jnp.bfloat16), "ep", 2, 2, 1)
     yield None
     own = own + got_x.astype(jnp.float32) + got_y.astype(jnp.float32)
@@ -407,8 +409,8 @@
     w_up,
     w_down,
 ):
-    packed, numbers = fetch_pages(page_pool, page_owner, page_slot)
-    source = (queries, packed, suffix_latent, numbers, prefix_len)
+    pieces, numbers = fetch_pages(page_pool, page_owner, page_slot)
+    source = (queries, pieces + [suffix_latent], numbers, prefix_len)
     moe_args = (moe_input, expert_ids, gate_weights, w_gate, w_up, w_down)
     head_count = queries.shape[1] // KEY
     if not can_square(moe_input.shape[0], w_gate.shape[2]):
@@ -417,10 +419,9 @@
     stages = experts_square(*moe_args)
     heads = 4
     steps = head_count // heads
-    next(stages)
-    cuts = [0, steps // 4, 5 * steps // 8, steps]
+    cuts = [0, steps // 8, 3 * steps // 8, 6 * steps // 8, steps]
     attn_context = None
-    for n in range(3):
+    for n in range(4):
         next(stages)
         start, count = cuts[n] * heads, (cuts[n + 1] - cuts[n]) * heads
         if count:

time: 198 us -> 205 us (1.035)
  waiting for transfers between devices: 75.2 us -> 84.5 us
  starting transfers between devices: 36.9 us -> 28.5 us
  Pallas kernels: 61 us -> 67.4 us
  other arithmetic: 12.4 us -> 14.8 us
    all_to_all x2 -> x0, starting transfers between devices: 12.4 us -> none  [the longest x1 6.22 us: fetch_pages(): lax.all_to_all(chosen, 'ep', split_axis=0, concat_axis=0, tiled=True)]
    ppermute x20 -> x29, waiting for transfers between devices: 73.1 us -> 84.5 us  [pull(): return lax.ppermute(values, axis, pairs)]
    ppermute x20 -> x29, starting transfers between devices: 24.5 us -> 28.5 us  [pull(): return lax.ppermute(values, axis, pairs)]
    pallas_call x3 -> x4, Pallas kernels: 42.5 us -> 46.1 us  [attend(): pl.pallas_call(functools.partial(attention_body, heads=heads, together=to...]
    pallas_call x1 -> x2, Pallas kernels: 2.84 us -> 5.59 us  [pick_pages(): pl.pallas_call(functools.partial(pick_body, count=len(pools), total=total...]
    all_to_all x2 -> x0, waiting for transfers between devices: 2.15 us -> none  [the longest x1 2.14 us: fetch_pages(): lax.all_to_all(wanted, 'ep', split_axis=0, concat_axis=0, tiled=True)]
    unnamed x29 -> x49, local copies, waits for them, and re-layouts: 6.25 us -> 5.74 us
    another operation x3 -> x4, other arithmetic: 7.2 us -> 7.3 us
  transfers between devices with their start and end apart: 22 -> 29, of which waited for: 13 -> 14; matrix products, arithmetic and copies ran while one was open for 5% -> 7% of each run, Pallas kernels for 1% -> 25%
where the time goes in v3:
time: 205 us; the launch traced here: 203 us
  waiting for transfers between devices  84.5 us (41%)
  Pallas kernels  67.4 us (33%)
  starting transfers between devices  28.5 us (14%)
  other arithmetic  14.8 us (7%)
  local copies, waits for them, and re-layouts  6.71 us (3%)
    ppermute x29, waiting for transfers between devices, pull(): return lax.ppermute(values, axis, pairs)  84.5 us
    pallas_call x4, Pallas kernels, attend(): pl.pallas_call(functools.partial(attention_body, heads=heads, together=to...  46.1 us
    ppermute x29, starting transfers between devices, pull(): return lax.ppermute(values, axis, pairs)  28.5 us
    pallas_call x1, Pallas kernels, expert_call(): pl.pallas_call(functools.partial(expert_body, places=places, hidden_steps...  15.7 us
    another operation x2, other arithmetic  5.98 us
    unnamed x49, local copies, waits for them, and re-layouts  5.74 us
    pallas_call x2, Pallas kernels, pick_pages(): pl.pallas_call(functools.partial(pick_body, count=len(pools), total=total...  5.59 us
  transfers between devices with their start and end apart: 29, of which 14 were waited for; matrix products, arithmetic and copies ran while one was open for 7% of the time, Pallas kernels for 25%

profile of v3, /device:TPU:15, one launch (start us, length us, event | category | flops | bytes accessed | tf_op | source)
XLA Modules:
  0.0 203.4 jit_solution(8350251844082552378)
XLA Ops:
  3.5 2.3 %collective-permute-start.13 = (bf16[16,3712]{1,0:T(8,128)(2,1)S(1)}, bf16[16,3712]{1,0:T(8,128)(2,1)S(1)}, u32[]{:S(2)}, u32[]{:S(2)}) collective-permute-start(bf16[16,3712]{1,0:T(8,128)(2,1)S(1)} %pad_maximum_fusion.1), channel_id=1, source_target_pairs={{8,0},{9,1},{10,2},{11,3},{12,4},{13,5},{14,6},{15,7},{0,8},{1,9},... | collective-permute-start | bytes 356360 | tf_op jit(solution)/shard_map/ppermute | solution.py:32
  6.0 1.5 collective-permute-done.12
  7.4 3.6 %collective-permute-done.13 = bf16[16,3712]{1,0:T(8,128)(2,1)S(1)} collective-permute-done((bf16[16,3712]{1,0:T(8,128)(2,1)S(1)}, bf16[16,3712]{1,0:T(8,128)(2,1)S(1)}, u32[]{:S(2)}, u32[]{:S(2)}) %collective-permute-start.13) | collective-permute-done | bytes 118816 | tf_op jit(solution)/shard_map/ppermute | solution.py:32
  11.0 4.9 %collective-permute-done.14 = bf16[16,3712]{1,0:T(8,128)(2,1)S(1)} collective-permute-done((bf16[16,3712]{1,0:T(8,128)(2,1)S(1)}, bf16[16,3712]{1,0:T(8,128)(2,1)S(1)}, u32[]{:S(2)}, u32[]{:S(2)}) %collective-permute-start.14) | collective-permute-done | bytes 118816 | tf_op jit(solution)/shard_map/ppermute | solution.py:32
  17.4 10.0 %collective-permute-done.16.refs_2_ = bf16[64,3712]{1,0:T(8,128)(2,1)S(1)} collective-permute-done((bf16[64,3712]{1,0:T(8,128)(2,1)S(1)}, bf16[64,3712]{1,0:T(8,128)(2,1)S(1)}, u32[]{:S(2)}, u32[]{:S(2)}) %collective-permute-start.16) | collective-permute-done | bytes 475168 | tf_op jit(solution)/shard_map/ppermute | solution.py:32
  27.6 3.1 %collective-permute-start.18 = (bf16[64,3712]{1,0:T(8,128)(2,1)S(1)}, bf16[64,3712]{1,0:T(8,128)(2,1)S(1)}, u32[]{:S(2)}, u32[]{:S(2)}) collective-permute-start(bf16[64,3712]{1,0:T(8,128)(2,1)S(1)} %pad_maximum_fusion.refs_0_), channel_id=1, source_target_pairs={{1,0},{0,1},{3,2},{2,3},{5,4},{4,5},{7,6},{6,7},{9,8},{8,9},{11,10... | collective-permute-start | bytes 1425416 | tf_op jit(solution)/shard_map/ppermute | solution.py:32
  31.2 5.7 %collective-permute-done.17.refs_3_ = bf16[64,3712]{1,0:T(8,128)(2,1)S(1)} collective-permute-done((bf16[64,3712]{1,0:T(8,128)(2,1)S(1)}, bf16[64,3712]{1,0:T(8,128)(2,1)S(1)}, u32[]{:S(2)}, u32[]{:S(2)}) %collective-permute-start.17) | collective-permute-done | bytes 475168 | tf_op jit(solution)/shard_map/ppermute | solution.py:32
  36.9 3.7 %collective-permute-start.21 = (bf16[64,3712]{1,0:T(8,128)(2,1)S(1)}, bf16[64,3712]{1,0:T(8,128)(2,1)}, u32[]{:S(2)}, u32[]{:S(2)}) collective-permute-start(bf16[64,3712]{1,0:T(8,128)(2,1)S(1)} %collective-permute-done.17.refs_3_), channel_id=1, source_target_pairs={{1,0},{0,1},{3,2},{2,3},{5,4},{4,5},{7,6},{6,7},{9,8},{8,9},{11,10... | collective-permute-start | bytes 1425416 | tf_op jit(solution)/shard_map/ppermute | solution.py:32
  40.7 1.6 collective-permute-done.21.refs_7_
  42.3 15.7 %expert.1 = (f32[256,3584]{1,0:T(8,128)}, bf16[256,3584]{1,0:T(8,128)(2,1)}) custom-call(s32[1]{0:T(128)} %bitcast.5.me_ref, bf16[64,3712]{1,0:T(8,128)(2,1)} %copy-done.7, bf16[64,3712]{1,0:T(8,128)(2,1)} %copy-done.13, bf16[64,3712]{1,0:T(8,128)(2,1)} %copy-done.12, bf16[64,3712]{1,0:T(8,128)(2,1)} %copy-done.14, bf16[64,3712]{1,0:T(8,128)(2,1)} %copy-done.15, ...), custom_call_target="tpu_custom_call" | custom-call | tf_op jit(solution)/shard_map/expert/pallas_call | solution.py:314
  58.7 1.2 collective-permute-start.1
  62.1 4.5 %fusion.15 = (bf16[256,3584]{1,0:T(8,128)(2,1)S(1)}, f32[256,3584]{1,0:T(8,128)}) fusion(f32[256,3584]{1,0:T(8,128)} %get-tuple-element.20, bf16[256,3584]{1,0:T(8,128)(2,1)S(1)} %collective-permute-done.22), kind=kLoop, calls=%fused_computation.37 | loop fusion | flops 2752512 | bytes 11010048 | tf_op jit(solution)/shard_map/convert.4
  67.7 2.2 %collective-permute-start.8 = (bf16[8,64,576]{2,1,0:T(8,128)(2,1)S(1)}, bf16[8,64,576]{2,1,0:T(8,128)(2,1)S(1)}, u32[]{:S(2)}, u32[]{:S(2)}) collective-permute-start(bf16[8,64,576]{2,1,0:T(8,128)(2,1)S(1)} %reshape.68.refs_4_), channel_id=1, source_target_pairs={{12,0},{13,1},{14,2},{15,3},{8,4},{9,5},{10,6},{11,7},{4,8},{5,9},... | collective-permute-start | bytes 1769480 | tf_op jit(solution)/shard_map/ppermute | solution.py:32
  69.9 8.6 %collective-permute-done.24 = bf16[64,3584]{1,0:T(8,128)(2,1)S(1)} collective-permute-done((bf16[64,3584]{1,0:T(8,128)(2,1)S(1)}, bf16[64,3584]{1,0:T(8,128)(2,1)S(1)}, u32[]{:S(2)}, u32[]{:S(2)}) %collective-permute-start.24) | collective-permute-done | bytes 458784 | tf_op jit(solution)/shard_map/ppermute | solution.py:32
  78.5 3.0 %collective-permute-start.3 = (bf16[8,64,576]{2,1,0:T(8,128)(2,1)S(1)}, bf16[8,64,576]{2,1,0:T(8,128)(2,1)S(1)}, u32[]{:S(2)}, u32[]{:S(2)}) collective-permute-start(bf16[8,64,576]{2,1,0:T(8,128)(2,1)S(1)} %reshape.68.refs_4_), channel_id=1, source_target_pairs={{4,0},{5,1},{6,2},{7,3},{0,4},{1,5},{2,6},{3,7},{12,8},{13,9},{14,... | collective-permute-start | bytes 1769480 | tf_op jit(solution)/shard_map/ppermute | solution.py:32
  81.5 2.0 fusion
  85.3 1.7 copy.34.refs_8_
  89.9 14.0 %collective-permute-done.7.refs_4_ = bf16[8,64,576]{2,1,0:T(8,128)(2,1)S(1)} collective-permute-done((bf16[8,64,576]{2,1,0:T(8,128)(2,1)S(1)}, bf16[8,64,576]{2,1,0:T(8,128)(2,1)S(1)}, u32[]{:S(2)}, u32[]{:S(2)}) %collective-permute-start.7) | collective-permute-done | bytes 589856 | tf_op jit(solution)/shard_map/ppermute | solution.py:32
  103.9 17.2 %collective-permute-done.8.refs_5_ = bf16[8,64,576]{2,1,0:T(8,128)(2,1)S(1)} collective-permute-done((bf16[8,64,576]{2,1,0:T(8,128)(2,1)S(1)}, bf16[8,64,576]{2,1,0:T(8,128)(2,1)S(1)}, u32[]{:S(2)}, u32[]{:S(2)}) %collective-permute-start.8) | collective-permute-done | bytes 589856 | tf_op jit(solution)/shard_map/ppermute | solution.py:32
  122.0 2.8 %pick.3 = (bf16[256,576]{1,0:T(8,128)(2,1)}, bf16[256,576]{1,0:T(8,128)(2,1)}, bf16[256,576]{1,0:T(8,128)(2,1)}, bf16[256,576]{1,0:T(8,128)(2,1)}) custom-call(s32[2]{0:T(128)} %pad_add_fusion.2.host_ref, s32[2,32]{1,0:T(2,128)} %copy-done.17, s32[2,32]{1,0:T(2,128)} %copy-done.18, s32[2,32]{1,0:T(2,128)} %collective-permute-done.1.refs_2_, ...), custom_call_target="tpu_custom_call" | custom-call | tf_op jit(solution)/shard_map/pick/pallas_call | solution.py:205
  125.6 1.3 collective-permute-start.11
  127.7 2.8 %pick.2 = (bf16[256,576]{1,0:T(8,128)(2,1)}, bf16[256,576]{1,0:T(8,128)(2,1)}, bf16[256,576]{1,0:T(8,128)(2,1)}, bf16[256,576]{1,0:T(8,128)(2,1)}) custom-call(s32[2]{0:T(128)} %pad_add_fusion.1.host_ref, s32[2,32]{1,0:T(2,128)} %copy-done.17, s32[2,32]{1,0:T(2,128)} %copy-done.18, s32[2,32]{1,0:T(2,128)} %collective-permute-done.1.refs_2_, ...), custom_call_target="tpu_custom_call" | custom-call | tf_op jit(solution)/shard_map/pick/pallas_call | solution.py:205
  131.4 1.5 fusion.13
  133.9 2.8 %collective-permute-start.6 = (bf16[256,576]{1,0:T(8,128)(2,1)}, bf16[256,576]{1,0:T(8,128)(2,1)S(1)}, u32[]{:S(2)}, u32[]{:S(2)}) collective-permute-start(bf16[256,576]{1,0:T(8,128)(2,1)} %get-tuple-element.15), channel_id=1, source_target_pairs={{3,0},{2,1},{1,2},{0,3},{7,4},{6,5},{5,6},{4,7},{11,8},{10,9},{9,1... | collective-permute-start | bytes 884744 | tf_op jit(solution)/shard_map/ppermute | solution.py:32
  136.7 5.6 %collective-permute-done.11.refs_7_ = bf16[256,576]{1,0:T(8,128)(2,1)S(1)} collective-permute-done((bf16[256,576]{1,0:T(8,128)(2,1)}, bf16[256,576]{1,0:T(8,128)(2,1)S(1)}, u32[]{:S(2)}, u32[]{:S(2)}) %collective-permute-start.11) | collective-permute-done | bytes 294944 | tf_op jit(solution)/shard_map/ppermute | solution.py:32
  142.9 2.1 %collective-permute-start.28 = (bf16[16,3584]{1,0:T(8,128)(2,1)S(1)}, bf16[16,3584]{1,0:T(8,128)(2,1)S(1)}, u32[]{:S(2)}, u32[]{:S(2)}) collective-permute-start(bf16[16,3584]{1,0:T(8,128)(2,1)S(1)} %get-tuple-element.29), channel_id=1, source_target_pairs={{0,12},{1,13},{2,14},{3,15},{4,8},{5,9},{6,10},{7,11},{8,4},{9,5},... | collective-permute-start | bytes 344072 | tf_op jit(solution)/shard_map/ppermute | solution.py:32
  145.5 2.4 %collective-permute-done.5.refs_2_ = bf16[256,576]{1,0:T(8,128)(2,1)S(1)} collective-permute-done((bf16[256,576]{1,0:T(8,128)(2,1)}, bf16[256,576]{1,0:T(8,128)(2,1)S(1)}, u32[]{:S(2)}, u32[]{:S(2)}) %collective-permute-start.5) | collective-permute-done | bytes 294944 | tf_op jit(solution)/shard_map/ppermute | solution.py:32
  147.9 7.9 %collective-permute-done.6.refs_3_ = bf16[256,576]{1,0:T(8,128)(2,1)S(1)} collective-permute-done((bf16[256,576]{1,0:T(8,128)(2,1)}, bf16[256,576]{1,0:T(8,128)(2,1)S(1)}, u32[]{:S(2)}, u32[]{:S(2)}) %collective-permute-start.6) | collective-permute-done | bytes 294944 | tf_op jit(solution)/shard_map/ppermute | solution.py:32
  156.6 7.5 %attend.4.refs_9_ = bf16[128,16384]{1,0:T(8,128)(2,1)} custom-call(s32[32]{0:T(128)} %broadcast_add_fusion.number_ref, s32[1]{0:T(128)S(6)} %copy.40.length_ref, bf16[128,18432]{1,0:T(8,128)(2,1)} %q_ref.7, bf16[256,576]{1,0:T(8,128)(2,1)} %get-tuple-element.12.refs_0_, bf16[256,576]{1,0:T(8,128)(2,1)} %copy-done.3, bf16[256,576]{1,0:T(8,128)(2,1)} %copy-done.4, ...), custom_call_target="tpu_custom_call" | custom-call | tf_op jit(solution)/shard_map/attend/pallas_call | solution.py:121
  164.1 11.7 %attend.5.refs_9_ = bf16[128,16384]{1,0:T(8,128)(2,1)} custom-call(s32[32]{0:T(128)} %broadcast_add_fusion.number_ref, s32[1]{0:T(128)S(6)} %copy.40.length_ref, bf16[128,18432]{1,0:T(8,128)(2,1)} %q_ref.7, bf16[256,576]{1,0:T(8,128)(2,1)} %get-tuple-element.12.refs_0_, bf16[256,576]{1,0:T(8,128)(2,1)} %copy-done.3, ...), custom_call_target="tpu_custom_call", output_to_operand_aliasing={{}: (12, {})} | custom-call | tf_op jit(solution)/shard_map/attend/pallas_call | solution.py:121
  175.8 15.4 %attend.6.refs_9_ = bf16[128,16384]{1,0:T(8,128)(2,1)} custom-call(s32[32]{0:T(128)} %broadcast_add_fusion.number_ref, s32[1]{0:T(128)S(6)} %copy.40.length_ref, bf16[128,18432]{1,0:T(8,128)(2,1)} %q_ref.7, bf16[256,576]{1,0:T(8,128)(2,1)} %get-tuple-element.12.refs_0_, bf16[256,576]{1,0:T(8,128)(2,1)} %copy-done.3, ...), custom_call_target="tpu_custom_call", output_to_operand_aliasing={{}: (12, {})} | custom-call | tf_op jit(solution)/shard_map/attend/pallas_call | solution.py:121
  191.2 11.5 %attend.7 = bf16[128,16384]{1,0:T(8,128)(2,1)} custom-call(s32[32]{0:T(128)} %broadcast_add_fusion.number_ref, s32[1]{0:T(128)S(6)} %copy.40.length_ref, bf16[128,18432]{1,0:T(8,128)(2,1)} %q_ref.7, bf16[256,576]{1,0:T(8,128)(2,1)} %get-tuple-element.12.refs_0_, bf16[256,576]{1,0:T(8,128)(2,1)} %copy-done.3, ...), custom_call_target="tpu_custom_call", output_to_operand_aliasing={{}: (12, {})} | custom-call | tf_op jit(solution)/shard_map/attend/pallas_call | solution.py:121
  (104 shorter events, 20.0 us)
Async XLA Ops:
  3.3 4.2 %collective-permute-start.12 = (bf16[16,3712]{1,0:T(8,128)(2,1)S(1)}, bf16[16,3712]{1,0:T(8,128)(2,1)S(1)}, u32[]{:S(2)}, u32[]{:S(2)}) collective-permute-start(bf16[16,3712]{1,0:T(8,128)(2,1)S(1)} %pad_maximum_fusion.1), channel_id=1, source_target_pairs={{4,0},{5,1},{6,2},{7,3},{0,4},{1,5},{2,6},{3,7},{12,8},{13,9},{14,... | collective-permute-start | bytes 356360 | tf_op jit(solution)/shard_map/ppermute | solution.py:32
  3.5 7.5 %collective-permute-start.13 = (bf16[16,3712]{1,0:T(8,128)(2,1)S(1)}, bf16[16,3712]{1,0:T(8,128)(2,1)S(1)}, u32[]{:S(2)}, u32[]{:S(2)}) collective-permute-start(bf16[16,3712]{1,0:T(8,128)(2,1)S(1)} %pad_maximum_fusion.1), channel_id=1, source_target_pairs={{8,0},{9,1},{10,2},{11,3},{12,4},{13,5},{14,6},{15,7},{0,8},{1,9},... | collective-permute-start | bytes 356360 | tf_op jit(solution)/shard_map/ppermute | solution.py:32
  5.8 10.1 %collective-permute-start.14 = (bf16[16,3712]{1,0:T(8,128)(2,1)S(1)}, bf16[16,3712]{1,0:T(8,128)(2,1)S(1)}, u32[]{:S(2)}, u32[]{:S(2)}) collective-permute-start(bf16[16,3712]{1,0:T(8,128)(2,1)S(1)} %pad_maximum_fusion.1), channel_id=1, source_target_pairs={{12,0},{13,1},{14,2},{15,3},{8,4},{9,5},{10,6},{11,7},{4,8},{5,9},... | collective-permute-start | bytes 356360 | tf_op jit(solution)/shard_map/ppermute | solution.py:32
  16.8 25.4 %copy-start.7 = (bf16[64,3712]{1,0:T(8,128)(2,1)}, bf16[64,3712]{1,0:T(8,128)(2,1)S(1)}, u32[]{:S(2)}) copy-start(bf16[64,3712]{1,0:T(8,128)(2,1)S(1)} %pad_maximum_fusion.refs_0_) | copy-start | bytes 1425412
  16.8 10.5 %collective-permute-start.16 = (bf16[64,3712]{1,0:T(8,128)(2,1)S(1)}, bf16[64,3712]{1,0:T(8,128)(2,1)S(1)}, u32[]{:S(2)}, u32[]{:S(2)}) collective-permute-start(bf16[64,3712]{1,0:T(8,128)(2,1)S(1)} %pad_maximum_fusion.refs_0_), channel_id=1, source_target_pairs={{2,0},{3,1},{0,2},{1,3},{6,4},{7,5},{4,6},{5,7},{10,8},{11,9},{8,1... | collective-permute-start | bytes 1425416 | tf_op jit(solution)/shard_map/ppermute | solution.py:32
  17.1 13.6 %collective-permute-start.15 = (bf16[64,3712]{1,0:T(8,128)(2,1)S(1)}, bf16[64,3712]{1,0:T(8,128)(2,1)S(1)}, u32[]{:S(2)}, u32[]{:S(2)}) collective-permute-start(bf16[64,3712]{1,0:T(8,128)(2,1)S(1)} %pad_maximum_fusion.refs_0_), channel_id=1, source_target_pairs={{16,0},{0,16},{17,1},{1,17},{18,2},{2,18},{19,3},{3,19},{20,4},{4,... | collective-permute-start | bytes 1425416 | tf_op jit(solution)/shard_map/ppermute | solution.py:32
  27.3 9.6 %collective-permute-start.17 = (bf16[64,3712]{1,0:T(8,128)(2,1)S(1)}, bf16[64,3712]{1,0:T(8,128)(2,1)S(1)}, u32[]{:S(2)}, u32[]{:S(2)}) collective-permute-start(bf16[64,3712]{1,0:T(8,128)(2,1)S(1)} %collective-permute-done.16.refs_2_), channel_id=1, source_target_pairs={{16,0},{0,16},{17,1},{1,17},{18,2},{2,18},{19,3},{3,19},{20,4},{4,... | collective-permute-start | bytes 1425416 | tf_op jit(solution)/shard_map/ppermute | solution.py:32
  27.6 13.0 %collective-permute-start.18 = (bf16[64,3712]{1,0:T(8,128)(2,1)S(1)}, bf16[64,3712]{1,0:T(8,128)(2,1)S(1)}, u32[]{:S(2)}, u32[]{:S(2)}) collective-permute-start(bf16[64,3712]{1,0:T(8,128)(2,1)S(1)} %pad_maximum_fusion.refs_0_), channel_id=1, source_target_pairs={{1,0},{0,1},{3,2},{2,3},{5,4},{4,5},{7,6},{6,7},{9,8},{8,9},{11,10... | collective-permute-start | bytes 1425416 | tf_op jit(solution)/shard_map/ppermute | solution.py:32
  30.7 9.9 %collective-permute-start.20 = (bf16[64,3712]{1,0:T(8,128)(2,1)S(1)}, bf16[64,3712]{1,0:T(8,128)(2,1)S(1)}, u32[]{:S(2)}, u32[]{:S(2)}) collective-permute-start(bf16[64,3712]{1,0:T(8,128)(2,1)S(1)} %collective-permute-done.16.refs_2_), channel_id=1, source_target_pairs={{1,0},{0,1},{3,2},{2,3},{5,4},{4,5},{7,6},{6,7},{9,8},{8,9},{11,10... | collective-permute-start | bytes 1425416 | tf_op jit(solution)/shard_map/ppermute | solution.py:32
  30.7 9.9 %collective-permute-start.19 = (bf16[64,3712]{1,0:T(8,128)(2,1)S(1)}, bf16[64,3712]{1,0:T(8,128)(2,1)}, u32[]{:S(2)}, u32[]{:S(2)}) collective-permute-start(bf16[64,3712]{1,0:T(8,128)(2,1)S(1)} %collective-permute-done.15.refs_1_), channel_id=1, source_target_pairs={{1,0},{0,1},{3,2},{2,3},{5,4},{4,5},{7,6},{6,7},{9,8},{8,9},{11,10... | collective-permute-start | bytes 1425416 | tf_op jit(solution)/shard_map/ppermute | solution.py:32
  36.9 5.3 %collective-permute-start.21 = (bf16[64,3712]{1,0:T(8,128)(2,1)S(1)}, bf16[64,3712]{1,0:T(8,128)(2,1)}, u32[]{:S(2)}, u32[]{:S(2)}) collective-permute-start(bf16[64,3712]{1,0:T(8,128)(2,1)S(1)} %collective-permute-done.17.refs_3_), channel_id=1, source_target_pairs={{1,0},{0,1},{3,2},{2,3},{5,4},{4,5},{7,6},{6,7},{9,8},{8,9},{11,10... | collective-permute-start | bytes 1425416 | tf_op jit(solution)/shard_map/ppermute | solution.py:32
  58.0 4.1 %collective-permute-start.22 = (bf16[256,3584]{1,0:T(8,128)(2,1)}, bf16[256,3584]{1,0:T(8,128)(2,1)S(1)}, u32[]{:S(2)}, u32[]{:S(2)}) collective-permute-start(bf16[256,3584]{1,0:T(8,128)(2,1)} %get-tuple-element.21), channel_id=1, source_target_pairs={{1,0},{0,1},{3,2},{2,3},{5,4},{4,5},{7,6},{6,7},{9,8},{8,9},{11,10... | collective-permute-start | bytes 5505032 | tf_op jit(solution)/shard_map/ppermute | solution.py:32
  58.5 9.2 %collective-permute-start = (s32[2,32]{1,0:T(2,128)S(1)}, s32[2,32]{1,0:T(2,128)S(1)}, u32[]{:S(2)}, u32[]{:S(2)}) collective-permute-start(s32[2,32]{1,0:T(2,128)S(1)} %pad_add_fusion.refs_0_), channel_id=1, source_target_pairs={{0,1},{1,0},{2,3},{3,2},{4,5},{5,4},{6,7},{7,6},{8,9},{9,8},{10,11... | collective-permute-start | bytes 776 | tf_op jit(solution)/shard_map/ppermute | solution.py:32
  58.7 24.8 %collective-permute-start.1 = (s32[2,32]{1,0:T(2,128)S(1)}, s32[2,32]{1,0:T(2,128)}, u32[]{:S(2)}, u32[]{:S(2)}) collective-permute-start(s32[2,32]{1,0:T(2,128)S(1)} %pad_add_fusion.refs_0_), channel_id=1, source_target_pairs={{0,2},{1,3},{2,0},{3,1},{4,6},{5,7},{6,4},{7,5},{8,10},{9,11},{10,... | collective-permute-start | bytes 776 | tf_op jit(solution)/shard_map/ppermute | solution.py:32
  59.9 23.9 %collective-permute-start.2 = (s32[2,32]{1,0:T(2,128)S(1)}, s32[2,32]{1,0:T(2,128)}, u32[]{:S(2)}, u32[]{:S(2)}) collective-permute-start(s32[2,32]{1,0:T(2,128)S(1)} %pad_add_fusion.refs_0_), channel_id=1, source_target_pairs={{0,3},{1,2},{2,1},{3,0},{4,7},{5,6},{6,5},{7,4},{8,11},{9,10},{10,... | collective-permute-start | bytes 776 | tf_op jit(solution)/shard_map/ppermute | solution.py:32
  61.5 42.4 %collective-permute-start.7 = (bf16[8,64,576]{2,1,0:T(8,128)(2,1)S(1)}, bf16[8,64,576]{2,1,0:T(8,128)(2,1)S(1)}, u32[]{:S(2)}, u32[]{:S(2)}) collective-permute-start(bf16[8,64,576]{2,1,0:T(8,128)(2,1)S(1)} %reshape.68.refs_4_), channel_id=1, source_target_pairs={{8,0},{9,1},{10,2},{11,3},{12,4},{13,5},{14,6},{15,7},{0,8},{1,9},... | collective-permute-start | bytes 1769480 | tf_op jit(solution)/shard_map/ppermute | solution.py:32
  66.7 11.8 %collective-permute-start.24 = (bf16[64,3584]{1,0:T(8,128)(2,1)S(1)}, bf16[64,3584]{1,0:T(8,128)(2,1)S(1)}, u32[]{:S(2)}, u32[]{:S(2)}) collective-permute-start(bf16[64,3584]{1,0:T(8,128)(2,1)S(1)} %get-tuple-element.27), channel_id=1, source_target_pairs={{16,0},{0,16},{17,1},{1,17},{18,2},{2,18},{19,3},{3,19},{20,4},{4,... | collective-permute-start | bytes 1376264 | tf_op jit(solution)/shard_map/ppermute | solution.py:32
  67.7 53.5 %copy-start.18 = (s32[2,32]{1,0:T(2,128)}, s32[2,32]{1,0:T(2,128)S(1)}, u32[]{:S(2)}) copy-start(s32[2,32]{1,0:T(2,128)S(1)} %collective-permute-done.refs_1_) | copy-start | bytes 772
  67.7 53.5 %collective-permute-start.8 = (bf16[8,64,576]{2,1,0:T(8,128)(2,1)S(1)}, bf16[8,64,576]{2,1,0:T(8,128)(2,1)S(1)}, u32[]{:S(2)}, u32[]{:S(2)}) collective-permute-start(bf16[8,64,576]{2,1,0:T(8,128)(2,1)S(1)} %reshape.68.refs_4_), channel_id=1, source_target_pairs={{12,0},{13,1},{14,2},{15,3},{8,4},{9,5},{10,6},{11,7},{4,8},{5,9},... | collective-permute-start | bytes 1769480 | tf_op jit(solution)/shard_map/ppermute | solution.py:32
  78.5 48.4 %collective-permute-start.3 = (bf16[8,64,576]{2,1,0:T(8,128)(2,1)S(1)}, bf16[8,64,576]{2,1,0:T(8,128)(2,1)S(1)}, u32[]{:S(2)}, u32[]{:S(2)}) collective-permute-start(bf16[8,64,576]{2,1,0:T(8,128)(2,1)S(1)} %reshape.68.refs_4_), channel_id=1, source_target_pairs={{4,0},{5,1},{6,2},{7,3},{0,4},{1,5},{2,6},{3,7},{12,8},{13,9},{14,... | collective-permute-start | bytes 1769480 | tf_op jit(solution)/shard_map/ppermute | solution.py:32
  83.6 47.0 %collective-permute-start.23 = (bf16[64,3584]{1,0:T(8,128)(2,1)S(1)}, bf16[64,3584]{1,0:T(8,128)(2,1)S(1)}, u32[]{:S(2)}, u32[]{:S(2)}) collective-permute-start(bf16[64,3584]{1,0:T(8,128)(2,1)S(1)} %get-tuple-element.26), channel_id=1, source_target_pairs={{16,0},{0,16},{17,1},{1,17},{18,2},{2,18},{19,3},{3,19},{20,4},{4,... | collective-permute-start | bytes 1376264 | tf_op jit(solution)/shard_map/ppermute | solution.py:32
  83.8 46.7 %collective-permute-start.25 = (bf16[64,3584]{1,0:T(8,128)(2,1)}, bf16[64,3584]{1,0:T(8,128)(2,1)}, u32[]{:S(2)}, u32[]{:S(2)}) collective-permute-start(bf16[64,3584]{1,0:T(8,128)(2,1)} %fusion), channel_id=1, source_target_pairs={{2,0},{3,1},{0,2},{1,3},{6,4},{7,5},{4,6},{5,7},{10,8},{11,9},{8,1... | collective-permute-start | bytes 1376264 | tf_op jit(solution)/shard_map/ppermute | solution.py:32
  124.8 9.1 %collective-permute-start.10 = (bf16[256,576]{1,0:T(8,128)(2,1)}, bf16[256,576]{1,0:T(8,128)(2,1)S(1)}, u32[]{:S(2)}, u32[]{:S(2)}) collective-permute-start(bf16[256,576]{1,0:T(8,128)(2,1)} %get-tuple-element.18), channel_id=1, source_target_pairs={{2,0},{3,1},{0,2},{1,3},{6,4},{7,5},{4,6},{5,7},{10,8},{11,9},{8,1... | collective-permute-start | bytes 884744 | tf_op jit(solution)/shard_map/ppermute | solution.py:32
  125.6 16.8 %collective-permute-start.11 = (bf16[256,576]{1,0:T(8,128)(2,1)}, bf16[256,576]{1,0:T(8,128)(2,1)S(1)}, u32[]{:S(2)}, u32[]{:S(2)}) collective-permute-start(bf16[256,576]{1,0:T(8,128)(2,1)} %get-tuple-element.19), channel_id=1, source_target_pairs={{3,0},{2,1},{1,2},{0,3},{7,4},{6,5},{5,6},{4,7},{11,8},{10,9},{9,1... | collective-permute-start | bytes 884744 | tf_op jit(solution)/shard_map/ppermute | solution.py:32
  126.9 15.5 %collective-permute-start.9 = (bf16[256,576]{1,0:T(8,128)(2,1)}, bf16[256,576]{1,0:T(8,128)(2,1)S(1)}, u32[]{:S(2)}, u32[]{:S(2)}) collective-permute-start(bf16[256,576]{1,0:T(8,128)(2,1)} %get-tuple-element.17), channel_id=1, source_target_pairs={{1,0},{0,1},{3,2},{2,3},{5,4},{4,5},{7,6},{6,7},{9,8},{8,9},{11,10... | collective-permute-start | bytes 884744 | tf_op jit(solution)/shard_map/ppermute | solution.py:32
  130.5 12.4 %collective-permute-start.4 = (bf16[256,576]{1,0:T(8,128)(2,1)}, bf16[256,576]{1,0:T(8,128)(2,1)S(1)}, u32[]{:S(2)}, u32[]{:S(2)}) collective-permute-start(bf16[256,576]{1,0:T(8,128)(2,1)} %get-tuple-element.13), channel_id=1, source_target_pairs={{1,0},{0,1},{3,2},{2,3},{5,4},{4,5},{7,6},{6,7},{9,8},{8,9},{11,10... | collective-permute-start | bytes 884744 | tf_op jit(solution)/shard_map/ppermute | solution.py:32
  130.6 17.4 %collective-permute-start.5 = (bf16[256,576]{1,0:T(8,128)(2,1)}, bf16[256,576]{1,0:T(8,128)(2,1)S(1)}, u32[]{:S(2)}, u32[]{:S(2)}) collective-permute-start(bf16[256,576]{1,0:T(8,128)(2,1)} %get-tuple-element.14), channel_id=1, source_target_pairs={{2,0},{3,1},{0,2},{1,3},{6,4},{7,5},{4,6},{5,7},{10,8},{11,9},{8,1... | collective-permute-start | bytes 884744 | tf_op jit(solution)/shard_map/ppermute | solution.py:32
  133.9 22.0 %copy-start = (bf16[256,576]{1,0:T(8,128)(2,1)}, bf16[256,576]{1,0:T(8,128)(2,1)S(1)}, u32[]{:S(2)}) copy-start(bf16[256,576]{1,0:T(8,128)(2,1)S(1)} %collective-permute-done.10.refs_6_) | copy-start | bytes 884740
  133.9 21.9 %collective-permute-start.6 = (bf16[256,576]{1,0:T(8,128)(2,1)}, bf16[256,576]{1,0:T(8,128)(2,1)S(1)}, u32[]{:S(2)}, u32[]{:S(2)}) collective-permute-start(bf16[256,576]{1,0:T(8,128)(2,1)} %get-tuple-element.15), channel_id=1, source_target_pairs={{3,0},{2,1},{1,2},{0,3},{7,4},{6,5},{5,6},{4,7},{11,8},{10,9},{9,1... | collective-permute-start | bytes 884744 | tf_op jit(solution)/shard_map/ppermute | solution.py:32
  142.4 60.3 %collective-permute-start.26 = (bf16[16,3584]{1,0:T(8,128)(2,1)S(1)}, bf16[16,3584]{1,0:T(8,128)(2,1)S(1)}, u32[]{:S(2)}, u32[]{:S(2)}) collective-permute-start(bf16[16,3584]{1,0:T(8,128)(2,1)S(1)} %get-tuple-element.28), channel_id=1, source_target_pairs={{0,4},{1,5},{2,6},{3,7},{4,0},{5,1},{6,2},{7,3},{8,12},{9,13},{10,... | collective-permute-start | bytes 344072 | tf_op jit(solution)/shard_map/ppermute | solution.py:32
  142.4 60.3 %collective-permute-start.27 = (bf16[16,3584]{1,0:T(8,128)(2,1)S(1)}, bf16[16,3584]{1,0:T(8,128)(2,1)S(1)}, u32[]{:S(2)}, u32[]{:S(2)}) collective-permute-start(bf16[16,3584]{1,0:T(8,128)(2,1)S(1)} %get-tuple-element.30), channel_id=1, source_target_pairs={{0,8},{1,9},{2,10},{3,11},{4,12},{5,13},{6,14},{7,15},{8,0},{9,1},... | collective-permute-start | bytes 344072 | tf_op jit(solution)/shard_map/ppermute | solution.py:32
  142.9 59.8 %collective-permute-start.28 = (bf16[16,3584]{1,0:T(8,128)(2,1)S(1)}, bf16[16,3584]{1,0:T(8,128)(2,1)S(1)}, u32[]{:S(2)}, u32[]{:S(2)}) collective-permute-start(bf16[16,3584]{1,0:T(8,128)(2,1)S(1)} %get-tuple-element.29), channel_id=1, source_target_pairs={{0,12},{1,13},{2,14},{3,15},{4,8},{5,9},{6,10},{7,11},{8,4},{9,5},... | collective-permute-start | bytes 344072 | tf_op jit(solution)/shard_map/ppermute | solution.py:32
  (20 other events, 189.4 us)

commit v4 on v2

--- a/solution.py
+++ b/solution.py
@@ -51,13 +51,21 @@
     return [stage for stage in stages if stage[2] > 1]
 
 
-def attention_body(
-    number_ref, length_ref, q_ref, packed_ref, suffix_ref, *refs, heads, together, aliased
-):
-    o_ref, k_ref, tail_ref, rotary_ref, bias_ref, sem = refs[aliased:]
+def attention_body(*refs, heads, together, tail, begins, ends, aliased):
+    number_ref, length_ref, q_ref, packed_ref, *refs = refs
+    if tail:
+        suffix_ref, *refs = refs
+    if not begins:
+        acc_in_ref, state_in_ref, *refs = refs
+    refs = refs[aliased:]
+    if ends:
+        o_ref, *refs = refs
+    else:
+        acc_ref, state_ref, *refs = refs
+    k_ref, page_ref, rotary_ref, bias_ref, sem = refs
     tokens = q_ref.shape[0]
-    steps, rows, _ = k_ref.shape
-    prefix = steps * rows
+    steps = page_ref.shape[0]
+    prefix = steps * PAGE
     slabs = LATENT // LANES
     factor = score_scale * math.log2(math.e)
 
@@ -67,18 +75,21 @@
         for t in range(slabs):
             copies.append(
                 pltpu.make_async_copy(
-                    packed_ref.at[:, pl.ds(t * rows, rows)],
-                    k_ref.at[:, :, pl.ds(t * LANES, LANES)],
+                    packed_ref.at[:, pl.ds(t * PAGE, PAGE)],
+                    page_ref.at[:, :, pl.ds(t * LANES, LANES)],
                     sem.at[t],
                 )
             )
-        last = packed_ref.at[:, pl.ds(slabs * rows, rows // 2)]
+        last = packed_ref.at[:, pl.ds(slabs * PAGE, PAGE // 2)]
         copies.append(pltpu.make_async_copy(last, rotary_ref, sem.at[slabs]))
-        copies.append(pltpu.make_async_copy(suffix_ref, tail_ref, sem.at[slabs + 1]))
+        if tail:
+            copies.append(
+                pltpu.make_async_copy(suffix_ref, k_ref.at[pl.ds(prefix, tail)], sem.at[slabs + 1])
+            )
         for copy in copies:
             copy.start()
         lane = lax.broadcasted_iota(jnp.int32, (1, 2 * PAGE), 1)
-        for pair in range(prefix // (2 * PAGE)):
+        for pair in range(steps // 2):
             low = number_ref[2 * pair] * PAGE
             high = number_ref[2 * pair + 1] * PAGE - PAGE
             position = lane + jnp.where(lane < PAGE, low, high)
@@ -86,72 +97,130 @@
             bias_ref[:, 2 * PAGE * pair : 2 * PAGE * (pair + 1)] = seen.astype(jnp.float32)
         for copy in copies:
             copy.wait()
+        half = PAGE // 2
         for n in range(steps):
+            start = n * PAGE
+            k_ref[start : start + PAGE, :LATENT] = page_ref[n]
             both = rotary_ref[n]
-            k_ref[n, : rows // 2, LATENT:] = both[:, : LANES - ROPE]
-            k_ref[n, rows // 2 :, LATENT:] = both[:, LANES - ROPE :]
+            k_ref[start : start + half, LATENT:] = both[:, :ROPE]
+            k_ref[start + half : start + PAGE, LATENT:] = both[:, ROPE:]
 
     bias = bias_ref[...]
-    suffix = tail_ref.shape[0]
-    row = lax.broadcasted_iota(jnp.int32, (tokens, suffix), 0)
-    col = lax.broadcasted_iota(jnp.int32, (tokens, suffix), 1)
-    causal = jnp.where(col <= row, 0.0, neg_large).astype(jnp.float32)
-    causal = jnp.concatenate([causal] * together, axis=0)
-    keys = jnp.concatenate([k_ref[...].reshape(prefix, KEY), tail_ref[...]], axis=0)
+    if tail:
+        row = lax.broadcasted_iota(jnp.int32, (tokens, tail), 0)
+        col = lax.broadcasted_iota(jnp.int32, (tokens, tail), 1)
+        causal = jnp.where(col <= row, 0.0, neg_large).astype(jnp.float32)
+        causal = jnp.concatenate([causal] * together, axis=0)
     for first in range(0, heads, together):
         group = range(first, first + together)
         q = jnp.concatenate([q_ref[:, h * KEY : (h + 1) * KEY] for h in group], axis=0)
         s = lax.dot_general(
-            q, keys, (((1,), (1,)), ((), ())), preferred_element_type=jnp.float32
+            q, k_ref[...], (((1,), (1,)), ((), ())), preferred_element_type=jnp.float32
         )
-        sp = s[:, :prefix] + bias
-        ss = s[:, prefix:] + causal
-        m = jnp.maximum(jnp.max(sp, axis=1, keepdims=True), jnp.max(ss, axis=1, keepdims=True))
+        blocks = [s[:, :prefix] + bias]
+        if tail:
+            blocks.append(s[:, prefix:] + causal)
+        tops = [jnp.max(block, axis=1, keepdims=True) for block in blocks]
+        if not begins:
+            states = [state_in_ref[:, h * LANES : (h + 1) * LANES] for h in group]
+            state = jnp.concatenate(states, axis=0)
+            before = state[:, :1]
+            tops.append(before)
+        m = functools.reduce(jnp.maximum, tops)
         shift = m * factor
-        pp = jnp.exp2(sp * factor - shift)
-        ps = jnp.exp2(ss * factor - shift)
-        total = jnp.sum(pp, axis=1, keepdims=True) + jnp.sum(ps, axis=1, keepdims=True)
-        p = jnp.concatenate([pp.astype(jnp.bfloat16), ps.astype(jnp.bfloat16)], axis=1)
-        acc = jnp.dot(p, keys[:, :LATENT], preferred_element_type=jnp.float32) / total
+        powers = [jnp.exp2(block * factor - shift) for block in blocks]
+        total = sum(jnp.sum(power, axis=1, keepdims=True) for power in powers)
+        p = jnp.concatenate([power.astype(jnp.bfloat16) for power in powers], axis=1)
+        acc = jnp.dot(p, k_ref[:, :LATENT], preferred_element_type=jnp.float32)
+        if not begins:
+            scale = jnp.exp2(before * factor - shift)
+            total = total + state[:, LANES - 1 :] * scale
+            olds = [acc_in_ref[:, h * LATENT : (h + 1) * LATENT] for h in group]
+            acc = acc + jnp.concatenate(olds, axis=0) * scale
+        if ends:
+            acc = acc / total
+        else:
+            lane = lax.broadcasted_iota(jnp.int32, (acc.shape[0], LANES), 1)
+            state = jnp.where(lane < LANES // 2, m, total)
         for n, h in enumerate(group):
-            part = acc[n * tokens : (n + 1) * tokens]
-            o_ref[:, h * LATENT : (h + 1) * LATENT] = part.astype(jnp.bfloat16)
-
-
-def attend(queries, packed, suffix, numbers, length, start, count, heads, so_far=None):
+            rows = slice(n * tokens, (n + 1) * tokens)
+            if ends:
+                o_ref[:, h * LATENT : (h + 1) * LATENT] = acc[rows].astype(jnp.bfloat16)
+            else:
+                acc_ref[:, h * LATENT : (h + 1) * LATENT] = acc[rows]
+                state_ref[:, h * LANES : (h + 1) * LANES] = state[rows]
+
+
+def attend(
+    queries, packed, suffix, numbers, length, start, count, heads, before=None, ends=True, so_far=None
+):
     tokens = queries.shape[0]
     head_count = queries.shape[1] // KEY
-    prefix = numbers.shape[0] * PAGE
     steps = packed.shape[0]
-    rows = prefix // steps
-    scalars = pl.BlockSpec(memory_space=pltpu.SMEM)
+    prefix = steps * PAGE
+    begins = before is None
+    tail = suffix.shape[0] if begins else 0
     together = 4 if heads % 4 == 0 and prefix <= 2048 else 2
     offset = start // heads
     aliased = 0 if so_far is None else 1
+    scalars = pl.BlockSpec(memory_space=pltpu.SMEM)
     anywhere = pl.BlockSpec(memory_space=pl.ANY)
-    extra = [so_far] if aliased else []
+    operands = [numbers, length, queries, packed]
+    in_specs = [
+        scalars,
+        scalars,
+        pl.BlockSpec((tokens, heads * KEY), lambda i: (0, i + offset)),
+        anywhere,
+    ]
+    if begins:
+        operands.append(suffix)
+        in_specs.append(anywhere)
+    else:
+        operands += before
+        in_specs += [
+            pl.BlockSpec((tokens, heads * LATENT), lambda i: (0, i)),
+            pl.BlockSpec((tokens, heads * LANES), lambda i: (0, i)),
+        ]
+    if aliased:
+        operands.append(so_far)
+        in_specs.append(anywhere)
+    if ends:
+        out_specs = pl.BlockSpec((tokens, heads * LATENT), lambda i: (0, i + offset))
+        out_shape = jax.ShapeDtypeStruct((tokens, head_count * LATENT), jnp.bfloat16)
+    else:
+        out_specs = [
+            pl.BlockSpec((tokens, heads * LATENT), lambda i: (0, i)),
+            pl.BlockSpec((tokens, heads * LANES), lambda i: (0, i)),
+        ]
+        out_shape = [
+            jax.ShapeDtypeStruct((tokens, count * LATENT), jnp.float32),
+            jax.ShapeDtypeStruct((tokens, count * LANES), jnp.float32),
+        ]
     return pl.pallas_call(
-        functools.partial(attention_body, heads=heads, together=together, aliased=aliased),
+        functools.partial(
+            attention_body,
+            heads=heads,
+            together=together,
+            tail=tail,
+            begins=begins,
+            ends=ends,
+            aliased=aliased,
+        ),
         grid=(count // heads,),
-        in_specs=[
-            scalars,
-            scalars,
-            pl.BlockSpec((tokens, heads * KEY), lambda i: (0, i + offset)),
-            *[anywhere] * (2 + aliased),
-        ],
-        out_specs=pl.BlockSpec((tokens, heads * LATENT), lambda i: (0, i + offset)),
-        out_shape=jax.ShapeDtypeStruct((tokens, head_count * LATENT), jnp.bfloat16),
+        in_specs=in_specs,
+        out_specs=out_specs,
+        out_shape=out_shape,
         scratch_shapes=[
-            pltpu.VMEM((steps, rows, KEY), jnp.bfloat16),
-            pltpu.VMEM(suffix.shape, jnp.bfloat16),
-            pltpu.VMEM((steps, rows // 2, LANES), jnp.bfloat16),
+            pltpu.VMEM((prefix + tail, KEY), jnp.bfloat16),
+            pltpu.VMEM((steps, PAGE, LATENT), jnp.bfloat16),
+            pltpu.VMEM((steps, PAGE // 2, LANES), jnp.bfloat16),
             pltpu.VMEM((1, prefix), jnp.float32),
             pltpu.SemaphoreType.DMA((LATENT // LANES + 2,)),
         ],
-        input_output_aliases={5: 0} if aliased else {},
+        input_output_aliases={len(operands) - 1: 0} if aliased else {},
         compiler_params=pltpu.CompilerParams(vmem_limit_bytes=58 << 20),
         name="attend",
-    )(numbers, length, queries, packed, suffix, *extra)
+    )(*operands)
 
 
 def fetch_pages(page_pool, page_owner, page_slot):
@@ -165,44 +234,57 @@
         page_id[None, None, :] // ep_size == rank_id[None, :, None]
     )
     wanted = jnp.sum(jnp.where(match, page_slot[0][None, None, :], 0), axis=2)
-    place = jnp.arange(ep_size * ranks, dtype=jnp.int32)
-    seat = page_owner[0] * ranks + page_id // ep_size
-    hit = place[:, None] == seat[None, :]
-    numbers = pages + jnp.sum(jnp.where(hit, page_id[None, :] - pages, 0), axis=1)
     asked = lax.all_to_all(wanted, "ep", split_axis=0, concat_axis=0, tiled=True)
     pool = page_pool.reshape(page_pool.shape[0], PAGE, KEY)
-    chosen = pick_pages(asked, pool)
-    fetched = lax.all_to_all(chosen, "ep", split_axis=0, concat_axis=0, tiled=True)
+    place = jnp.arange(ep_size, dtype=jnp.int32)
+
+    def number(first):
+        low = first * ep_size
+        ids = low + jnp.arange(min(ep_size, pages), dtype=jnp.int32)
+        held = lax.dynamic_slice_in_dim(page_owner[0], low, min(ep_size, pages))
+        hit = place[:, None] == held[None, :]
+        return pages + jnp.sum(jnp.where(hit, ids[None, :] - pages, 0), axis=1)
+
+    dp_size = lax.axis_size("dp")
+    if ranks == dp_size and pages == ranks * ep_size:
+        plane = lax.axis_index("dp").astype(jnp.int32)
+        chosen = pick_pages(plane.reshape(1), asked, pool)
+        own = lax.all_to_all(chosen, "ep", split_axis=0, concat_axis=0, tiled=True)
+        fetched, numbers = [own], [number(plane)]
+        for shift in range(1, dp_size):
+            fetched.append(pull(own, "dp", 1, dp_size, shift))
+            numbers.append(number(partner(plane, jnp.int32(shift), dp_size)))
+        return fetched, numbers
+    fetched, numbers = [], []
+    for r in range(ranks):
+        chosen = pick_pages(jnp.full((1,), r, jnp.int32), asked, pool)
+        fetched.append(lax.all_to_all(chosen, "ep", split_axis=0, concat_axis=0, tiled=True))
+        numbers.append(number(jnp.int32(r)))
     return fetched, numbers
 
 
-def pick_body(asked_ref, pool_ref, out_ref):
-    steps, ranks = asked_ref.shape
-    rows = ranks * PAGE
+def pick_body(rank_ref, asked_ref, pool_ref, out_ref):
     slabs = LATENT // LANES
-    for n in range(steps):
-        rotary = []
-        for r in range(ranks):
-            page = pool_ref[asked_ref[n, r]]
-            for t in range(slabs):
-                start = t * rows + r * PAGE
-                out_ref[n, start : start + PAGE] = page[:, t * LANES : (t + 1) * LANES]
-            rotary.append(page[:, LATENT:])
-        rotary = jnp.concatenate(rotary, axis=0)
-        low, high = rotary[: rows // 2], rotary[rows // 2 :]
-        out_ref[n, slabs * rows :] = jnp.concatenate([low, high], axis=1)
-
-
-def pick_pages(asked, pool):
-    steps, ranks = asked.shape
+    half = PAGE // 2
+    for n in range(asked_ref.shape[0]):
+        page = pool_ref[asked_ref[n, rank_ref[0]]]
+        for t in range(slabs):
+            out_ref[n, t * PAGE : (t + 1) * PAGE] = page[:, t * LANES : (t + 1) * LANES]
+        rotary = page[:, LATENT:]
+        out_ref[n, slabs * PAGE :] = jnp.concatenate([rotary[:half], rotary[half:]], axis=1)
+
+
+def pick_pages(rank, asked, pool):
+    scalars = pl.BlockSpec(memory_space=pltpu.SMEM)
     whole = pl.BlockSpec(memory_space=pltpu.VMEM)
+    shape = (asked.shape[0], PAGE * KEY // LANES, LANES)
     return pl.pallas_call(
         pick_body,
-        in_specs=[pl.BlockSpec(memory_space=pltpu.SMEM), whole],
+        in_specs=[scalars, scalars, whole],
         out_specs=whole,
-        out_shape=jax.ShapeDtypeStruct((steps, ranks * PAGE * KEY // LANES, LANES), pool.dtype),
+        out_shape=jax.ShapeDtypeStruct(shape, pool.dtype),
         name="pick",
-    )(asked, pool)
+    )(rank, asked, pool)
 
 
 def split_exact(values):
@@ -339,8 +421,7 @@
 def experts_square(moe_input, expert_ids, gate_weights, w_gate, w_up, w_down):
     ep_size = lax.axis_size("ep")
     outer = ep_size // 4
-    tokens, features = moe_input.shape
-    left = features // 256 * 128
+    tokens, _ = moe_input.shape
     experts = jnp.arange(ep_size, dtype=jnp.int32)
     named = expert_ids[:, :, None] == experts[None, None, :]
     dense = jnp.sum(jnp.where(named, gate_weights[:, :, None], 0.0), axis=1)
@@ -354,17 +435,13 @@
     own = jnp.concatenate([rows] + far, axis=0)
     by_x = pull(own, "dp", 1, 2, 1)
     by_y = pull(own, "ep", 2, 2, 1)
-    both_a = pull(by_x[:, :left], "ep", 2, 2, 1)
-    both_b = pull(by_y[:, left:], "dp", 1, 2, 1)
-    near = [own, by_x, by_y, both_a, both_b]
+    both = pull(by_y, "dp", 1, 2, 1)
+    near = [own, by_x, by_y, both]
     across = []
     for piece in near:
         across.append(pull(piece, "ep", 1, 2, 1))
     block = own.shape[0]
-    places = []
-    for base in (0, 4 * block):
-        places += [(base + n * block, 0) for n in range(3)]
-        places += [(base + 3 * block, 0), (base + 3 * block, left)]
+    places = [(n * block, 0) for n in range(8)]
     me = lax.axis_index("ep").astype(jnp.int32).reshape(1)
     keep, send = expert_call(
         me, near + across, tuple(places), 8 * block, ep_size, w_gate[0], w_up[0], w_down[0]
@@ -373,13 +450,11 @@
     yield None
     keep = keep + got.astype(jnp.float32)
     own, by_x, by_y, both = (keep[n * block : (n + 1) * block] for n in range(4))
-    got_a = pull(both[:, :left].astype(jnp.bfloat16), "ep", 2, 2, 1)
-    got_b = pull(both[:, left:].astype(jnp.bfloat16), "dp", 1, 2, 1)
+    got_both = pull(both.astype(jnp.bfloat16), "ep", 2, 2, 1)
+    got_y = pull(by_y.astype(jnp.bfloat16), "ep", 2, 2, 1)
     yield None
-    by_x = jnp.concatenate([by_x[:, :left] + got_a.astype(jnp.float32), by_x[:, left:]], axis=1)
-    by_y = jnp.concatenate([by_y[:, :left], by_y[:, left:] + got_b.astype(jnp.float32)], axis=1)
+    by_x = by_x + got_both.astype(jnp.float32)
     got_x = pull(by_x.astype(jnp.bfloat16), "dp", 1, 2, 1)
-    got_y = pull(by_y.astype(jnp.bfloat16), "ep", 2, 2, 1)
     yield None
     own = own + got_x.astype(jnp.float32) + got_y.astype(jnp.float32)
     got = []
@@ -408,23 +483,43 @@
     w_down,
 ):
     packed, numbers = fetch_pages(page_pool, page_owner, page_slot)
-    source = (queries, packed, suffix_latent, numbers, prefix_len)
     moe_args = (moe_input, expert_ids, gate_weights, w_gate, w_up, w_down)
     head_count = queries.shape[1] // KEY
-    if not can_square(moe_input.shape[0], w_gate.shape[2]):
+    ranks = len(packed)
+
+    def phase(rank, start, count, heads, before, so_far):
+        return attend(
+            queries,
+            packed[rank],
+            suffix_latent,
+            numbers[rank],
+            prefix_len,
+            start,
+            count,
+            heads,
+            before,
+            rank == ranks - 1,
+            so_far,
+        )
+
+    if ranks != 2 or not can_square(moe_input.shape[0], w_gate.shape[2]):
         moe_output = experts_staged(*moe_args)
-        return (attend(*source, 0, head_count, 2), moe_output)
+        state = None
+        for rank in range(ranks):
+            state = phase(rank, 0, head_count, 2, state, None)
+        return (state, moe_output)
     stages = experts_square(*moe_args)
     heads = 4
-    steps = head_count // heads
-    next(stages)
-    cuts = [0, steps // 4, 5 * steps // 8, steps]
+    half = head_count // (2 * heads) * heads
+    parts = [(0, half), (half, head_count - half)]
+    states = []
+    for part in parts:
+        next(stages)
+        states.append(phase(0, *part, heads, None, None))
     attn_context = None
-    for n in range(3):
+    for n, part in enumerate(parts):
         next(stages)
-        start, count = cuts[n] * heads, (cuts[n + 1] - cuts[n]) * heads
-        if count:
-            attn_context = attend(*source, start, count, heads, attn_context)
+        attn_context = phase(1, *part, heads, states[n], attn_context)
     moe_output = next(stages)
     return (attn_context, moe_output)
 

time: 198 us -> 182 us (0.919)
  the two profiles are of different devices: /device:TPU:15 before, /device:TPU:0 now
where the time goes in v4:
time: 182 us
  Pallas kernels  72.5 us (40%)
  waiting for transfers between devices  61.6 us (34%)
  starting transfers between devices  27.3 us (15%)
  other arithmetic  11.2 us (6%)
  local copies, waits for them, and re-layouts  7.43 us (4%)
    ppermute x18, waiting for transfers between devices, pull(): return lax.ppermute(values, axis, pairs)  56.9 us
    pallas_call x4, Pallas kernels, attend(): pl.pallas_call(functools.partial(attention_body, heads=heads, together=to...  54.4 us
    ppermute x18, starting transfers between devices, pull(): return lax.ppermute(values, axis, pairs)  19.3 us
    pallas_call x1, Pallas kernels, expert_call(): pl.pallas_call(functools.partial(expert_body, places=places, hidden_steps...  15.8 us
    another operation x2, other arithmetic  5.82 us
    unnamed x29, local copies, waits for them, and re-layouts  4.94 us
    all_to_all x1, waiting for transfers between devices, fetch_pages(): lax.all_to_all(wanted, 'ep', split_axis=0, concat_axis=0, tiled=True)  4.7 us
    all_to_all x1, starting transfers between devices, fetch_pages(): lax.all_to_all(wanted, 'ep', split_axis=0, concat_axis=0, tiled=True)  4.11 us
  transfers between devices with their start and end apart: 20, of which 9 were waited for; matrix products, arithmetic and copies ran while one was open for 7% of the time, Pallas kernels for 31%

profile of v4, /device:TPU:0, one launch (start us, length us, event | category | flops | bytes accessed | tf_op | source)
XLA Modules:
  0.0 181.6 jit_solution(8746553800797716526)
XLA Ops:
  2.4 0.9 pad_maximum_fusion.1
  3.3 5.1 %collective-permute-start.3 = (bf16[16,3712]{1,0:T(8,128)(2,1)S(1)}, bf16[16,3712]{1,0:T(8,128)(2,1)S(1)}, u32[]{:S(2)}, u32[]{:S(2)}) collective-permute-start(bf16[16,3712]{1,0:T(8,128)(2,1)S(1)} %pad_maximum_fusion.1), channel_id=1, source_target_pairs={{12,0},{13,1},{14,2},{15,3},{8,4},{9,5},{10,6},{11,7},{4,8},{5,9},... | collective-permute-start | bytes 356360 | tf_op jit(solution)/shard_map/ppermute | solution.py:33
  9.0 3.5 %collective-permute-done.3 = bf16[16,3712]{1,0:T(8,128)(2,1)S(1)} collective-permute-done((bf16[16,3712]{1,0:T(8,128)(2,1)S(1)}, bf16[16,3712]{1,0:T(8,128)(2,1)S(1)}, u32[]{:S(2)}, u32[]{:S(2)}) %collective-permute-start.3) | collective-permute-done | bytes 118816 | tf_op jit(solution)/shard_map/ppermute | solution.py:33
  12.6 5.8 %collective-permute-done.2 = bf16[16,3712]{1,0:T(8,128)(2,1)S(1)} collective-permute-done((bf16[16,3712]{1,0:T(8,128)(2,1)S(1)}, bf16[16,3712]{1,0:T(8,128)(2,1)S(1)}, u32[]{:S(2)}, u32[]{:S(2)}) %collective-permute-start.2) | collective-permute-done | bytes 118816 | tf_op jit(solution)/shard_map/ppermute | solution.py:33
  18.4 0.9 pad_maximum_fusion.refs_0_
  19.4 1.6 collective-permute-start.5
  21.0 1.5 collective-permute-start.4
  22.4 8.9 %collective-permute-done.5.refs_2_ = bf16[64,3712]{1,0:T(8,128)(2,1)S(1)} collective-permute-done((bf16[64,3712]{1,0:T(8,128)(2,1)S(1)}, bf16[64,3712]{1,0:T(8,128)(2,1)S(1)}, u32[]{:S(2)}, u32[]{:S(2)}) %collective-permute-start.5) | collective-permute-done | bytes 475168 | tf_op jit(solution)/shard_map/ppermute | solution.py:33
  31.4 1.5 collective-permute-start.6
  33.5 9.3 %collective-permute-done.6.refs_3_ = bf16[64,3712]{1,0:T(8,128)(2,1)S(1)} collective-permute-done((bf16[64,3712]{1,0:T(8,128)(2,1)S(1)}, bf16[64,3712]{1,0:T(8,128)(2,1)S(1)}, u32[]{:S(2)}, u32[]{:S(2)}) %collective-permute-start.6) | collective-permute-done | bytes 475168 | tf_op jit(solution)/shard_map/ppermute | solution.py:33
  42.9 1.9 %collective-permute-done.10.refs_7_ = bf16[64,3712]{1,0:T(8,128)(2,1)} collective-permute-done((bf16[64,3712]{1,0:T(8,128)(2,1)S(1)}, bf16[64,3712]{1,0:T(8,128)(2,1)}, u32[]{:S(2)}, u32[]{:S(2)}) %collective-permute-start.10) | collective-permute-done | bytes 475168 | tf_op jit(solution)/shard_map/ppermute | solution.py:33
  44.9 15.8 %expert.1 = (f32[256,3584]{1,0:T(8,128)}, bf16[256,3584]{1,0:T(8,128)(2,1)}) custom-call(s32[1]{0:T(128)} %bitcast.7.me_ref, bf16[64,3712]{1,0:T(8,128)(2,1)} %copy-done.2, bf16[64,3712]{1,0:T(8,128)(2,1)} %copy-done.5, bf16[64,3712]{1,0:T(8,128)(2,1)} %copy-done.4, bf16[64,3712]{1,0:T(8,128)(2,1)} %copy-done.6, bf16[64,3712]{1,0:T(8,128)(2,1)} %copy-done.7, ...), custom_call_target="tpu_custom_call" | custom-call | tf_op jit(solution)/shard_map/expert/pallas_call | solution.py:387
  61.7 4.1 %all-to-all-start = ((s32[16,1,2]{2,1,0:T(1,128)}), s32[16,1,2]{2,1,0:T(1,128)S(1)}, u32[]{:S(2)}, u32[]{:S(2)}) async-start(s32[16,1,2]{2,1,0:T(1,128)} %copy.27), calls=%async_computation | async-start | bytes 16384 | tf_op jit(solution)/shard_map/all_to_all | solution.py:237
  65.8 1.6 reshape.119.pool_ref
  67.4 4.7 %all-to-all-done = s32[16,1,2]{2,1,0:T(1,128)S(1)} async-done(((s32[16,1,2]{2,1,0:T(1,128)}), s32[16,1,2]{2,1,0:T(1,128)S(1)}, u32[]{:S(2)}, u32[]{:S(2)}) %all-to-all-start) | async-done | bytes 160 | tf_op jit(solution)/shard_map/all_to_all | solution.py:237
  72.7 2.3 %pick.1 = bf16[16,288,128]{2,1,0:T(8,128)(2,1)} custom-call(s32[1]{0:T(128)} %bitcast.1.rank_ref, s32[16,2]{1,0:T(8,128)} %bitcast.16, bf16[8,64,576]{2,1,0:T(8,128)(2,1)} %reshape.119.pool_ref), custom_call_target="tpu_custom_call" | custom-call | tf_op jit(solution)/shard_map/pick/pallas_call | solution.py:281
  75.1 3.9 %all-to-all-start.1 = ((bf16[16,288,128]{2,1,0:T(8,128)(2,1)}), bf16[16,288,128]{2,1,0:T(8,128)(2,1)S(1)}, u32[]{:S(2)}, u32[]{:S(2)}) async-start(bf16[16,288,128]{2,1,0:T(8,128)(2,1)} %pick.1), calls=%async_computation.1 | async-start | bytes 2359296 | tf_op jit(solution)/shard_map/all_to_all | solution.py:252
  79.0 4.5 %fusion.13 = (bf16[256,3584]{1,0:T(8,128)(2,1)S(1)}, f32[256,3584]{1,0:T(8,128)}) fusion(f32[256,3584]{1,0:T(8,128)} %get-tuple-element.12, bf16[256,3584]{1,0:T(8,128)(2,1)S(1)} %collective-permute-done.11), kind=kLoop, calls=%fused_computation.40 | loop fusion | flops 2752512 | bytes 11010048 | tf_op jit(solution)/shard_map/convert.4
  83.5 1.7 collective-permute-start.12
  85.7 19.0 %collective-permute-done.12 = bf16[64,3584]{1,0:T(8,128)(2,1)S(1)} collective-permute-done((bf16[64,3584]{1,0:T(8,128)(2,1)S(1)}, bf16[64,3584]{1,0:T(8,128)(2,1)S(1)}, u32[]{:S(2)}, u32[]{:S(2)}) %collective-permute-start.12) | collective-permute-done | bytes 458784 | tf_op jit(solution)/shard_map/ppermute | solution.py:33
  104.8 1.3 fusion
  106.0 1.6 collective-permute-start.13
  108.2 1.7 copy.30.refs_4_
  111.2 2.8 %collective-permute-done.14 = bf16[64,3584]{1,0:T(8,128)(2,1)S(1)} collective-permute-done((bf16[64,3584]{1,0:T(8,128)(2,1)S(1)}, bf16[64,3584]{1,0:T(8,128)(2,1)S(1)}, u32[]{:S(2)}, u32[]{:S(2)}) %collective-permute-start.14) | collective-permute-done | bytes 458784 | tf_op jit(solution)/shard_map/ppermute | solution.py:33
  114.1 5.4 %collective-permute-done.13 = bf16[64,3584]{1,0:T(8,128)(2,1)S(1)} collective-permute-done((bf16[64,3584]{1,0:T(8,128)(2,1)S(1)}, bf16[64,3584]{1,0:T(8,128)(2,1)S(1)}, u32[]{:S(2)}, u32[]{:S(2)}) %collective-permute-start.13) | collective-permute-done | bytes 458784 | tf_op jit(solution)/shard_map/ppermute | solution.py:33
  119.5 1.3 fusion.11
  121.2 3.2 %collective-permute-start.17 = (bf16[16,3584]{1,0:T(8,128)(2,1)S(1)}, bf16[16,3584]{1,0:T(8,128)(2,1)S(1)}, u32[]{:S(2)}, u32[]{:S(2)}) collective-permute-start(bf16[16,3584]{1,0:T(8,128)(2,1)S(1)} %get-tuple-element.21), channel_id=1, source_target_pairs={{0,12},{1,13},{2,14},{3,15},{4,8},{5,9},{6,10},{7,11},{8,4},{9,5},... | collective-permute-start | bytes 344072 | tf_op jit(solution)/shard_map/ppermute | solution.py:33
  125.4 12.8 %attend.5 = (f32[128,8192]{1,0:T(8,128)}, f32[128,2048]{1,0:T(8,128)}) custom-call(s32[16]{0:T(128)} %broadcast_add_fusion.refs_0_, s32[1]{0:T(128)S(6)} %copy.36.refs_1_, bf16[128,18432]{1,0:T(8,128)(2,1)} %refs_2_.7, bf16[16,288,128]{2,1,0:T(8,128)(2,1)} %copy-done, bf16[128,576]{1,0:T(8,128)(2,1)} %copy.30.refs_4_), custom_call_target="tpu_custom_call" | custom-call | tf_op jit(solution)/shard_map/attend/pallas_call | solution.py:199
  138.2 12.8 %attend.4 = (f32[128,8192]{1,0:T(8,128)}, f32[128,2048]{1,0:T(8,128)}) custom-call(s32[16]{0:T(128)} %broadcast_add_fusion.refs_0_, s32[1]{0:T(128)S(6)} %copy.36.refs_1_, bf16[128,18432]{1,0:T(8,128)(2,1)} %refs_2_.7, bf16[16,288,128]{2,1,0:T(8,128)(2,1)} %copy-done, bf16[128,576]{1,0:T(8,128)(2,1)} %copy.30.refs_4_), custom_call_target="tpu_custom_call" | custom-call | tf_op jit(solution)/shard_map/attend/pallas_call | solution.py:199
  151.0 1.1 copy-done.1
  152.0 14.4 %attend.6.refs_6_ = bf16[128,16384]{1,0:T(8,128)(2,1)} custom-call(s32[16]{0:T(128)} %broadcast_add_fusion.1.refs_0_, s32[1]{0:T(128)S(6)} %copy.36.refs_1_, bf16[128,18432]{1,0:T(8,128)(2,1)} %refs_2_.7, bf16[16,288,128]{2,1,0:T(8,128)(2,1)} %copy-done.1, f32[128,8192]{1,0:T(8,128)} %get-tuple-element.10.refs_4_, f32[128,2048]{1,0:T(8,128)} %get-tuple-element.11.refs_5_), custom_call_target="tpu_custom_call" | custom-call | tf_op jit(solution)/shard_map/attend/pallas_call | solution.py:199
  166.4 14.4 %attend.7 = bf16[128,16384]{1,0:T(8,128)(2,1)} custom-call(s32[16]{0:T(128)} %broadcast_add_fusion.1.refs_0_, s32[1]{0:T(128)S(6)} %copy.36.refs_1_, bf16[128,18432]{1,0:T(8,128)(2,1)} %refs_2_.7, bf16[16,288,128]{2,1,0:T(8,128)(2,1)} %copy-done.1, f32[128,8192]{1,0:T(8,128)} %get-tuple-element.8.refs_4_, ...), custom_call_target="tpu_custom_call", output_to_operand_aliasing={{}: (6, {})} | custom-call | tf_op jit(solution)/shard_map/attend/pallas_call | solution.py:199
  (67 shorter events, 8.6 us)
Async XLA Ops:
  3.3 9.3 %collective-permute-start.3 = (bf16[16,3712]{1,0:T(8,128)(2,1)S(1)}, bf16[16,3712]{1,0:T(8,128)(2,1)S(1)}, u32[]{:S(2)}, u32[]{:S(2)}) collective-permute-start(bf16[16,3712]{1,0:T(8,128)(2,1)S(1)} %pad_maximum_fusion.1), channel_id=1, source_target_pairs={{12,0},{13,1},{14,2},{15,3},{8,4},{9,5},{10,6},{11,7},{4,8},{5,9},... | collective-permute-start | bytes 356360 | tf_op jit(solution)/shard_map/ppermute | solution.py:33
  8.4 10.0 %collective-permute-start.2 = (bf16[16,3712]{1,0:T(8,128)(2,1)S(1)}, bf16[16,3712]{1,0:T(8,128)(2,1)S(1)}, u32[]{:S(2)}, u32[]{:S(2)}) collective-permute-start(bf16[16,3712]{1,0:T(8,128)(2,1)S(1)} %pad_maximum_fusion.1), channel_id=1, source_target_pairs={{8,0},{9,1},{10,2},{11,3},{12,4},{13,5},{14,6},{15,7},{0,8},{1,9},... | collective-permute-start | bytes 356360 | tf_op jit(solution)/shard_map/ppermute | solution.py:33
  8.4 10.0 %collective-permute-start.1 = (bf16[16,3712]{1,0:T(8,128)(2,1)S(1)}, bf16[16,3712]{1,0:T(8,128)(2,1)S(1)}, u32[]{:S(2)}, u32[]{:S(2)}) collective-permute-start(bf16[16,3712]{1,0:T(8,128)(2,1)S(1)} %pad_maximum_fusion.1), channel_id=1, source_target_pairs={{4,0},{5,1},{6,2},{7,3},{0,4},{1,5},{2,6},{3,7},{12,8},{13,9},{14,... | collective-permute-start | bytes 356360 | tf_op jit(solution)/shard_map/ppermute | solution.py:33
  19.4 25.4 %copy-start.2 = (bf16[64,3712]{1,0:T(8,128)(2,1)}, bf16[64,3712]{1,0:T(8,128)(2,1)S(1)}, u32[]{:S(2)}) copy-start(bf16[64,3712]{1,0:T(8,128)(2,1)S(1)} %pad_maximum_fusion.refs_0_) | copy-start | bytes 1425412
  19.4 12.0 %collective-permute-start.5 = (bf16[64,3712]{1,0:T(8,128)(2,1)S(1)}, bf16[64,3712]{1,0:T(8,128)(2,1)S(1)}, u32[]{:S(2)}, u32[]{:S(2)}) collective-permute-start(bf16[64,3712]{1,0:T(8,128)(2,1)S(1)} %pad_maximum_fusion.refs_0_), channel_id=1, source_target_pairs={{2,0},{3,1},{0,2},{1,3},{6,4},{7,5},{4,6},{5,7},{10,8},{11,9},{8,1... | collective-permute-start | bytes 1425416 | tf_op jit(solution)/shard_map/ppermute | solution.py:33
  21.0 12.4 %collective-permute-start.4 = (bf16[64,3712]{1,0:T(8,128)(2,1)S(1)}, bf16[64,3712]{1,0:T(8,128)(2,1)S(1)}, u32[]{:S(2)}, u32[]{:S(2)}) collective-permute-start(bf16[64,3712]{1,0:T(8,128)(2,1)S(1)} %pad_maximum_fusion.refs_0_), channel_id=1, source_target_pairs={{16,0},{0,16},{17,1},{1,17},{18,2},{2,18},{19,3},{3,19},{20,4},{4,... | collective-permute-start | bytes 1425416 | tf_op jit(solution)/shard_map/ppermute | solution.py:33
  31.4 13.4 %copy-start.4 = (bf16[64,3712]{1,0:T(8,128)(2,1)}, bf16[64,3712]{1,0:T(8,128)(2,1)S(1)}, u32[]{:S(2)}) copy-start(bf16[64,3712]{1,0:T(8,128)(2,1)S(1)} %collective-permute-done.5.refs_2_) | copy-start | bytes 1425412
  31.4 11.4 %collective-permute-start.6 = (bf16[64,3712]{1,0:T(8,128)(2,1)S(1)}, bf16[64,3712]{1,0:T(8,128)(2,1)S(1)}, u32[]{:S(2)}, u32[]{:S(2)}) collective-permute-start(bf16[64,3712]{1,0:T(8,128)(2,1)S(1)} %collective-permute-done.5.refs_2_), channel_id=1, source_target_pairs={{16,0},{0,16},{17,1},{1,17},{18,2},{2,18},{19,3},{3,19},{20,4},{4,... | collective-permute-start | bytes 1425416 | tf_op jit(solution)/shard_map/ppermute | solution.py:33
  32.9 9.9 %collective-permute-start.7 = (bf16[64,3712]{1,0:T(8,128)(2,1)S(1)}, bf16[64,3712]{1,0:T(8,128)(2,1)S(1)}, u32[]{:S(2)}, u32[]{:S(2)}) collective-permute-start(bf16[64,3712]{1,0:T(8,128)(2,1)S(1)} %pad_maximum_fusion.refs_0_), channel_id=1, source_target_pairs={{1,0},{0,1},{3,2},{2,3},{5,4},{4,5},{7,6},{6,7},{9,8},{8,9},{11,10... | collective-permute-start | bytes 1425416 | tf_op jit(solution)/shard_map/ppermute | solution.py:33
  32.9 9.9 %collective-permute-start.9 = (bf16[64,3712]{1,0:T(8,128)(2,1)S(1)}, bf16[64,3712]{1,0:T(8,128)(2,1)S(1)}, u32[]{:S(2)}, u32[]{:S(2)}) collective-permute-start(bf16[64,3712]{1,0:T(8,128)(2,1)S(1)} %collective-permute-done.5.refs_2_), channel_id=1, source_target_pairs={{1,0},{0,1},{3,2},{2,3},{5,4},{4,5},{7,6},{6,7},{9,8},{8,9},{11,10... | collective-permute-start | bytes 1425416 | tf_op jit(solution)/shard_map/ppermute | solution.py:33
  33.4 11.4 %copy-start.5 = (bf16[64,3712]{1,0:T(8,128)(2,1)}, bf16[64,3712]{1,0:T(8,128)(2,1)S(1)}, u32[]{:S(2)}) copy-start(bf16[64,3712]{1,0:T(8,128)(2,1)S(1)} %collective-permute-done.4.refs_1_) | copy-start | bytes 1425412
  33.4 9.5 %collective-permute-start.8 = (bf16[64,3712]{1,0:T(8,128)(2,1)S(1)}, bf16[64,3712]{1,0:T(8,128)(2,1)S(1)}, u32[]{:S(2)}, u32[]{:S(2)}) collective-permute-start(bf16[64,3712]{1,0:T(8,128)(2,1)S(1)} %collective-permute-done.4.refs_1_), channel_id=1, source_target_pairs={{1,0},{0,1},{3,2},{2,3},{5,4},{4,5},{7,6},{6,7},{9,8},{8,9},{11,10... | collective-permute-start | bytes 1425416 | tf_op jit(solution)/shard_map/ppermute | solution.py:33
  42.8 2.0 %copy-start.6 = (bf16[64,3712]{1,0:T(8,128)(2,1)}, bf16[64,3712]{1,0:T(8,128)(2,1)S(1)}, u32[]{:S(2)}) copy-start(bf16[64,3712]{1,0:T(8,128)(2,1)S(1)} %collective-permute-done.6.refs_3_) | copy-start | bytes 1425412
  42.8 2.0 %collective-permute-start.10 = (bf16[64,3712]{1,0:T(8,128)(2,1)S(1)}, bf16[64,3712]{1,0:T(8,128)(2,1)}, u32[]{:S(2)}, u32[]{:S(2)}) collective-permute-start(bf16[64,3712]{1,0:T(8,128)(2,1)S(1)} %collective-permute-done.6.refs_3_), channel_id=1, source_target_pairs={{1,0},{0,1},{3,2},{2,3},{5,4},{4,5},{7,6},{6,7},{9,8},{8,9},{11,10... | collective-permute-start | bytes 1425416 | tf_op jit(solution)/shard_map/ppermute | solution.py:33
  42.8 2.0 %copy-start.7 = (bf16[64,3712]{1,0:T(8,128)(2,1)}, bf16[64,3712]{1,0:T(8,128)(2,1)S(1)}, u32[]{:S(2)}) copy-start(bf16[64,3712]{1,0:T(8,128)(2,1)S(1)} %collective-permute-done.7.refs_4_) | copy-start | bytes 1425412
  42.8 2.0 %copy-start.8 = (bf16[64,3712]{1,0:T(8,128)(2,1)}, bf16[64,3712]{1,0:T(8,128)(2,1)S(1)}, u32[]{:S(2)}) copy-start(bf16[64,3712]{1,0:T(8,128)(2,1)S(1)} %collective-permute-done.9.refs_6_) | copy-start | bytes 1425412
  42.9 1.9 %copy-start.9 = (bf16[64,3712]{1,0:T(8,128)(2,1)}, bf16[64,3712]{1,0:T(8,128)(2,1)S(1)}, u32[]{:S(2)}) copy-start(bf16[64,3712]{1,0:T(8,128)(2,1)S(1)} %collective-permute-done.8.refs_5_) | copy-start | bytes 1425412
  44.8 16.0 %copy-start.11 = (s32[1,32]{1,0:T(1,128)S(1)}, s32[1,32]{1,0:T(1,128)}, u32[]{:S(2)}) copy-start(s32[1,32]{1,0:T(1,128)} %param.15) | copy-start | bytes 388
  44.8 16.0 %copy-start.12 = (s32[1,32]{1,0:T(1,128)S(1)}, s32[1,32]{1,0:T(1,128)}, u32[]{:S(2)}) copy-start(s32[1,32]{1,0:T(1,128)} %param.16) | copy-start | bytes 388
  44.8 20.9 %copy-start.3 = (bf16[8,36864]{1,0:T(8,128)(2,1)S(1)}, bf16[8,36864]{1,0:T(8,128)(2,1)}, u32[]{:S(2)}) copy-start(bf16[8,36864]{1,0:T(8,128)(2,1)} %param.14) | copy-start | bytes 1769476
  60.6 18.3 %collective-permute-start.11 = (bf16[256,3584]{1,0:T(8,128)(2,1)}, bf16[256,3584]{1,0:T(8,128)(2,1)S(1)}, u32[]{:S(2)}, u32[]{:S(2)}) collective-permute-start(bf16[256,3584]{1,0:T(8,128)(2,1)} %get-tuple-element.13), channel_id=1, source_target_pairs={{1,0},{0,1},{3,2},{2,3},{5,4},{4,5},{7,6},{6,7},{9,8},{8,9},{11,10... | collective-permute-start | bytes 5505032 | tf_op jit(solution)/shard_map/ppermute | solution.py:33
  61.7 10.5 %all-to-all-start = ((s32[16,1,2]{2,1,0:T(1,128)}), s32[16,1,2]{2,1,0:T(1,128)S(1)}, u32[]{:S(2)}, u32[]{:S(2)}) async-start(s32[16,1,2]{2,1,0:T(1,128)} %copy.27), calls=%async_computation | async-start | bytes 16384 | tf_op jit(solution)/shard_map/all_to_all | solution.py:237
  75.1 35.6 %all-to-all-start.1 = ((bf16[16,288,128]{2,1,0:T(8,128)(2,1)}), bf16[16,288,128]{2,1,0:T(8,128)(2,1)S(1)}, u32[]{:S(2)}, u32[]{:S(2)}) async-start(bf16[16,288,128]{2,1,0:T(8,128)(2,1)} %pick.1), calls=%async_computation.1 | async-start | bytes 2359296 | tf_op jit(solution)/shard_map/all_to_all | solution.py:252
  83.5 21.2 %collective-permute-start.12 = (bf16[64,3584]{1,0:T(8,128)(2,1)S(1)}, bf16[64,3584]{1,0:T(8,128)(2,1)S(1)}, u32[]{:S(2)}, u32[]{:S(2)}) collective-permute-start(bf16[64,3584]{1,0:T(8,128)(2,1)S(1)} %get-tuple-element.18), channel_id=1, source_target_pairs={{2,0},{3,1},{0,2},{1,3},{6,4},{7,5},{4,6},{5,7},{10,8},{11,9},{8,1... | collective-permute-start | bytes 1376264 | tf_op jit(solution)/shard_map/ppermute | solution.py:33
  85.3 28.8 %collective-permute-start.14 = (bf16[64,3584]{1,0:T(8,128)(2,1)S(1)}, bf16[64,3584]{1,0:T(8,128)(2,1)S(1)}, u32[]{:S(2)}, u32[]{:S(2)}) collective-permute-start(bf16[64,3584]{1,0:T(8,128)(2,1)S(1)} %get-tuple-element.19), channel_id=1, source_target_pairs={{2,0},{3,1},{0,2},{1,3},{6,4},{7,5},{4,6},{5,7},{10,8},{11,9},{8,1... | collective-permute-start | bytes 1376264 | tf_op jit(solution)/shard_map/ppermute | solution.py:33
  106.0 13.5 %collective-permute-start.13 = (bf16[64,3584]{1,0:T(8,128)(2,1)S(1)}, bf16[64,3584]{1,0:T(8,128)(2,1)S(1)}, u32[]{:S(2)}, u32[]{:S(2)}) collective-permute-start(bf16[64,3584]{1,0:T(8,128)(2,1)S(1)} %fusion), channel_id=1, source_target_pairs={{16,0},{0,16},{17,1},{1,17},{18,2},{2,18},{19,3},{3,19},{20,4},{4,... | collective-permute-start | bytes 1376264 | tf_op jit(solution)/shard_map/ppermute | solution.py:33
  110.7 14.7 %copy-start = (bf16[16,288,128]{2,1,0:T(8,128)(2,1)}, bf16[16,288,128]{2,1,0:T(8,128)(2,1)S(1)}, u32[]{:S(2)}) copy-start(bf16[16,288,128]{2,1,0:T(8,128)(2,1)S(1)} %all-to-all-done.1.refs_3_) | copy-start | bytes 3538948
  110.7 40.3 %collective-permute-start = (bf16[16,288,128]{2,1,0:T(8,128)(2,1)S(1)}, bf16[16,288,128]{2,1,0:T(8,128)(2,1)S(1)}, u32[]{:S(2)}, u32[]{:S(2)}) collective-permute-start(bf16[16,288,128]{2,1,0:T(8,128)(2,1)S(1)} %all-to-all-done.1.refs_3_), channel_id=1, source_target_pairs={{16,0},{0,16},{17,1},{1,17},{18,2},{2,18},{19,3},{3,19},{20,4},{4,... | collective-permute-start | bytes 3538952 | tf_op jit(solution)/shard_map/ppermute | solution.py:33
  120.8 60.1 %collective-permute-start.15 = (bf16[16,3584]{1,0:T(8,128)(2,1)S(1)}, bf16[16,3584]{1,0:T(8,128)(2,1)S(1)}, u32[]{:S(2)}, u32[]{:S(2)}) collective-permute-start(bf16[16,3584]{1,0:T(8,128)(2,1)S(1)} %get-tuple-element.20), channel_id=1, source_target_pairs={{0,4},{1,5},{2,6},{3,7},{4,0},{5,1},{6,2},{7,3},{8,12},{9,13},{10,... | collective-permute-start | bytes 344072 | tf_op jit(solution)/shard_map/ppermute | solution.py:33
  121.2 59.7 %collective-permute-start.17 = (bf16[16,3584]{1,0:T(8,128)(2,1)S(1)}, bf16[16,3584]{1,0:T(8,128)(2,1)S(1)}, u32[]{:S(2)}, u32[]{:S(2)}) collective-permute-start(bf16[16,3584]{1,0:T(8,128)(2,1)S(1)} %get-tuple-element.21), channel_id=1, source_target_pairs={{0,12},{1,13},{2,14},{3,15},{4,8},{5,9},{6,10},{7,11},{8,4},{9,5},... | collective-permute-start | bytes 344072 | tf_op jit(solution)/shard_map/ppermute | solution.py:33
  124.4 56.5 %collective-permute-start.16 = (bf16[16,3584]{1,0:T(8,128)(2,1)S(1)}, bf16[16,3584]{1,0:T(8,128)(2,1)S(1)}, u32[]{:S(2)}, u32[]{:S(2)}) collective-permute-start(bf16[16,3584]{1,0:T(8,128)(2,1)S(1)} %get-tuple-element.22), channel_id=1, source_target_pairs={{0,8},{1,9},{2,10},{3,11},{4,12},{5,13},{6,14},{7,15},{8,0},{9,1},... | collective-permute-start | bytes 344072 | tf_op jit(solution)/shard_map/ppermute | solution.py:33
  151.0 1.1 copy-start.1
  (1 other events, 0.6 us)

commit v5 on v4

--- a/solution.py
+++ b/solution.py
@@ -62,9 +62,9 @@
         o_ref, *refs = refs
     else:
         acc_ref, state_ref, *refs = refs
-    k_ref, page_ref, rotary_ref, bias_ref, sem = refs
+    k_ref, rotary_ref, bias_ref, sem = refs
     tokens = q_ref.shape[0]
-    steps = page_ref.shape[0]
+    steps = rotary_ref.shape[0]
     prefix = steps * PAGE
     slabs = LATENT // LANES
     factor = score_scale * math.log2(math.e)
@@ -76,16 +76,21 @@
             copies.append(
                 pltpu.make_async_copy(
                     packed_ref.at[:, pl.ds(t * PAGE, PAGE)],
-                    page_ref.at[:, :, pl.ds(t * LANES, LANES)],
+                    k_ref.at[pl.ds(0, steps), :, pl.ds(t * LANES, LANES)],
                     sem.at[t],
                 )
             )
         last = packed_ref.at[:, pl.ds(slabs * PAGE, PAGE // 2)]
         copies.append(pltpu.make_async_copy(last, rotary_ref, sem.at[slabs]))
         if tail:
-            copies.append(
-                pltpu.make_async_copy(suffix_ref, k_ref.at[pl.ds(prefix, tail)], sem.at[slabs + 1])
-            )
+            for n in range(tail // PAGE):
+                copies.append(
+                    pltpu.make_async_copy(
+                        suffix_ref.at[pl.ds(n * PAGE, PAGE)],
+                        k_ref.at[steps + n],
+                        sem.at[slabs + 1 + n],
+                    )
+                )
         for copy in copies:
             copy.start()
         lane = lax.broadcasted_iota(jnp.int32, (1, 2 * PAGE), 1)
@@ -99,13 +104,12 @@
             copy.wait()
         half = PAGE // 2
         for n in range(steps):
-            start = n * PAGE
-            k_ref[start : start + PAGE, :LATENT] = page_ref[n]
             both = rotary_ref[n]
-            k_ref[start : start + half, LATENT:] = both[:, :ROPE]
-            k_ref[start + half : start + PAGE, LATENT:] = both[:, ROPE:]
+            k_ref[n, :half, LATENT:] = both[:, :ROPE]
+            k_ref[n, half:, LATENT:] = both[:, ROPE:]
 
     bias = bias_ref[...]
+    keys = k_ref[...].reshape(prefix + tail, KEY)
     if tail:
         row = lax.broadcasted_iota(jnp.int32, (tokens, tail), 0)
         col = lax.broadcasted_iota(jnp.int32, (tokens, tail), 1)
@@ -115,7 +119,7 @@
         group = range(first, first + together)
         q = jnp.concatenate([q_ref[:, h * KEY : (h + 1) * KEY] for h in group], axis=0)
         s = lax.dot_general(
-            q, k_ref[...], (((1,), (1,)), ((), ())), preferred_element_type=jnp.float32
+            q, keys, (((1,), (1,)), ((), ())), preferred_element_type=jnp.float32
         )
         blocks = [s[:, :prefix] + bias]
         if tail:
@@ -131,7 +135,7 @@
         powers = [jnp.exp2(block * factor - shift) for block in blocks]
         total = sum(jnp.sum(power, axis=1, keepdims=True) for power in powers)
         p = jnp.concatenate([power.astype(jnp.bfloat16) for power in powers], axis=1)
-        acc = jnp.dot(p, k_ref[:, :LATENT], preferred_element_type=jnp.float32)
+        acc = jnp.dot(p, keys[:, :LATENT], preferred_element_type=jnp.float32)
         if not begins:
             scale = jnp.exp2(before * factor - shift)
             total = total + state[:, LANES - 1 :] * scale
@@ -211,11 +215,10 @@
         out_specs=out_specs,
         out_shape=out_shape,
         scratch_shapes=[
-            pltpu.VMEM((prefix + tail, KEY), jnp.bfloat16),
-            pltpu.VMEM((steps, PAGE, LATENT), jnp.bfloat16),
+            pltpu.VMEM((steps + tail // PAGE, PAGE, KEY), jnp.bfloat16),
             pltpu.VMEM((steps, PAGE // 2, LANES), jnp.bfloat16),
             pltpu.VMEM((1, prefix), jnp.float32),
-            pltpu.SemaphoreType.DMA((LATENT // LANES + 2,)),
+            pltpu.SemaphoreType.DMA((LATENT // LANES + 1 + tail // PAGE,)),
         ],
         input_output_aliases={len(operands) - 1: 0} if aliased else {},
         compiler_params=pltpu.CompilerParams(vmem_limit_bytes=58 << 20),

time: 182 us -> 182 us (level)
  no operation moved by 1% of the time
where the time goes in v5:
time: 182 us; the launch traced here: 181 us
  Pallas kernels  72.2 us (40%)
  waiting for transfers between devices  61.6 us (34%)
  starting transfers between devices  27.3 us (15%)
  other arithmetic  11.2 us (6%)
  local copies, waits for them, and re-layouts  7.43 us (4%)
    ppermute x18, waiting for transfers between devices, pull(): return lax.ppermute(values, axis, pairs)  56.9 us
    pallas_call x4, Pallas kernels, attend(): pl.pallas_call(functools.partial(attention_body, heads=heads, together=to...  54.1 us
    ppermute x18, starting transfers between devices, pull(): return lax.ppermute(values, axis, pairs)  19.3 us
    pallas_call x1, Pallas kernels, expert_call(): pl.pallas_call(functools.partial(expert_body, places=places, hidden_steps...  15.8 us
    another operation x2, other arithmetic  5.82 us
    unnamed x29, local copies, waits for them, and re-layouts  4.94 us
    all_to_all x1, waiting for transfers between devices, fetch_pages(): lax.all_to_all(wanted, 'ep', split_axis=0, concat_axis=0, tiled=True)  4.7 us
    all_to_all x1, starting transfers between devices, fetch_pages(): lax.all_to_all(wanted, 'ep', split_axis=0, concat_axis=0, tiled=True)  4.11 us
  transfers between devices with their start and end apart: 20, of which 9 were waited for; matrix products, arithmetic and copies ran while one was open for 7% of the time, Pallas kernels for 31%

profile of v5, /device:TPU:0, one launch (start us, length us, event | category | flops | bytes accessed | tf_op | source)
XLA Modules:
  0.0 181.3 jit_solution(9080184318735719322)
XLA Ops:
  2.4 0.9 pad_maximum_fusion.1
  3.3 5.1 %collective-permute-start.3 = (bf16[16,3712]{1,0:T(8,128)(2,1)S(1)}, bf16[16,3712]{1,0:T(8,128)(2,1)S(1)}, u32[]{:S(2)}, u32[]{:S(2)}) collective-permute-start(bf16[16,3712]{1,0:T(8,128)(2,1)S(1)} %pad_maximum_fusion.1), channel_id=1, source_target_pairs={{12,0},{13,1},{14,2},{15,3},{8,4},{9,5},{10,6},{11,7},{4,8},{5,9},... | collective-permute-start | bytes 356360 | tf_op jit(solution)/shard_map/ppermute | solution.py:33
  9.0 3.5 %collective-permute-done.3 = bf16[16,3712]{1,0:T(8,128)(2,1)S(1)} collective-permute-done((bf16[16,3712]{1,0:T(8,128)(2,1)S(1)}, bf16[16,3712]{1,0:T(8,128)(2,1)S(1)}, u32[]{:S(2)}, u32[]{:S(2)}) %collective-permute-start.3) | collective-permute-done | bytes 118816 | tf_op jit(solution)/shard_map/ppermute | solution.py:33
  12.6 5.8 %collective-permute-done.2 = bf16[16,3712]{1,0:T(8,128)(2,1)S(1)} collective-permute-done((bf16[16,3712]{1,0:T(8,128)(2,1)S(1)}, bf16[16,3712]{1,0:T(8,128)(2,1)S(1)}, u32[]{:S(2)}, u32[]{:S(2)}) %collective-permute-start.2) | collective-permute-done | bytes 118816 | tf_op jit(solution)/shard_map/ppermute | solution.py:33
  18.4 0.9 pad_maximum_fusion.refs_0_
  19.4 1.6 collective-permute-start.5
  21.0 1.5 collective-permute-start.4
  22.4 8.9 %collective-permute-done.5.refs_2_ = bf16[64,3712]{1,0:T(8,128)(2,1)S(1)} collective-permute-done((bf16[64,3712]{1,0:T(8,128)(2,1)S(1)}, bf16[64,3712]{1,0:T(8,128)(2,1)S(1)}, u32[]{:S(2)}, u32[]{:S(2)}) %collective-permute-start.5) | collective-permute-done | bytes 475168 | tf_op jit(solution)/shard_map/ppermute | solution.py:33
  31.4 1.5 collective-permute-start.6
  33.5 9.3 %collective-permute-done.6.refs_3_ = bf16[64,3712]{1,0:T(8,128)(2,1)S(1)} collective-permute-done((bf16[64,3712]{1,0:T(8,128)(2,1)S(1)}, bf16[64,3712]{1,0:T(8,128)(2,1)S(1)}, u32[]{:S(2)}, u32[]{:S(2)}) %collective-permute-start.6) | collective-permute-done | bytes 475168 | tf_op jit(solution)/shard_map/ppermute | solution.py:33
  42.9 1.9 %collective-permute-done.10.refs_7_ = bf16[64,3712]{1,0:T(8,128)(2,1)} collective-permute-done((bf16[64,3712]{1,0:T(8,128)(2,1)S(1)}, bf16[64,3712]{1,0:T(8,128)(2,1)}, u32[]{:S(2)}, u32[]{:S(2)}) %collective-permute-start.10) | collective-permute-done | bytes 475168 | tf_op jit(solution)/shard_map/ppermute | solution.py:33
  44.9 15.8 %expert.1 = (f32[256,3584]{1,0:T(8,128)}, bf16[256,3584]{1,0:T(8,128)(2,1)}) custom-call(s32[1]{0:T(128)} %bitcast.7.me_ref, bf16[64,3712]{1,0:T(8,128)(2,1)} %copy-done.2, bf16[64,3712]{1,0:T(8,128)(2,1)} %copy-done.5, bf16[64,3712]{1,0:T(8,128)(2,1)} %copy-done.4, bf16[64,3712]{1,0:T(8,128)(2,1)} %copy-done.6, bf16[64,3712]{1,0:T(8,128)(2,1)} %copy-done.7, ...), custom_call_target="tpu_custom_call" | custom-call | tf_op jit(solution)/shard_map/expert/pallas_call | solution.py:390
  61.7 4.1 %all-to-all-start = ((s32[16,1,2]{2,1,0:T(1,128)}), s32[16,1,2]{2,1,0:T(1,128)S(1)}, u32[]{:S(2)}, u32[]{:S(2)}) async-start(s32[16,1,2]{2,1,0:T(1,128)} %copy.27), calls=%async_computation | async-start | bytes 16384 | tf_op jit(solution)/shard_map/all_to_all | solution.py:240
  65.8 1.6 reshape.119.pool_ref
  67.4 4.7 %all-to-all-done = s32[16,1,2]{2,1,0:T(1,128)S(1)} async-done(((s32[16,1,2]{2,1,0:T(1,128)}), s32[16,1,2]{2,1,0:T(1,128)S(1)}, u32[]{:S(2)}, u32[]{:S(2)}) %all-to-all-start) | async-done | bytes 160 | tf_op jit(solution)/shard_map/all_to_all | solution.py:240
  72.7 2.3 %pick.1 = bf16[16,288,128]{2,1,0:T(8,128)(2,1)} custom-call(s32[1]{0:T(128)} %bitcast.1.rank_ref, s32[16,2]{1,0:T(8,128)} %bitcast.16, bf16[8,64,576]{2,1,0:T(8,128)(2,1)} %reshape.119.pool_ref), custom_call_target="tpu_custom_call" | custom-call | tf_op jit(solution)/shard_map/pick/pallas_call | solution.py:284
  75.1 3.9 %all-to-all-start.1 = ((bf16[16,288,128]{2,1,0:T(8,128)(2,1)}), bf16[16,288,128]{2,1,0:T(8,128)(2,1)S(1)}, u32[]{:S(2)}, u32[]{:S(2)}) async-start(bf16[16,288,128]{2,1,0:T(8,128)(2,1)} %pick.1), calls=%async_computation.1 | async-start | bytes 2359296 | tf_op jit(solution)/shard_map/all_to_all | solution.py:255
  79.0 4.5 %fusion.13 = (bf16[256,3584]{1,0:T(8,128)(2,1)S(1)}, f32[256,3584]{1,0:T(8,128)}) fusion(f32[256,3584]{1,0:T(8,128)} %get-tuple-element.12, bf16[256,3584]{1,0:T(8,128)(2,1)S(1)} %collective-permute-done.11), kind=kLoop, calls=%fused_computation.40 | loop fusion | flops 2752512 | bytes 11010048 | tf_op jit(solution)/shard_map/convert.4
  83.5 1.7 collective-permute-start.12
  85.7 19.0 %collective-permute-done.12 = bf16[64,3584]{1,0:T(8,128)(2,1)S(1)} collective-permute-done((bf16[64,3584]{1,0:T(8,128)(2,1)S(1)}, bf16[64,3584]{1,0:T(8,128)(2,1)S(1)}, u32[]{:S(2)}, u32[]{:S(2)}) %collective-permute-start.12) | collective-permute-done | bytes 458784 | tf_op jit(solution)/shard_map/ppermute | solution.py:33
  104.8 1.3 fusion
  106.0 1.6 collective-permute-start.13
  108.2 1.7 copy.30.refs_4_
  111.2 2.8 %collective-permute-done.14 = bf16[64,3584]{1,0:T(8,128)(2,1)S(1)} collective-permute-done((bf16[64,3584]{1,0:T(8,128)(2,1)S(1)}, bf16[64,3584]{1,0:T(8,128)(2,1)S(1)}, u32[]{:S(2)}, u32[]{:S(2)}) %collective-permute-start.14) | collective-permute-done | bytes 458784 | tf_op jit(solution)/shard_map/ppermute | solution.py:33
  114.1 5.4 %collective-permute-done.13 = bf16[64,3584]{1,0:T(8,128)(2,1)S(1)} collective-permute-done((bf16[64,3584]{1,0:T(8,128)(2,1)S(1)}, bf16[64,3584]{1,0:T(8,128)(2,1)S(1)}, u32[]{:S(2)}, u32[]{:S(2)}) %collective-permute-start.13) | collective-permute-done | bytes 458784 | tf_op jit(solution)/shard_map/ppermute | solution.py:33
  119.5 1.3 fusion.11
  121.2 3.2 %collective-permute-start.17 = (bf16[16,3584]{1,0:T(8,128)(2,1)S(1)}, bf16[16,3584]{1,0:T(8,128)(2,1)S(1)}, u32[]{:S(2)}, u32[]{:S(2)}) collective-permute-start(bf16[16,3584]{1,0:T(8,128)(2,1)S(1)} %get-tuple-element.21), channel_id=1, source_target_pairs={{0,12},{1,13},{2,14},{3,15},{4,8},{5,9},{6,10},{7,11},{8,4},{9,5},... | collective-permute-start | bytes 344072 | tf_op jit(solution)/shard_map/ppermute | solution.py:33
  125.4 12.7 %attend.5 = (f32[128,8192]{1,0:T(8,128)}, f32[128,2048]{1,0:T(8,128)}) custom-call(s32[16]{0:T(128)} %broadcast_add_fusion.refs_0_, s32[1]{0:T(128)S(6)} %copy.36.refs_1_, bf16[128,18432]{1,0:T(8,128)(2,1)} %refs_2_.7, bf16[16,288,128]{2,1,0:T(8,128)(2,1)} %copy-done, bf16[128,576]{1,0:T(8,128)(2,1)} %copy.30.refs_4_), custom_call_target="tpu_custom_call" | custom-call | tf_op jit(solution)/shard_map/attend/pallas_call | solution.py:203
  138.1 12.8 %attend.4 = (f32[128,8192]{1,0:T(8,128)}, f32[128,2048]{1,0:T(8,128)}) custom-call(s32[16]{0:T(128)} %broadcast_add_fusion.refs_0_, s32[1]{0:T(128)S(6)} %copy.36.refs_1_, bf16[128,18432]{1,0:T(8,128)(2,1)} %refs_2_.7, bf16[16,288,128]{2,1,0:T(8,128)(2,1)} %copy-done, bf16[128,576]{1,0:T(8,128)(2,1)} %copy.30.refs_4_), custom_call_target="tpu_custom_call" | custom-call | tf_op jit(solution)/shard_map/attend/pallas_call | solution.py:203
  150.9 1.1 copy-done.1
  151.9 14.3 %attend.6.refs_6_ = bf16[128,16384]{1,0:T(8,128)(2,1)} custom-call(s32[16]{0:T(128)} %broadcast_add_fusion.1.refs_0_, s32[1]{0:T(128)S(6)} %copy.36.refs_1_, bf16[128,18432]{1,0:T(8,128)(2,1)} %refs_2_.7, bf16[16,288,128]{2,1,0:T(8,128)(2,1)} %copy-done.1, f32[128,8192]{1,0:T(8,128)} %get-tuple-element.10.refs_4_, f32[128,2048]{1,0:T(8,128)} %get-tuple-element.11.refs_5_), custom_call_target="tpu_custom_call" | custom-call | tf_op jit(solution)/shard_map/attend/pallas_call | solution.py:203
  166.2 14.3 %attend.7 = bf16[128,16384]{1,0:T(8,128)(2,1)} custom-call(s32[16]{0:T(128)} %broadcast_add_fusion.1.refs_0_, s32[1]{0:T(128)S(6)} %copy.36.refs_1_, bf16[128,18432]{1,0:T(8,128)(2,1)} %refs_2_.7, bf16[16,288,128]{2,1,0:T(8,128)(2,1)} %copy-done.1, f32[128,8192]{1,0:T(8,128)} %get-tuple-element.8.refs_4_, ...), custom_call_target="tpu_custom_call", output_to_operand_aliasing={{}: (6, {})} | custom-call | tf_op jit(solution)/shard_map/attend/pallas_call | solution.py:203
  (67 shorter events, 8.6 us)
Async XLA Ops:
  3.3 9.3 %collective-permute-start.3 = (bf16[16,3712]{1,0:T(8,128)(2,1)S(1)}, bf16[16,3712]{1,0:T(8,128)(2,1)S(1)}, u32[]{:S(2)}, u32[]{:S(2)}) collective-permute-start(bf16[16,3712]{1,0:T(8,128)(2,1)S(1)} %pad_maximum_fusion.1), channel_id=1, source_target_pairs={{12,0},{13,1},{14,2},{15,3},{8,4},{9,5},{10,6},{11,7},{4,8},{5,9},... | collective-permute-start | bytes 356360 | tf_op jit(solution)/shard_map/ppermute | solution.py:33
  8.4 10.0 %collective-permute-start.2 = (bf16[16,3712]{1,0:T(8,128)(2,1)S(1)}, bf16[16,3712]{1,0:T(8,128)(2,1)S(1)}, u32[]{:S(2)}, u32[]{:S(2)}) collective-permute-start(bf16[16,3712]{1,0:T(8,128)(2,1)S(1)} %pad_maximum_fusion.1), channel_id=1, source_target_pairs={{8,0},{9,1},{10,2},{11,3},{12,4},{13,5},{14,6},{15,7},{0,8},{1,9},... | collective-permute-start | bytes 356360 | tf_op jit(solution)/shard_map/ppermute | solution.py:33
  8.4 10.0 %collective-permute-start.1 = (bf16[16,3712]{1,0:T(8,128)(2,1)S(1)}, bf16[16,3712]{1,0:T(8,128)(2,1)S(1)}, u32[]{:S(2)}, u32[]{:S(2)}) collective-permute-start(bf16[16,3712]{1,0:T(8,128)(2,1)S(1)} %pad_maximum_fusion.1), channel_id=1, source_target_pairs={{4,0},{5,1},{6,2},{7,3},{0,4},{1,5},{2,6},{3,7},{12,8},{13,9},{14,... | collective-permute-start | bytes 356360 | tf_op jit(solution)/shard_map/ppermute | solution.py:33
  19.4 25.4 %copy-start.2 = (bf16[64,3712]{1,0:T(8,128)(2,1)}, bf16[64,3712]{1,0:T(8,128)(2,1)S(1)}, u32[]{:S(2)}) copy-start(bf16[64,3712]{1,0:T(8,128)(2,1)S(1)} %pad_maximum_fusion.refs_0_) | copy-start | bytes 1425412
  19.4 12.0 %collective-permute-start.5 = (bf16[64,3712]{1,0:T(8,128)(2,1)S(1)}, bf16[64,3712]{1,0:T(8,128)(2,1)S(1)}, u32[]{:S(2)}, u32[]{:S(2)}) collective-permute-start(bf16[64,3712]{1,0:T(8,128)(2,1)S(1)} %pad_maximum_fusion.refs_0_), channel_id=1, source_target_pairs={{2,0},{3,1},{0,2},{1,3},{6,4},{7,5},{4,6},{5,7},{10,8},{11,9},{8,1... | collective-permute-start | bytes 1425416 | tf_op jit(solution)/shard_map/ppermute | solution.py:33
  21.0 12.4 %collective-permute-start.4 = (bf16[64,3712]{1,0:T(8,128)(2,1)S(1)}, bf16[64,3712]{1,0:T(8,128)(2,1)S(1)}, u32[]{:S(2)}, u32[]{:S(2)}) collective-permute-start(bf16[64,3712]{1,0:T(8,128)(2,1)S(1)} %pad_maximum_fusion.refs_0_), channel_id=1, source_target_pairs={{16,0},{0,16},{17,1},{1,17},{18,2},{2,18},{19,3},{3,19},{20,4},{4,... | collective-permute-start | bytes 1425416 | tf_op jit(solution)/shard_map/ppermute | solution.py:33
  31.4 13.4 %copy-start.4 = (bf16[64,3712]{1,0:T(8,128)(2,1)}, bf16[64,3712]{1,0:T(8,128)(2,1)S(1)}, u32[]{:S(2)}) copy-start(bf16[64,3712]{1,0:T(8,128)(2,1)S(1)} %collective-permute-done.5.refs_2_) | copy-start | bytes 1425412
  31.4 11.4 %collective-permute-start.6 = (bf16[64,3712]{1,0:T(8,128)(2,1)S(1)}, bf16[64,3712]{1,0:T(8,128)(2,1)S(1)}, u32[]{:S(2)}, u32[]{:S(2)}) collective-permute-start(bf16[64,3712]{1,0:T(8,128)(2,1)S(1)} %collective-permute-done.5.refs_2_), channel_id=1, source_target_pairs={{16,0},{0,16},{17,1},{1,17},{18,2},{2,18},{19,3},{3,19},{20,4},{4,... | collective-permute-start | bytes 1425416 | tf_op jit(solution)/shard_map/ppermute | solution.py:33
  32.9 9.9 %collective-permute-start.7 = (bf16[64,3712]{1,0:T(8,128)(2,1)S(1)}, bf16[64,3712]{1,0:T(8,128)(2,1)S(1)}, u32[]{:S(2)}, u32[]{:S(2)}) collective-permute-start(bf16[64,3712]{1,0:T(8,128)(2,1)S(1)} %pad_maximum_fusion.refs_0_), channel_id=1, source_target_pairs={{1,0},{0,1},{3,2},{2,3},{5,4},{4,5},{7,6},{6,7},{9,8},{8,9},{11,10... | collective-permute-start | bytes 1425416 | tf_op jit(solution)/shard_map/ppermute | solution.py:33
  32.9 9.9 %collective-permute-start.9 = (bf16[64,3712]{1,0:T(8,128)(2,1)S(1)}, bf16[64,3712]{1,0:T(8,128)(2,1)S(1)}, u32[]{:S(2)}, u32[]{:S(2)}) collective-permute-start(bf16[64,3712]{1,0:T(8,128)(2,1)S(1)} %collective-permute-done.5.refs_2_), channel_id=1, source_target_pairs={{1,0},{0,1},{3,2},{2,3},{5,4},{4,5},{7,6},{6,7},{9,8},{8,9},{11,10... | collective-permute-start | bytes 1425416 | tf_op jit(solution)/shard_map/ppermute | solution.py:33
  33.4 11.4 %copy-start.5 = (bf16[64,3712]{1,0:T(8,128)(2,1)}, bf16[64,3712]{1,0:T(8,128)(2,1)S(1)}, u32[]{:S(2)}) copy-start(bf16[64,3712]{1,0:T(8,128)(2,1)S(1)} %collective-permute-done.4.refs_1_) | copy-start | bytes 1425412
  33.4 9.5 %collective-permute-start.8 = (bf16[64,3712]{1,0:T(8,128)(2,1)S(1)}, bf16[64,3712]{1,0:T(8,128)(2,1)S(1)}, u32[]{:S(2)}, u32[]{:S(2)}) collective-permute-start(bf16[64,3712]{1,0:T(8,128)(2,1)S(1)} %collective-permute-done.4.refs_1_), channel_id=1, source_target_pairs={{1,0},{0,1},{3,2},{2,3},{5,4},{4,5},{7,6},{6,7},{9,8},{8,9},{11,10... | collective-permute-start | bytes 1425416 | tf_op jit(solution)/shard_map/ppermute | solution.py:33
  42.8 2.0 %copy-start.6 = (bf16[64,3712]{1,0:T(8,128)(2,1)}, bf16[64,3712]{1,0:T(8,128)(2,1)S(1)}, u32[]{:S(2)}) copy-start(bf16[64,3712]{1,0:T(8,128)(2,1)S(1)} %collective-permute-done.6.refs_3_) | copy-start | bytes 1425412
  42.8 2.0 %collective-permute-start.10 = (bf16[64,3712]{1,0:T(8,128)(2,1)S(1)}, bf16[64,3712]{1,0:T(8,128)(2,1)}, u32[]{:S(2)}, u32[]{:S(2)}) collective-permute-start(bf16[64,3712]{1,0:T(8,128)(2,1)S(1)} %collective-permute-done.6.refs_3_), channel_id=1, source_target_pairs={{1,0},{0,1},{3,2},{2,3},{5,4},{4,5},{7,6},{6,7},{9,8},{8,9},{11,10... | collective-permute-start | bytes 1425416 | tf_op jit(solution)/shard_map/ppermute | solution.py:33
  42.8 2.0 %copy-start.7 = (bf16[64,3712]{1,0:T(8,128)(2,1)}, bf16[64,3712]{1,0:T(8,128)(2,1)S(1)}, u32[]{:S(2)}) copy-start(bf16[64,3712]{1,0:T(8,128)(2,1)S(1)} %collective-permute-done.7.refs_4_) | copy-start | bytes 1425412
  42.8 2.0 %copy-start.8 = (bf16[64,3712]{1,0:T(8,128)(2,1)}, bf16[64,3712]{1,0:T(8,128)(2,1)S(1)}, u32[]{:S(2)}) copy-start(bf16[64,3712]{1,0:T(8,128)(2,1)S(1)} %collective-permute-done.9.refs_6_) | copy-start | bytes 1425412
  42.9 1.9 %copy-start.9 = (bf16[64,3712]{1,0:T(8,128)(2,1)}, bf16[64,3712]{1,0:T(8,128)(2,1)S(1)}, u32[]{:S(2)}) copy-start(bf16[64,3712]{1,0:T(8,128)(2,1)S(1)} %collective-permute-done.8.refs_5_) | copy-start | bytes 1425412
  44.8 16.0 %copy-start.11 = (s32[1,32]{1,0:T(1,128)S(1)}, s32[1,32]{1,0:T(1,128)}, u32[]{:S(2)}) copy-start(s32[1,32]{1,0:T(1,128)} %param.15) | copy-start | bytes 388
  44.8 16.0 %copy-start.12 = (s32[1,32]{1,0:T(1,128)S(1)}, s32[1,32]{1,0:T(1,128)}, u32[]{:S(2)}) copy-start(s32[1,32]{1,0:T(1,128)} %param.16) | copy-start | bytes 388
  44.8 20.9 %copy-start.3 = (bf16[8,36864]{1,0:T(8,128)(2,1)S(1)}, bf16[8,36864]{1,0:T(8,128)(2,1)}, u32[]{:S(2)}) copy-start(bf16[8,36864]{1,0:T(8,128)(2,1)} %param.14) | copy-start | bytes 1769476
  60.6 18.3 %collective-permute-start.11 = (bf16[256,3584]{1,0:T(8,128)(2,1)}, bf16[256,3584]{1,0:T(8,128)(2,1)S(1)}, u32[]{:S(2)}, u32[]{:S(2)}) collective-permute-start(bf16[256,3584]{1,0:T(8,128)(2,1)} %get-tuple-element.13), channel_id=1, source_target_pairs={{1,0},{0,1},{3,2},{2,3},{5,4},{4,5},{7,6},{6,7},{9,8},{8,9},{11,10... | collective-permute-start | bytes 5505032 | tf_op jit(solution)/shard_map/ppermute | solution.py:33
  61.7 10.5 %all-to-all-start = ((s32[16,1,2]{2,1,0:T(1,128)}), s32[16,1,2]{2,1,0:T(1,128)S(1)}, u32[]{:S(2)}, u32[]{:S(2)}) async-start(s32[16,1,2]{2,1,0:T(1,128)} %copy.27), calls=%async_computation | async-start | bytes 16384 | tf_op jit(solution)/shard_map/all_to_all | solution.py:240
  75.1 35.6 %all-to-all-start.1 = ((bf16[16,288,128]{2,1,0:T(8,128)(2,1)}), bf16[16,288,128]{2,1,0:T(8,128)(2,1)S(1)}, u32[]{:S(2)}, u32[]{:S(2)}) async-start(bf16[16,288,128]{2,1,0:T(8,128)(2,1)} %pick.1), calls=%async_computation.1 | async-start | bytes 2359296 | tf_op jit(solution)/shard_map/all_to_all | solution.py:255
  83.5 21.2 %collective-permute-start.12 = (bf16[64,3584]{1,0:T(8,128)(2,1)S(1)}, bf16[64,3584]{1,0:T(8,128)(2,1)S(1)}, u32[]{:S(2)}, u32[]{:S(2)}) collective-permute-start(bf16[64,3584]{1,0:T(8,128)(2,1)S(1)} %get-tuple-element.18), channel_id=1, source_target_pairs={{2,0},{3,1},{0,2},{1,3},{6,4},{7,5},{4,6},{5,7},{10,8},{11,9},{8,1... | collective-permute-start | bytes 1376264 | tf_op jit(solution)/shard_map/ppermute | solution.py:33
  85.3 28.8 %collective-permute-start.14 = (bf16[64,3584]{1,0:T(8,128)(2,1)S(1)}, bf16[64,3584]{1,0:T(8,128)(2,1)S(1)}, u32[]{:S(2)}, u32[]{:S(2)}) collective-permute-start(bf16[64,3584]{1,0:T(8,128)(2,1)S(1)} %get-tuple-element.19), channel_id=1, source_target_pairs={{2,0},{3,1},{0,2},{1,3},{6,4},{7,5},{4,6},{5,7},{10,8},{11,9},{8,1... | collective-permute-start | bytes 1376264 | tf_op jit(solution)/shard_map/ppermute | solution.py:33
  106.0 13.5 %collective-permute-start.13 = (bf16[64,3584]{1,0:T(8,128)(2,1)S(1)}, bf16[64,3584]{1,0:T(8,128)(2,1)S(1)}, u32[]{:S(2)}, u32[]{:S(2)}) collective-permute-start(bf16[64,3584]{1,0:T(8,128)(2,1)S(1)} %fusion), channel_id=1, source_target_pairs={{16,0},{0,16},{17,1},{1,17},{18,2},{2,18},{19,3},{3,19},{20,4},{4,... | collective-permute-start | bytes 1376264 | tf_op jit(solution)/shard_map/ppermute | solution.py:33
  110.7 14.7 %copy-start = (bf16[16,288,128]{2,1,0:T(8,128)(2,1)}, bf16[16,288,128]{2,1,0:T(8,128)(2,1)S(1)}, u32[]{:S(2)}) copy-start(bf16[16,288,128]{2,1,0:T(8,128)(2,1)S(1)} %all-to-all-done.1.refs_3_) | copy-start | bytes 3538948
  110.7 40.2 %collective-permute-start = (bf16[16,288,128]{2,1,0:T(8,128)(2,1)S(1)}, bf16[16,288,128]{2,1,0:T(8,128)(2,1)S(1)}, u32[]{:S(2)}, u32[]{:S(2)}) collective-permute-start(bf16[16,288,128]{2,1,0:T(8,128)(2,1)S(1)} %all-to-all-done.1.refs_3_), channel_id=1, source_target_pairs={{16,0},{0,16},{17,1},{1,17},{18,2},{2,18},{19,3},{3,19},{20,4},{4,... | collective-permute-start | bytes 3538952 | tf_op jit(solution)/shard_map/ppermute | solution.py:33
  120.8 59.7 %collective-permute-start.15 = (bf16[16,3584]{1,0:T(8,128)(2,1)S(1)}, bf16[16,3584]{1,0:T(8,128)(2,1)S(1)}, u32[]{:S(2)}, u32[]{:S(2)}) collective-permute-start(bf16[16,3584]{1,0:T(8,128)(2,1)S(1)} %get-tuple-element.20), channel_id=1, source_target_pairs={{0,4},{1,5},{2,6},{3,7},{4,0},{5,1},{6,2},{7,3},{8,12},{9,13},{10,... | collective-permute-start | bytes 344072 | tf_op jit(solution)/shard_map/ppermute | solution.py:33
  121.2 59.3 %collective-permute-start.17 = (bf16[16,3584]{1,0:T(8,128)(2,1)S(1)}, bf16[16,3584]{1,0:T(8,128)(2,1)S(1)}, u32[]{:S(2)}, u32[]{:S(2)}) collective-permute-start(bf16[16,3584]{1,0:T(8,128)(2,1)S(1)} %get-tuple-element.21), channel_id=1, source_target_pairs={{0,12},{1,13},{2,14},{3,15},{4,8},{5,9},{6,10},{7,11},{8,4},{9,5},... | collective-permute-start | bytes 344072 | tf_op jit(solution)/shard_map/ppermute | solution.py:33
  124.4 56.2 %collective-permute-start.16 = (bf16[16,3584]{1,0:T(8,128)(2,1)S(1)}, bf16[16,3584]{1,0:T(8,128)(2,1)S(1)}, u32[]{:S(2)}, u32[]{:S(2)}) collective-permute-start(bf16[16,3584]{1,0:T(8,128)(2,1)S(1)} %get-tuple-element.22), channel_id=1, source_target_pairs={{0,8},{1,9},{2,10},{3,11},{4,12},{5,13},{6,14},{7,15},{8,0},{9,1},... | collective-permute-start | bytes 344072 | tf_op jit(solution)/shard_map/ppermute | solution.py:33
  150.9 1.1 copy-start.1
  (1 other events, 0.6 us)

commit v6 on v5

--- a/solution.py
+++ b/solution.py
@@ -182,8 +182,8 @@
     else:
         operands += before
         in_specs += [
-            pl.BlockSpec((tokens, heads * LATENT), lambda i: (0, i)),
-            pl.BlockSpec((tokens, heads * LANES), lambda i: (0, i)),
+            pl.BlockSpec((tokens, heads * LATENT), lambda i: (0, i + offset)),
+            pl.BlockSpec((tokens, heads * LANES), lambda i: (0, i + offset)),
         ]
     if aliased:
         operands.append(so_far)
@@ -226,6 +226,22 @@
     )(*operands)
 
 
+def lay_body(first_ref, second_ref, rows_ref, out_ref):
+    out_ref[...] = rows_ref[...]
+
+
+def lay_rows(first, second, rows):
+    scalars = pl.BlockSpec(memory_space=pltpu.SMEM)
+    whole = pl.BlockSpec(memory_space=pltpu.VMEM)
+    return pl.pallas_call(
+        lay_body,
+        in_specs=[scalars, scalars, whole],
+        out_specs=whole,
+        out_shape=jax.ShapeDtypeStruct(rows.shape, rows.dtype),
+        name="lay",
+    )(first, second, rows)
+
+
 def fetch_pages(page_pool, page_owner, page_slot):
     ep_size = lax.axis_size("ep")
     pages = page_owner.shape[1]
@@ -383,7 +399,7 @@
     features, hidden = w_gate.shape
     width = pieces[0].shape[1]
     block = 256
-    wide = 512 if features % 512 == 0 else 128
+    wide = features // 2 if features % 512 == 0 else 128
     steps = hidden // block
     anywhere = pl.BlockSpec(memory_space=pl.ANY)
     outs = pl.BlockSpec((rows // 2, wide), lambda i: (0, jnp.maximum(i - steps, 0)))
@@ -450,23 +466,25 @@
         me, near + across, tuple(places), 8 * block, ep_size, w_gate[0], w_up[0], w_down[0]
     )
     got = pull(send, "ep", 1, 2, 1)
+
+    def part(n):
+        rows = slice(n * block, (n + 1) * block)
+        return keep[rows] + got[rows].astype(jnp.float32)
+
+    got_both = pull(part(3).astype(jnp.bfloat16), "ep", 2, 2, 1)
+    got_y = pull(part(2).astype(jnp.bfloat16), "ep", 2, 2, 1)
     yield None
-    keep = keep + got.astype(jnp.float32)
-    own, by_x, by_y, both = (keep[n * block : (n + 1) * block] for n in range(4))
-    got_both = pull(both.astype(jnp.bfloat16), "ep", 2, 2, 1)
-    got_y = pull(by_y.astype(jnp.bfloat16), "ep", 2, 2, 1)
-    yield None
-    by_x = by_x + got_both.astype(jnp.float32)
+    by_x = part(1) + got_both.astype(jnp.float32)
     got_x = pull(by_x.astype(jnp.bfloat16), "dp", 1, 2, 1)
     yield None
-    own = own + got_x.astype(jnp.float32) + got_y.astype(jnp.float32)
-    got = []
+    own = part(0) + got_x.astype(jnp.float32) + got_y.astype(jnp.float32)
+    near = []
     for shift in range(1, outer):
         piece = own[shift * tokens : (shift + 1) * tokens].astype(jnp.bfloat16)
-        got.append(push(piece, "ep", 4, outer, shift))
+        near.append(push(piece, "ep", 4, outer, shift))
     yield None
     total = own[:tokens]
-    for piece in got:
+    for piece in near:
         total = total + piece.astype(jnp.float32)
     yield total.astype(jnp.bfloat16)
 
@@ -511,18 +529,17 @@
         for rank in range(ranks):
             state = phase(rank, 0, head_count, 2, state, None)
         return (state, moe_output)
+    suffix_latent = lay_rows(*numbers, suffix_latent)
     stages = experts_square(*moe_args)
     heads = 4
     half = head_count // (2 * heads) * heads
     parts = [(0, half), (half, head_count - half)]
-    states = []
+    next(stages)
+    state = phase(0, 0, head_count, heads, None, None)
+    attn_context = None
     for part in parts:
         next(stages)
-        states.append(phase(0, *part, heads, None, None))
-    attn_context = None
-    for n, part in enumerate(parts):
-        next(stages)
-        attn_context = phase(1, *part, heads, states[n], attn_context)
+        attn_context = phase(1, *part, heads, state, attn_context)
     moe_output = next(stages)
     return (attn_context, moe_output)
 

time: 182 us -> 180 us (0.989)
  Pallas kernels: 72.2 us -> 67.9 us
  starting transfers between devices: 27.3 us -> 29.3 us
    another operation x2 -> x1, other arithmetic: 5.82 us -> 1.8 us
    pallas_call x4 -> x3, Pallas kernels: 54.1 us -> 50.4 us  [attend(): pl.pallas_call(functools.partial(attention_body, heads=heads, together=to...]
    pallas_call x1, Pallas kernels: 15.8 us -> 13.5 us  [expert_call(): pl.pallas_call(functools.partial(expert_body, places=places, hidden_steps...]
    ppermute x18, starting transfers between devices: 19.3 us -> 21.3 us  [pull(): return lax.ppermute(values, axis, pairs)]
    convert_element_type x0 -> x1, other arithmetic: none -> 1.92 us  [experts_square(): got_both = pull(part(3).astype(jnp.bfloat16), 'ep', 2, 2, 1)]
    unnamed x29 -> x31, local copies, waits for them, and re-layouts: 4.94 us -> 4.89 us
  transfers between devices with their start and end apart: 20 -> 20, of which waited for: 9 -> 9; matrix products, arithmetic and copies ran while one was open for 7% -> 7% of each run, Pallas kernels for 31% -> 30%
where the time goes in v6:
time: 180 us
  Pallas kernels  67.9 us (38%)
  waiting for transfers between devices  61.6 us (34%)
  starting transfers between devices  29.3 us (16%)
  other arithmetic  11.5 us (6%)
  local copies, waits for them, and re-layouts  7.99 us (4%)
    ppermute x18, waiting for transfers between devices, pull(): return lax.ppermute(values, axis, pairs)  56.9 us
    pallas_call x3, Pallas kernels, attend(): pl.pallas_call(functools.partial(attention_body, heads=heads, together=to...  50.4 us
    ppermute x18, starting transfers between devices, pull(): return lax.ppermute(values, axis, pairs)  21.3 us
    pallas_call x1, Pallas kernels, expert_call(): pl.pallas_call(functools.partial(expert_body, places=places, hidden_steps...  13.5 us
    unnamed x31, local copies, waits for them, and re-layouts  4.89 us
    all_to_all x1, waiting for transfers between devices, fetch_pages(): lax.all_to_all(wanted, 'ep', split_axis=0, concat_axis=0, tiled=True)  4.69 us
    all_to_all x1, starting transfers between devices, fetch_pages(): lax.all_to_all(wanted, 'ep', split_axis=0, concat_axis=0, tiled=True)  4.11 us
    all_to_all x1, starting transfers between devices, fetch_pages(): own = lax.all_to_all(chosen, 'ep', split_axis=0, concat_axis=0, tiled=True)  3.88 us
  transfers between devices with their start and end apart: 20, of which 9 were waited for; matrix products, arithmetic and copies ran while one was open for 7% of the time, Pallas kernels for 30%

profile of v6, /device:TPU:0, one launch (start us, length us, event | category | flops | bytes accessed | tf_op | source)
XLA Modules:
  0.0 179.7 jit_solution(9455224698997859908)
XLA Ops:
  3.3 5.1 %collective-permute-start.3 = (bf16[16,3712]{1,0:T(8,128)(2,1)S(1)}, bf16[16,3712]{1,0:T(8,128)(2,1)S(1)}, u32[]{:S(2)}, u32[]{:S(2)}) collective-permute-start(bf16[16,3712]{1,0:T(8,128)(2,1)S(1)} %pad_maximum_fusion.1), channel_id=1, source_target_pairs={{12,0},{13,1},{14,2},{15,3},{8,4},{9,5},{10,6},{11,7},{4,8},{5,9},... | collective-permute-start | bytes 356360 | tf_op jit(solution)/shard_map/ppermute | solution.py:33
  9.0 3.5 %collective-permute-done.3 = bf16[16,3712]{1,0:T(8,128)(2,1)S(1)} collective-permute-done((bf16[16,3712]{1,0:T(8,128)(2,1)S(1)}, bf16[16,3712]{1,0:T(8,128)(2,1)S(1)}, u32[]{:S(2)}, u32[]{:S(2)}) %collective-permute-start.3) | collective-permute-done | bytes 118816 | tf_op jit(solution)/shard_map/ppermute | solution.py:33
  12.6 5.8 %collective-permute-done.2 = bf16[16,3712]{1,0:T(8,128)(2,1)S(1)} collective-permute-done((bf16[16,3712]{1,0:T(8,128)(2,1)S(1)}, bf16[16,3712]{1,0:T(8,128)(2,1)S(1)}, u32[]{:S(2)}, u32[]{:S(2)}) %collective-permute-start.2) | collective-permute-done | bytes 118816 | tf_op jit(solution)/shard_map/ppermute | solution.py:33
  19.4 1.6 collective-permute-start.5
  21.0 1.5 collective-permute-start.4
  22.4 8.9 %collective-permute-done.5.refs_2_ = bf16[64,3712]{1,0:T(8,128)(2,1)S(1)} collective-permute-done((bf16[64,3712]{1,0:T(8,128)(2,1)S(1)}, bf16[64,3712]{1,0:T(8,128)(2,1)S(1)}, u32[]{:S(2)}, u32[]{:S(2)}) %collective-permute-start.5) | collective-permute-done | bytes 475168 | tf_op jit(solution)/shard_map/ppermute | solution.py:33
  31.4 1.5 collective-permute-start.6
  33.5 9.3 %collective-permute-done.6.refs_3_ = bf16[64,3712]{1,0:T(8,128)(2,1)S(1)} collective-permute-done((bf16[64,3712]{1,0:T(8,128)(2,1)S(1)}, bf16[64,3712]{1,0:T(8,128)(2,1)S(1)}, u32[]{:S(2)}, u32[]{:S(2)}) %collective-permute-start.6) | collective-permute-done | bytes 475168 | tf_op jit(solution)/shard_map/ppermute | solution.py:33
  42.9 1.9 %collective-permute-done.10.refs_7_ = bf16[64,3712]{1,0:T(8,128)(2,1)} collective-permute-done((bf16[64,3712]{1,0:T(8,128)(2,1)S(1)}, bf16[64,3712]{1,0:T(8,128)(2,1)}, u32[]{:S(2)}, u32[]{:S(2)}) %collective-permute-start.10) | collective-permute-done | bytes 475168 | tf_op jit(solution)/shard_map/ppermute | solution.py:33
  44.9 13.5 %expert.1 = (f32[256,3584]{1,0:T(8,128)}, bf16[256,3584]{1,0:T(8,128)(2,1)}) custom-call(s32[1]{0:T(128)} %bitcast.7.me_ref, bf16[64,3712]{1,0:T(8,128)(2,1)} %copy-done.2, bf16[64,3712]{1,0:T(8,128)(2,1)} %copy-done.6, bf16[64,3712]{1,0:T(8,128)(2,1)} %copy-done.5, bf16[64,3712]{1,0:T(8,128)(2,1)} %copy-done.7, bf16[64,3712]{1,0:T(8,128)(2,1)} %copy-done.8, ...), custom_call_target="tpu_custom_call" | custom-call | tf_op jit(solution)/shard_map/expert/pallas_call | solution.py:406
  59.4 4.1 %all-to-all-start = ((s32[16,1,2]{2,1,0:T(1,128)}), s32[16,1,2]{2,1,0:T(1,128)S(1)}, u32[]{:S(2)}, u32[]{:S(2)}) async-start(s32[16,1,2]{2,1,0:T(1,128)} %copy.25), calls=%async_computation | async-start | bytes 16384 | tf_op jit(solution)/shard_map/all_to_all | solution.py:256
  63.6 1.7 reshape.119.pool_ref
  65.2 4.7 %all-to-all-done = s32[16,1,2]{2,1,0:T(1,128)S(1)} async-done(((s32[16,1,2]{2,1,0:T(1,128)}), s32[16,1,2]{2,1,0:T(1,128)S(1)}, u32[]{:S(2)}, u32[]{:S(2)}) %all-to-all-start) | async-done | bytes 160 | tf_op jit(solution)/shard_map/all_to_all | solution.py:256
  70.5 2.3 %pick.1 = bf16[16,288,128]{2,1,0:T(8,128)(2,1)} custom-call(s32[1]{0:T(128)} %bitcast.1.rank_ref, s32[16,2]{1,0:T(8,128)} %bitcast.16, bf16[8,64,576]{2,1,0:T(8,128)(2,1)} %reshape.119.pool_ref), custom_call_target="tpu_custom_call" | custom-call | tf_op jit(solution)/shard_map/pick/pallas_call | solution.py:300
  72.8 3.9 %all-to-all-start.1 = ((bf16[16,288,128]{2,1,0:T(8,128)(2,1)}), bf16[16,288,128]{2,1,0:T(8,128)(2,1)S(1)}, u32[]{:S(2)}, u32[]{:S(2)}) async-start(bf16[16,288,128]{2,1,0:T(8,128)(2,1)} %pick.1), calls=%async_computation.1 | async-start | bytes 2359296 | tf_op jit(solution)/shard_map/all_to_all | solution.py:271
  76.7 1.9 %add_convert_fusion.2 = bf16[64,3584]{1,0:T(8,128)(2,1)S(1)} fusion(f32[256,3584]{1,0:T(8,128)} %get-tuple-element.8, bf16[256,3584]{1,0:T(8,128)(2,1)S(1)} %collective-permute-done.11), kind=kLoop, calls=%fused_computation.3 | loop fusion | flops 688128 | bytes 1835008 | tf_op jit(solution)/shard_map/convert_element_type | solution.py:474
  78.7 1.7 collective-permute-start.12
  80.4 19.0 %collective-permute-done.12 = bf16[64,3584]{1,0:T(8,128)(2,1)} collective-permute-done((bf16[64,3584]{1,0:T(8,128)(2,1)S(1)}, bf16[64,3584]{1,0:T(8,128)(2,1)}, u32[]{:S(2)}, u32[]{:S(2)}) %collective-permute-start.12) | collective-permute-done | bytes 458784 | tf_op jit(solution)/shard_map/ppermute | solution.py:33
  99.4 2.6 %add_convert_fusion.1 = (bf16[64,3584]{1,0:T(8,128)(2,1)S(1)}, bf16[64,3584]{1,0:T(8,128)(2,1)}) fusion(bf16[64,3584]{1,0:T(8,128)(2,1)} %collective-permute-done.12, f32[256,3584]{1,0:T(8,128)} %get-tuple-element.8, bf16[256,3584]{1,0:T(8,128)(2,1)S(1)} %collective-permute-done.11), kind=kLoop, calls=%fused_computation.2 | loop fusion | flops 1835008 | bytes 4128768 | tf_op jit(solution)/shard_map/convert_element_type | solution.py:478
  102.0 1.5 collective-permute-start.14
  103.5 1.5 collective-permute-start.13
  105.6 1.7 copy.28.rows_ref
  108.7 5.1 %collective-permute-done.14 = bf16[64,3584]{1,0:T(8,128)(2,1)} collective-permute-done((bf16[64,3584]{1,0:T(8,128)(2,1)}, bf16[64,3584]{1,0:T(8,128)(2,1)}, u32[]{:S(2)}, u32[]{:S(2)}) %collective-permute-start.14) | collective-permute-done | bytes 458784 | tf_op jit(solution)/shard_map/ppermute | solution.py:33
  113.8 3.2 %collective-permute-done.13 = bf16[64,3584]{1,0:T(8,128)(2,1)} collective-permute-done((bf16[64,3584]{1,0:T(8,128)(2,1)S(1)}, bf16[64,3584]{1,0:T(8,128)(2,1)}, u32[]{:S(2)}, u32[]{:S(2)}) %collective-permute-start.13) | collective-permute-done | bytes 458784 | tf_op jit(solution)/shard_map/ppermute | solution.py:33
  117.0 1.8 fusion.9
  119.5 4.3 %collective-permute-start.17 = (bf16[16,3584]{1,0:T(8,128)(2,1)}, bf16[16,3584]{1,0:T(8,128)(2,1)S(1)}, u32[]{:S(2)}, u32[]{:S(2)}) collective-permute-start(bf16[16,3584]{1,0:T(8,128)(2,1)} %get-tuple-element.15), channel_id=1, source_target_pairs={{0,12},{1,13},{2,14},{3,15},{4,8},{5,9},{6,10},{7,11},{8,4},{9,5},... | collective-permute-start | bytes 344072 | tf_op jit(solution)/shard_map/ppermute | solution.py:33
  125.0 1.6 lay.1.refs_4_
  126.6 21.9 %attend.3 = (f32[128,16384]{1,0:T(8,128)}, f32[128,4096]{1,0:T(8,128)}) custom-call(s32[16]{0:T(128)} %broadcast_add_fusion.first_ref.refs_0_, s32[1]{0:T(128)S(6)} %copy.33.refs_1_, bf16[128,18432]{1,0:T(8,128)(2,1)} %refs_2_.5, bf16[16,288,128]{2,1,0:T(8,128)(2,1)} %copy-done.1, bf16[128,576]{1,0:T(8,128)(2,1)} %lay.1.refs_4_), custom_call_target="tpu_custom_call" | custom-call | tf_op jit(solution)/shard_map/attend/pallas_call | solution.py:203
  148.5 1.0 copy-done
  149.5 14.3 %attend.4.refs_6_ = bf16[128,16384]{1,0:T(8,128)(2,1)} custom-call(s32[16]{0:T(128)} %broadcast_add_fusion.1.second_ref.refs_0_, s32[1]{0:T(128)S(6)} %copy.33.refs_1_, bf16[128,18432]{1,0:T(8,128)(2,1)} %refs_2_.5, bf16[16,288,128]{2,1,0:T(8,128)(2,1)} %copy-done, f32[128,16384]{1,0:T(8,128)} %get-tuple-element.6.refs_4_, f32[128,4096]{1,0:T(8,128)} %get-tuple-element.7.refs_5_), custom_call_target="tpu_custom_call" | custom-call | tf_op jit(solution)/shard_map/attend/pallas_call | solution.py:203
  163.8 14.3 %attend.5 = bf16[128,16384]{1,0:T(8,128)(2,1)} custom-call(s32[16]{0:T(128)} %broadcast_add_fusion.1.second_ref.refs_0_, s32[1]{0:T(128)S(6)} %copy.33.refs_1_, bf16[128,18432]{1,0:T(8,128)(2,1)} %refs_2_.5, bf16[16,288,128]{2,1,0:T(8,128)(2,1)} %copy-done, f32[128,16384]{1,0:T(8,128)} %get-tuple-element.6.refs_4_, ...), custom_call_target="tpu_custom_call", output_to_operand_aliasing={{}: (6, {})} | custom-call | tf_op jit(solution)/shard_map/attend/pallas_call | solution.py:203
  178.1 1.7 fusion.2
  (68 shorter events, 9.7 us)
Async XLA Ops:
  3.3 9.3 %collective-permute-start.3 = (bf16[16,3712]{1,0:T(8,128)(2,1)S(1)}, bf16[16,3712]{1,0:T(8,128)(2,1)S(1)}, u32[]{:S(2)}, u32[]{:S(2)}) collective-permute-start(bf16[16,3712]{1,0:T(8,128)(2,1)S(1)} %pad_maximum_fusion.1), channel_id=1, source_target_pairs={{12,0},{13,1},{14,2},{15,3},{8,4},{9,5},{10,6},{11,7},{4,8},{5,9},... | collective-permute-start | bytes 356360 | tf_op jit(solution)/shard_map/ppermute | solution.py:33
  8.4 10.0 %collective-permute-start.2 = (bf16[16,3712]{1,0:T(8,128)(2,1)S(1)}, bf16[16,3712]{1,0:T(8,128)(2,1)S(1)}, u32[]{:S(2)}, u32[]{:S(2)}) collective-permute-start(bf16[16,3712]{1,0:T(8,128)(2,1)S(1)} %pad_maximum_fusion.1), channel_id=1, source_target_pairs={{8,0},{9,1},{10,2},{11,3},{12,4},{13,5},{14,6},{15,7},{0,8},{1,9},... | collective-permute-start | bytes 356360 | tf_op jit(solution)/shard_map/ppermute | solution.py:33
  8.4 10.0 %collective-permute-start.1 = (bf16[16,3712]{1,0:T(8,128)(2,1)S(1)}, bf16[16,3712]{1,0:T(8,128)(2,1)S(1)}, u32[]{:S(2)}, u32[]{:S(2)}) collective-permute-start(bf16[16,3712]{1,0:T(8,128)(2,1)S(1)} %pad_maximum_fusion.1), channel_id=1, source_target_pairs={{4,0},{5,1},{6,2},{7,3},{0,4},{1,5},{2,6},{3,7},{12,8},{13,9},{14,... | collective-permute-start | bytes 356360 | tf_op jit(solution)/shard_map/ppermute | solution.py:33
  19.4 25.4 %copy-start.2 = (bf16[64,3712]{1,0:T(8,128)(2,1)}, bf16[64,3712]{1,0:T(8,128)(2,1)S(1)}, u32[]{:S(2)}) copy-start(bf16[64,3712]{1,0:T(8,128)(2,1)S(1)} %pad_maximum_fusion.refs_0_) | copy-start | bytes 1425412
  19.4 12.0 %collective-permute-start.5 = (bf16[64,3712]{1,0:T(8,128)(2,1)S(1)}, bf16[64,3712]{1,0:T(8,128)(2,1)S(1)}, u32[]{:S(2)}, u32[]{:S(2)}) collective-permute-start(bf16[64,3712]{1,0:T(8,128)(2,1)S(1)} %pad_maximum_fusion.refs_0_), channel_id=1, source_target_pairs={{2,0},{3,1},{0,2},{1,3},{6,4},{7,5},{4,6},{5,7},{10,8},{11,9},{8,1... | collective-permute-start | bytes 1425416 | tf_op jit(solution)/shard_map/ppermute | solution.py:33
  21.0 12.4 %collective-permute-start.4 = (bf16[64,3712]{1,0:T(8,128)(2,1)S(1)}, bf16[64,3712]{1,0:T(8,128)(2,1)S(1)}, u32[]{:S(2)}, u32[]{:S(2)}) collective-permute-start(bf16[64,3712]{1,0:T(8,128)(2,1)S(1)} %pad_maximum_fusion.refs_0_), channel_id=1, source_target_pairs={{16,0},{0,16},{17,1},{1,17},{18,2},{2,18},{19,3},{3,19},{20,4},{4,... | collective-permute-start | bytes 1425416 | tf_op jit(solution)/shard_map/ppermute | solution.py:33
  31.4 13.4 %copy-start.5 = (bf16[64,3712]{1,0:T(8,128)(2,1)}, bf16[64,3712]{1,0:T(8,128)(2,1)S(1)}, u32[]{:S(2)}) copy-start(bf16[64,3712]{1,0:T(8,128)(2,1)S(1)} %collective-permute-done.5.refs_2_) | copy-start | bytes 1425412
  31.4 11.4 %collective-permute-start.6 = (bf16[64,3712]{1,0:T(8,128)(2,1)S(1)}, bf16[64,3712]{1,0:T(8,128)(2,1)S(1)}, u32[]{:S(2)}, u32[]{:S(2)}) collective-permute-start(bf16[64,3712]{1,0:T(8,128)(2,1)S(1)} %collective-permute-done.5.refs_2_), channel_id=1, source_target_pairs={{16,0},{0,16},{17,1},{1,17},{18,2},{2,18},{19,3},{3,19},{20,4},{4,... | collective-permute-start | bytes 1425416 | tf_op jit(solution)/shard_map/ppermute | solution.py:33
  32.9 9.9 %collective-permute-start.7 = (bf16[64,3712]{1,0:T(8,128)(2,1)S(1)}, bf16[64,3712]{1,0:T(8,128)(2,1)S(1)}, u32[]{:S(2)}, u32[]{:S(2)}) collective-permute-start(bf16[64,3712]{1,0:T(8,128)(2,1)S(1)} %pad_maximum_fusion.refs_0_), channel_id=1, source_target_pairs={{1,0},{0,1},{3,2},{2,3},{5,4},{4,5},{7,6},{6,7},{9,8},{8,9},{11,10... | collective-permute-start | bytes 1425416 | tf_op jit(solution)/shard_map/ppermute | solution.py:33
  32.9 10.0 %collective-permute-start.9 = (bf16[64,3712]{1,0:T(8,128)(2,1)S(1)}, bf16[64,3712]{1,0:T(8,128)(2,1)S(1)}, u32[]{:S(2)}, u32[]{:S(2)}) collective-permute-start(bf16[64,3712]{1,0:T(8,128)(2,1)S(1)} %collective-permute-done.5.refs_2_), channel_id=1, source_target_pairs={{1,0},{0,1},{3,2},{2,3},{5,4},{4,5},{7,6},{6,7},{9,8},{8,9},{11,10... | collective-permute-start | bytes 1425416 | tf_op jit(solution)/shard_map/ppermute | solution.py:33
  33.4 11.4 %copy-start.6 = (bf16[64,3712]{1,0:T(8,128)(2,1)}, bf16[64,3712]{1,0:T(8,128)(2,1)S(1)}, u32[]{:S(2)}) copy-start(bf16[64,3712]{1,0:T(8,128)(2,1)S(1)} %collective-permute-done.4.refs_1_) | copy-start | bytes 1425412
  33.4 9.4 %collective-permute-start.8 = (bf16[64,3712]{1,0:T(8,128)(2,1)S(1)}, bf16[64,3712]{1,0:T(8,128)(2,1)S(1)}, u32[]{:S(2)}, u32[]{:S(2)}) collective-permute-start(bf16[64,3712]{1,0:T(8,128)(2,1)S(1)} %collective-permute-done.4.refs_1_), channel_id=1, source_target_pairs={{1,0},{0,1},{3,2},{2,3},{5,4},{4,5},{7,6},{6,7},{9,8},{8,9},{11,10... | collective-permute-start | bytes 1425416 | tf_op jit(solution)/shard_map/ppermute | solution.py:33
  42.8 2.0 %copy-start.7 = (bf16[64,3712]{1,0:T(8,128)(2,1)}, bf16[64,3712]{1,0:T(8,128)(2,1)S(1)}, u32[]{:S(2)}) copy-start(bf16[64,3712]{1,0:T(8,128)(2,1)S(1)} %collective-permute-done.6.refs_3_) | copy-start | bytes 1425412
  42.8 2.0 %collective-permute-start.10 = (bf16[64,3712]{1,0:T(8,128)(2,1)S(1)}, bf16[64,3712]{1,0:T(8,128)(2,1)}, u32[]{:S(2)}, u32[]{:S(2)}) collective-permute-start(bf16[64,3712]{1,0:T(8,128)(2,1)S(1)} %collective-permute-done.6.refs_3_), channel_id=1, source_target_pairs={{1,0},{0,1},{3,2},{2,3},{5,4},{4,5},{7,6},{6,7},{9,8},{8,9},{11,10... | collective-permute-start | bytes 1425416 | tf_op jit(solution)/shard_map/ppermute | solution.py:33
  42.8 2.0 %copy-start.8 = (bf16[64,3712]{1,0:T(8,128)(2,1)}, bf16[64,3712]{1,0:T(8,128)(2,1)S(1)}, u32[]{:S(2)}) copy-start(bf16[64,3712]{1,0:T(8,128)(2,1)S(1)} %collective-permute-done.7.refs_4_) | copy-start | bytes 1425412
  42.8 1.9 %copy-start.10 = (bf16[64,3712]{1,0:T(8,128)(2,1)}, bf16[64,3712]{1,0:T(8,128)(2,1)S(1)}, u32[]{:S(2)}) copy-start(bf16[64,3712]{1,0:T(8,128)(2,1)S(1)} %collective-permute-done.8.refs_5_) | copy-start | bytes 1425412
  42.9 2.0 %copy-start.9 = (bf16[64,3712]{1,0:T(8,128)(2,1)}, bf16[64,3712]{1,0:T(8,128)(2,1)S(1)}, u32[]{:S(2)}) copy-start(bf16[64,3712]{1,0:T(8,128)(2,1)S(1)} %collective-permute-done.9.refs_6_) | copy-start | bytes 1425412
  44.8 13.8 %copy-start.12 = (s32[1,32]{1,0:T(1,128)S(1)}, s32[1,32]{1,0:T(1,128)}, u32[]{:S(2)}) copy-start(s32[1,32]{1,0:T(1,128)} %param.15) | copy-start | bytes 388
  44.8 13.8 %copy-start.13 = (s32[1,32]{1,0:T(1,128)S(1)}, s32[1,32]{1,0:T(1,128)}, u32[]{:S(2)}) copy-start(s32[1,32]{1,0:T(1,128)} %param.16) | copy-start | bytes 388
  44.9 18.7 %copy-start.4 = (bf16[8,36864]{1,0:T(8,128)(2,1)S(1)}, bf16[8,36864]{1,0:T(8,128)(2,1)}, u32[]{:S(2)}) copy-start(bf16[8,36864]{1,0:T(8,128)(2,1)} %param.14) | copy-start | bytes 1769476
  58.4 18.3 %collective-permute-start.11 = (bf16[256,3584]{1,0:T(8,128)(2,1)}, bf16[256,3584]{1,0:T(8,128)(2,1)S(1)}, u32[]{:S(2)}, u32[]{:S(2)}) collective-permute-start(bf16[256,3584]{1,0:T(8,128)(2,1)} %get-tuple-element.9), channel_id=1, source_target_pairs={{1,0},{0,1},{3,2},{2,3},{5,4},{4,5},{7,6},{6,7},{9,8},{8,9},{11,10... | collective-permute-start | bytes 5505032 | tf_op jit(solution)/shard_map/ppermute | solution.py:33
  59.4 10.5 %all-to-all-start = ((s32[16,1,2]{2,1,0:T(1,128)}), s32[16,1,2]{2,1,0:T(1,128)S(1)}, u32[]{:S(2)}, u32[]{:S(2)}) async-start(s32[16,1,2]{2,1,0:T(1,128)} %copy.25), calls=%async_computation | async-start | bytes 16384 | tf_op jit(solution)/shard_map/all_to_all | solution.py:256
  72.8 35.3 %all-to-all-start.1 = ((bf16[16,288,128]{2,1,0:T(8,128)(2,1)}), bf16[16,288,128]{2,1,0:T(8,128)(2,1)S(1)}, u32[]{:S(2)}, u32[]{:S(2)}) async-start(bf16[16,288,128]{2,1,0:T(8,128)(2,1)} %pick.1), calls=%async_computation.1 | async-start | bytes 2359296 | tf_op jit(solution)/shard_map/all_to_all | solution.py:271
  76.7 31.4 %copy-start.3 = (bf16[256,3584]{1,0:T(8,128)(2,1)}, bf16[256,3584]{1,0:T(8,128)(2,1)S(1)}, u32[]{:S(2)}) copy-start(bf16[256,3584]{1,0:T(8,128)(2,1)S(1)} %collective-permute-done.11) | copy-start | bytes 5505028
  78.7 20.8 %collective-permute-start.12 = (bf16[64,3584]{1,0:T(8,128)(2,1)S(1)}, bf16[64,3584]{1,0:T(8,128)(2,1)}, u32[]{:S(2)}, u32[]{:S(2)}) collective-permute-start(bf16[64,3584]{1,0:T(8,128)(2,1)S(1)} %add_convert_fusion.2), channel_id=1, source_target_pairs={{2,0},{3,1},{0,2},{1,3},{6,4},{7,5},{4,6},{5,7},{10,8},{11,9},{8,1... | collective-permute-start | bytes 1376264 | tf_op jit(solution)/shard_map/ppermute | solution.py:33
  102.0 11.8 %collective-permute-start.14 = (bf16[64,3584]{1,0:T(8,128)(2,1)}, bf16[64,3584]{1,0:T(8,128)(2,1)}, u32[]{:S(2)}, u32[]{:S(2)}) collective-permute-start(bf16[64,3584]{1,0:T(8,128)(2,1)} %get-tuple-element.13), channel_id=1, source_target_pairs={{2,0},{3,1},{0,2},{1,3},{6,4},{7,5},{4,6},{5,7},{10,8},{11,9},{8,1... | collective-permute-start | bytes 1376264 | tf_op jit(solution)/shard_map/ppermute | solution.py:33
  103.5 13.5 %collective-permute-start.13 = (bf16[64,3584]{1,0:T(8,128)(2,1)S(1)}, bf16[64,3584]{1,0:T(8,128)(2,1)}, u32[]{:S(2)}, u32[]{:S(2)}) collective-permute-start(bf16[64,3584]{1,0:T(8,128)(2,1)S(1)} %get-tuple-element.12), channel_id=1, source_target_pairs={{16,0},{0,16},{17,1},{1,17},{18,2},{2,18},{19,3},{3,19},{20,4},{4,... | collective-permute-start | bytes 1376264 | tf_op jit(solution)/shard_map/ppermute | solution.py:33
  108.1 18.5 %copy-start.1 = (bf16[16,288,128]{2,1,0:T(8,128)(2,1)}, bf16[16,288,128]{2,1,0:T(8,128)(2,1)S(1)}, u32[]{:S(2)}) copy-start(bf16[16,288,128]{2,1,0:T(8,128)(2,1)S(1)} %all-to-all-done.1.refs_3_) | copy-start | bytes 3538948
  108.1 40.4 %collective-permute-start = (bf16[16,288,128]{2,1,0:T(8,128)(2,1)S(1)}, bf16[16,288,128]{2,1,0:T(8,128)(2,1)S(1)}, u32[]{:S(2)}, u32[]{:S(2)}) collective-permute-start(bf16[16,288,128]{2,1,0:T(8,128)(2,1)S(1)} %all-to-all-done.1.refs_3_), channel_id=1, source_target_pairs={{16,0},{0,16},{17,1},{1,17},{18,2},{2,18},{19,3},{3,19},{20,4},{4,... | collective-permute-start | bytes 3538952 | tf_op jit(solution)/shard_map/ppermute | solution.py:33
  119.5 58.6 %collective-permute-start.17 = (bf16[16,3584]{1,0:T(8,128)(2,1)}, bf16[16,3584]{1,0:T(8,128)(2,1)S(1)}, u32[]{:S(2)}, u32[]{:S(2)}) collective-permute-start(bf16[16,3584]{1,0:T(8,128)(2,1)} %get-tuple-element.15), channel_id=1, source_target_pairs={{0,12},{1,13},{2,14},{3,15},{4,8},{5,9},{6,10},{7,11},{8,4},{9,5},... | collective-permute-start | bytes 344072 | tf_op jit(solution)/shard_map/ppermute | solution.py:33
  123.8 54.2 %collective-permute-start.16 = (bf16[16,3584]{1,0:T(8,128)(2,1)}, bf16[16,3584]{1,0:T(8,128)(2,1)}, u32[]{:S(2)}, u32[]{:S(2)}) collective-permute-start(bf16[16,3584]{1,0:T(8,128)(2,1)} %get-tuple-element.16), channel_id=1, source_target_pairs={{0,8},{1,9},{2,10},{3,11},{4,12},{5,13},{6,14},{7,15},{8,0},{9,1},... | collective-permute-start | bytes 344072 | tf_op jit(solution)/shard_map/ppermute | solution.py:33
  123.8 54.3 %collective-permute-start.15 = (bf16[16,3584]{1,0:T(8,128)(2,1)S(1)}, bf16[16,3584]{1,0:T(8,128)(2,1)}, u32[]{:S(2)}, u32[]{:S(2)}) collective-permute-start(bf16[16,3584]{1,0:T(8,128)(2,1)S(1)} %get-tuple-element.14), channel_id=1, source_target_pairs={{0,4},{1,5},{2,6},{3,7},{4,0},{5,1},{6,2},{7,3},{8,12},{9,13},{10,... | collective-permute-start | bytes 344072 | tf_op jit(solution)/shard_map/ppermute | solution.py:33
  (2 other events, 1.6 us)

commit v7 on v6

--- a/solution.py
+++ b/solution.py
@@ -142,7 +142,7 @@
             olds = [acc_in_ref[:, h * LATENT : (h + 1) * LATENT] for h in group]
             acc = acc + jnp.concatenate(olds, axis=0) * scale
         if ends:
-            acc = acc / total
+            acc = acc * (1.0 / total)
         else:
             lane = lax.broadcasted_iota(jnp.int32, (acc.shape[0], LANES), 1)
             state = jnp.where(lane < LANES // 2, m, total)
@@ -353,7 +353,8 @@
 
 def expert_body(me_ref, *refs, places, hidden_steps, experts, features):
     pieces = refs[: len(places)]
-    gate_ref, up_ref, down_ref, keep_ref, send_ref, x_ref, h_ref, w_ref, sem = refs[len(places) :]
+    gate_ref, up_ref, down_ref, keep_ref, send_ref, far_ref, *refs = refs[len(places) :]
+    x_ref, h_ref, w_ref, sem = refs
     step = pl.program_id(0)
 
     @pl.when(step == 0)
@@ -392,7 +393,9 @@
         total = part * w_ref[...]
         half = keep_ref.shape[0]
         keep_ref[...] = total[:half]
-        send_ref[...] = total[half:].astype(jnp.bfloat16)
+        near = half + send_ref.shape[0]
+        send_ref[...] = total[half:near].astype(jnp.bfloat16)
+        far_ref[...] = total[near:].astype(jnp.bfloat16)
 
 
 def expert_call(me, pieces, places, rows, experts, w_gate, w_up, w_down):
@@ -402,7 +405,8 @@
     wide = features // 2 if features % 512 == 0 else 128
     steps = hidden // block
     anywhere = pl.BlockSpec(memory_space=pl.ANY)
-    outs = pl.BlockSpec((rows // 2, wide), lambda i: (0, jnp.maximum(i - steps, 0)))
+    heights = (rows // 2, 3 * rows // 8, rows // 8)
+    outs = [pl.BlockSpec((n, wide), lambda i: (0, jnp.maximum(i - steps, 0))) for n in heights]
     return pl.pallas_call(
         functools.partial(
             expert_body, places=places, hidden_steps=steps, experts=experts, features=features
@@ -415,10 +419,11 @@
             pl.BlockSpec((features, block), lambda i: (0, jnp.minimum(i, steps - 1))),
             pl.BlockSpec((hidden, wide), lambda i: (0, jnp.maximum(i - steps, 0))),
         ],
-        out_specs=[outs, outs],
+        out_specs=outs,
         out_shape=[
-            jax.ShapeDtypeStruct((rows // 2, features), jnp.float32),
-            jax.ShapeDtypeStruct((rows // 2, features), jnp.bfloat16),
+            jax.ShapeDtypeStruct((heights[0], features), jnp.float32),
+            jax.ShapeDtypeStruct((heights[1], features), jnp.bfloat16),
+            jax.ShapeDtypeStruct((heights[2], features), jnp.bfloat16),
         ],
         scratch_shapes=[
             pltpu.VMEM((rows, width), jnp.bfloat16),
@@ -442,8 +447,8 @@
     outer = ep_size // 4
     tokens, _ = moe_input.shape
     experts = jnp.arange(ep_size, dtype=jnp.int32)
-    named = expert_ids[:, :, None] == experts[None, None, :]
-    dense = jnp.sum(jnp.where(named, gate_weights[:, :, None], 0.0), axis=1)
+    named = expert_ids.T[None, :, :] == experts[:, None, None]
+    dense = jnp.sum(jnp.where(named, gate_weights.T[None, :, :], 0.0), axis=1).T
     extra = split_exact(dense)
     lanes = -(-extra.shape[1] // 128) * 128
     extra = jnp.pad(extra, ((0, 0), (0, lanes - extra.shape[1])))
@@ -462,14 +467,16 @@
     block = own.shape[0]
     places = [(n * block, 0) for n in range(8)]
     me = lax.axis_index("ep").astype(jnp.int32).reshape(1)
-    keep, send = expert_call(
+    keep, send, send_far = expert_call(
         me, near + across, tuple(places), 8 * block, ep_size, w_gate[0], w_up[0], w_down[0]
     )
+    got_far = pull(send_far, "ep", 1, 2, 1)
     got = pull(send, "ep", 1, 2, 1)
 
     def part(n):
         rows = slice(n * block, (n + 1) * block)
-        return keep[rows] + got[rows].astype(jnp.float32)
+        other = got_far if n == 3 else got[rows]
+        return keep[rows] + other.astype(jnp.float32)
 
     got_both = pull(part(3).astype(jnp.bfloat16), "ep", 2, 2, 1)
     got_y = pull(part(2).astype(jnp.bfloat16), "ep", 2, 2, 1)

time: 180 us -> 180 us (level)
  local copies, waits for them, and re-layouts: 7.99 us -> 5.65 us
    unnamed x31, local copies, waits for them, and re-layouts: 4.89 us -> 2.48 us
    ppermute x18 -> x19, waiting for transfers between devices: 56.9 us -> 58.3 us  [pull(): return lax.ppermute(values, axis, pairs)]
    ppermute x18 -> x19, starting transfers between devices: 21.3 us -> 21.5 us  [pull(): return lax.ppermute(values, axis, pairs)]
  transfers between devices with their start and end apart: 20 -> 21, of which waited for: 9 -> 9; matrix products, arithmetic and copies ran while one was open for 7% -> 6% of each run, Pallas kernels for 30% -> 30%
where the time goes in v7:
time: 180 us; the launch traced here: 179 us
  Pallas kernels  67.5 us (38%)
  waiting for transfers between devices  63 us (35%)
  starting transfers between devices  29.4 us (16%)
  other arithmetic  12 us (7%)
  local copies, waits for them, and re-layouts  5.65 us (3%)
    ppermute x19, waiting for transfers between devices, pull(): return lax.ppermute(values, axis, pairs)  58.3 us
    pallas_call x3, Pallas kernels, attend(): pl.pallas_call(functools.partial(attention_body, heads=heads, together=to...  50.1 us
    ppermute x19, starting transfers between devices, pull(): return lax.ppermute(values, axis, pairs)  21.5 us
    pallas_call x1, Pallas kernels, expert_call(): pl.pallas_call(functools.partial(expert_body, places=places, hidden_steps...  13.5 us
    all_to_all x1, waiting for transfers between devices, fetch_pages(): lax.all_to_all(wanted, 'ep', split_axis=0, concat_axis=0, tiled=True)  4.71 us
    all_to_all x1, starting transfers between devices, fetch_pages(): lax.all_to_all(wanted, 'ep', split_axis=0, concat_axis=0, tiled=True)  4.1 us
    all_to_all x1, starting transfers between devices, fetch_pages(): own = lax.all_to_all(chosen, 'ep', split_axis=0, concat_axis=0, tiled=True)  3.88 us
  transfers between devices with their start and end apart: 21, of which 9 were waited for; matrix products, arithmetic and copies ran while one was open for 6% of the time, Pallas kernels for 30%

profile of v7, /device:TPU:0, one launch (start us, length us, event | category | flops | bytes accessed | tf_op | source)
XLA Modules:
  0.0 179.1 jit_solution(12391604946711595845)
XLA Ops:
  2.4 5.1 %collective-permute-start.3 = (bf16[16,3712]{1,0:T(8,128)(2,1)S(1)}, bf16[16,3712]{1,0:T(8,128)(2,1)S(1)}, u32[]{:S(2)}, u32[]{:S(2)}) collective-permute-start(bf16[16,3712]{1,0:T(8,128)(2,1)S(1)} %pad_maximum_fusion.1), channel_id=1, source_target_pairs={{12,0},{13,1},{14,2},{15,3},{8,4},{9,5},{10,6},{11,7},{4,8},{5,9},... | collective-permute-start | bytes 356360 | tf_op jit(solution)/shard_map/ppermute | solution.py:33
  8.2 3.5 %collective-permute-done.3 = bf16[16,3712]{1,0:T(8,128)(2,1)S(1)} collective-permute-done((bf16[16,3712]{1,0:T(8,128)(2,1)S(1)}, bf16[16,3712]{1,0:T(8,128)(2,1)S(1)}, u32[]{:S(2)}, u32[]{:S(2)}) %collective-permute-start.3) | collective-permute-done | bytes 118816 | tf_op jit(solution)/shard_map/ppermute | solution.py:33
  11.8 5.8 %collective-permute-done.2 = bf16[16,3712]{1,0:T(8,128)(2,1)S(1)} collective-permute-done((bf16[16,3712]{1,0:T(8,128)(2,1)S(1)}, bf16[16,3712]{1,0:T(8,128)(2,1)S(1)}, u32[]{:S(2)}, u32[]{:S(2)}) %collective-permute-start.2) | collective-permute-done | bytes 118816 | tf_op jit(solution)/shard_map/ppermute | solution.py:33
  17.6 0.9 pad_maximum_fusion.refs_0_
  18.5 1.6 collective-permute-start.5
  20.1 1.5 collective-permute-start.4
  21.6 8.9 %collective-permute-done.5.refs_2_ = bf16[64,3712]{1,0:T(8,128)(2,1)S(1)} collective-permute-done((bf16[64,3712]{1,0:T(8,128)(2,1)S(1)}, bf16[64,3712]{1,0:T(8,128)(2,1)S(1)}, u32[]{:S(2)}, u32[]{:S(2)}) %collective-permute-start.5) | collective-permute-done | bytes 475168 | tf_op jit(solution)/shard_map/ppermute | solution.py:33
  30.6 1.5 collective-permute-start.6
  32.6 9.3 %collective-permute-done.6.refs_3_ = bf16[64,3712]{1,0:T(8,128)(2,1)S(1)} collective-permute-done((bf16[64,3712]{1,0:T(8,128)(2,1)S(1)}, bf16[64,3712]{1,0:T(8,128)(2,1)S(1)}, u32[]{:S(2)}, u32[]{:S(2)}) %collective-permute-start.6) | collective-permute-done | bytes 475168 | tf_op jit(solution)/shard_map/ppermute | solution.py:33
  42.0 1.9 %collective-permute-done.10.refs_7_ = bf16[64,3712]{1,0:T(8,128)(2,1)} collective-permute-done((bf16[64,3712]{1,0:T(8,128)(2,1)S(1)}, bf16[64,3712]{1,0:T(8,128)(2,1)}, u32[]{:S(2)}, u32[]{:S(2)}) %collective-permute-start.10) | collective-permute-done | bytes 475168 | tf_op jit(solution)/shard_map/ppermute | solution.py:33
  44.0 13.5 %expert.1 = (f32[256,3584]{1,0:T(8,128)}, bf16[192,3584]{1,0:T(8,128)(2,1)}, bf16[64,3584]{1,0:T(8,128)(2,1)}) custom-call(s32[1]{0:T(128)} %bitcast.7.me_ref, bf16[64,3712]{1,0:T(8,128)(2,1)} %copy-done.2, bf16[64,3712]{1,0:T(8,128)(2,1)} %copy-done.6, bf16[64,3712]{1,0:T(8,128)(2,1)} %copy-done.5, bf16[64,3712]{1,0:T(8,128)(2,1)} %copy-done.7, ...), custom_call_target="tpu_custom_call" | custom-call | tf_op jit(solution)/shard_map/expert/pallas_call | solution.py:410
  58.6 4.1 %all-to-all-start = ((s32[16,1,2]{2,1,0:T(1,128)}), s32[16,1,2]{2,1,0:T(1,128)S(1)}, u32[]{:S(2)}, u32[]{:S(2)}) async-start(s32[16,1,2]{2,1,0:T(1,128)} %copy.21), calls=%async_computation | async-start | bytes 16384 | tf_op jit(solution)/shard_map/all_to_all | solution.py:256
  62.7 1.6 reshape.119.pool_ref
  64.3 4.7 %all-to-all-done = s32[16,1,2]{2,1,0:T(1,128)S(1)} async-done(((s32[16,1,2]{2,1,0:T(1,128)}), s32[16,1,2]{2,1,0:T(1,128)S(1)}, u32[]{:S(2)}, u32[]{:S(2)}) %all-to-all-start) | async-done | bytes 160 | tf_op jit(solution)/shard_map/all_to_all | solution.py:256
  69.7 2.3 %pick.1 = bf16[16,288,128]{2,1,0:T(8,128)(2,1)} custom-call(s32[1]{0:T(128)} %bitcast.1.rank_ref, s32[16,2]{1,0:T(8,128)} %bitcast.31, bf16[8,64,576]{2,1,0:T(8,128)(2,1)} %reshape.119.pool_ref), custom_call_target="tpu_custom_call" | custom-call | tf_op jit(solution)/shard_map/pick/pallas_call | solution.py:300
  72.0 3.9 %all-to-all-start.1 = ((bf16[16,288,128]{2,1,0:T(8,128)(2,1)}), bf16[16,288,128]{2,1,0:T(8,128)(2,1)S(1)}, u32[]{:S(2)}, u32[]{:S(2)}) async-start(bf16[16,288,128]{2,1,0:T(8,128)(2,1)} %pick.1), calls=%async_computation.1 | async-start | bytes 2359296 | tf_op jit(solution)/shard_map/all_to_all | solution.py:271
  76.1 1.3 add_convert_fusion.2
  77.3 1.7 collective-permute-start.13
  79.1 19.4 %collective-permute-done.13 = bf16[64,3584]{1,0:T(8,128)(2,1)S(1)} collective-permute-done((bf16[64,3584]{1,0:T(8,128)(2,1)S(1)}, bf16[64,3584]{1,0:T(8,128)(2,1)S(1)}, u32[]{:S(2)}, u32[]{:S(2)}) %collective-permute-start.13) | collective-permute-done | bytes 458784 | tf_op jit(solution)/shard_map/ppermute | solution.py:33
  98.5 3.1 %add_convert_fusion.1 = (bf16[64,3584]{1,0:T(8,128)(2,1)}, bf16[64,3584]{1,0:T(8,128)(2,1)}) fusion(bf16[64,3584]{1,0:T(8,128)(2,1)S(1)} %collective-permute-done.13, f32[256,3584]{1,0:T(8,128)} %get-tuple-element.9, bf16[192,3584]{1,0:T(8,128)(2,1)S(1)} %collective-permute-done.11), kind=kLoop, calls=%fused_computation.2 | loop fusion | flops 1835008 | bytes 4128768 | tf_op jit(solution)/shard_map/convert_element_type | solution.py:485
  101.6 1.5 collective-permute-start.15
  103.1 1.5 collective-permute-start.14
  107.5 6.4 %collective-permute-done.15 = bf16[64,3584]{1,0:T(8,128)(2,1)} collective-permute-done((bf16[64,3584]{1,0:T(8,128)(2,1)}, bf16[64,3584]{1,0:T(8,128)(2,1)}, u32[]{:S(2)}, u32[]{:S(2)}) %collective-permute-start.15) | collective-permute-done | bytes 458784 | tf_op jit(solution)/shard_map/ppermute | solution.py:33
  113.9 2.9 %collective-permute-done.14 = bf16[64,3584]{1,0:T(8,128)(2,1)} collective-permute-done((bf16[64,3584]{1,0:T(8,128)(2,1)}, bf16[64,3584]{1,0:T(8,128)(2,1)}, u32[]{:S(2)}, u32[]{:S(2)}) %collective-permute-start.14) | collective-permute-done | bytes 458784 | tf_op jit(solution)/shard_map/ppermute | solution.py:33
  116.8 1.8 %fusion.9 = (bf16[64,3584]{1,0:T(8,128)(2,1)S(1)}, f32[64,3584]{1,0:T(8,128)S(1)}) fusion(bf16[64,3584]{1,0:T(8,128)(2,1)} %collective-permute-done.15, bf16[64,3584]{1,0:T(8,128)(2,1)} %collective-permute-done.14, bf16[192,3584]{1,0:T(8,128)(2,1)} %copy-done.3, f32[256,3584]{1,0:T(8,128)} %get-tuple-element.9), kind=kLoop, calls=%fused_computation.39 | loop fusion | flops 1605632 | bytes 3670016 | tf_op jit(solution)/shard_map/convert.2
  119.3 4.3 %collective-permute-start.18 = (bf16[16,3584]{1,0:T(8,128)(2,1)}, bf16[16,3584]{1,0:T(8,128)(2,1)S(1)}, u32[]{:S(2)}, u32[]{:S(2)}) collective-permute-start(bf16[16,3584]{1,0:T(8,128)(2,1)} %get-tuple-element.17), channel_id=1, source_target_pairs={{0,12},{1,13},{2,14},{3,15},{4,8},{5,9},{6,10},{7,11},{8,4},{9,5},... | collective-permute-start | bytes 344072 | tf_op jit(solution)/shard_map/ppermute | solution.py:33
  124.7 1.6 lay.1.refs_4_
  126.4 21.8 %attend.3 = (f32[128,16384]{1,0:T(8,128)}, f32[128,4096]{1,0:T(8,128)}) custom-call(s32[16]{0:T(128)} %broadcast_add_fusion.first_ref.refs_0_, s32[1]{0:T(128)S(6)} %copy.28.refs_1_, bf16[128,18432]{1,0:T(8,128)(2,1)} %refs_2_.5, bf16[16,288,128]{2,1,0:T(8,128)(2,1)} %copy-done.1, bf16[128,576]{1,0:T(8,128)(2,1)} %lay.1.refs_4_), custom_call_target="tpu_custom_call" | custom-call | tf_op jit(solution)/shard_map/attend/pallas_call | solution.py:203
  148.2 1.0 copy-done
  149.2 14.1 %attend.4.refs_6_ = bf16[128,16384]{1,0:T(8,128)(2,1)} custom-call(s32[16]{0:T(128)} %broadcast_add_fusion.1.second_ref.refs_0_, s32[1]{0:T(128)S(6)} %copy.28.refs_1_, bf16[128,18432]{1,0:T(8,128)(2,1)} %refs_2_.5, bf16[16,288,128]{2,1,0:T(8,128)(2,1)} %copy-done, f32[128,16384]{1,0:T(8,128)} %get-tuple-element.7.refs_4_, f32[128,4096]{1,0:T(8,128)} %get-tuple-element.8.refs_5_), custom_call_target="tpu_custom_call" | custom-call | tf_op jit(solution)/shard_map/attend/pallas_call | solution.py:203
  163.3 14.1 %attend.5 = bf16[128,16384]{1,0:T(8,128)(2,1)} custom-call(s32[16]{0:T(128)} %broadcast_add_fusion.1.second_ref.refs_0_, s32[1]{0:T(128)S(6)} %copy.28.refs_1_, bf16[128,18432]{1,0:T(8,128)(2,1)} %refs_2_.5, bf16[16,288,128]{2,1,0:T(8,128)(2,1)} %copy-done, f32[128,16384]{1,0:T(8,128)} %get-tuple-element.7.refs_4_, ...), custom_call_target="tpu_custom_call", output_to_operand_aliasing={{}: (6, {})} | custom-call | tf_op jit(solution)/shard_map/attend/pallas_call | solution.py:203
  177.5 1.7 fusion.2
  (72 shorter events, 9.0 us)
Async XLA Ops:
  2.4 9.3 %collective-permute-start.3 = (bf16[16,3712]{1,0:T(8,128)(2,1)S(1)}, bf16[16,3712]{1,0:T(8,128)(2,1)S(1)}, u32[]{:S(2)}, u32[]{:S(2)}) collective-permute-start(bf16[16,3712]{1,0:T(8,128)(2,1)S(1)} %pad_maximum_fusion.1), channel_id=1, source_target_pairs={{12,0},{13,1},{14,2},{15,3},{8,4},{9,5},{10,6},{11,7},{4,8},{5,9},... | collective-permute-start | bytes 356360 | tf_op jit(solution)/shard_map/ppermute | solution.py:33
  7.6 10.0 %collective-permute-start.2 = (bf16[16,3712]{1,0:T(8,128)(2,1)S(1)}, bf16[16,3712]{1,0:T(8,128)(2,1)S(1)}, u32[]{:S(2)}, u32[]{:S(2)}) collective-permute-start(bf16[16,3712]{1,0:T(8,128)(2,1)S(1)} %pad_maximum_fusion.1), channel_id=1, source_target_pairs={{8,0},{9,1},{10,2},{11,3},{12,4},{13,5},{14,6},{15,7},{0,8},{1,9},... | collective-permute-start | bytes 356360 | tf_op jit(solution)/shard_map/ppermute | solution.py:33
  7.6 10.0 %collective-permute-start.1 = (bf16[16,3712]{1,0:T(8,128)(2,1)S(1)}, bf16[16,3712]{1,0:T(8,128)(2,1)S(1)}, u32[]{:S(2)}, u32[]{:S(2)}) collective-permute-start(bf16[16,3712]{1,0:T(8,128)(2,1)S(1)} %pad_maximum_fusion.1), channel_id=1, source_target_pairs={{4,0},{5,1},{6,2},{7,3},{0,4},{1,5},{2,6},{3,7},{12,8},{13,9},{14,... | collective-permute-start | bytes 356360 | tf_op jit(solution)/shard_map/ppermute | solution.py:33
  18.5 25.4 %copy-start.2 = (bf16[64,3712]{1,0:T(8,128)(2,1)}, bf16[64,3712]{1,0:T(8,128)(2,1)S(1)}, u32[]{:S(2)}) copy-start(bf16[64,3712]{1,0:T(8,128)(2,1)S(1)} %pad_maximum_fusion.refs_0_) | copy-start | bytes 1425412
  18.5 12.0 %collective-permute-start.5 = (bf16[64,3712]{1,0:T(8,128)(2,1)S(1)}, bf16[64,3712]{1,0:T(8,128)(2,1)S(1)}, u32[]{:S(2)}, u32[]{:S(2)}) collective-permute-start(bf16[64,3712]{1,0:T(8,128)(2,1)S(1)} %pad_maximum_fusion.refs_0_), channel_id=1, source_target_pairs={{2,0},{3,1},{0,2},{1,3},{6,4},{7,5},{4,6},{5,7},{10,8},{11,9},{8,1... | collective-permute-start | bytes 1425416 | tf_op jit(solution)/shard_map/ppermute | solution.py:33
  20.1 12.4 %collective-permute-start.4 = (bf16[64,3712]{1,0:T(8,128)(2,1)S(1)}, bf16[64,3712]{1,0:T(8,128)(2,1)S(1)}, u32[]{:S(2)}, u32[]{:S(2)}) collective-permute-start(bf16[64,3712]{1,0:T(8,128)(2,1)S(1)} %pad_maximum_fusion.refs_0_), channel_id=1, source_target_pairs={{16,0},{0,16},{17,1},{1,17},{18,2},{2,18},{19,3},{3,19},{20,4},{4,... | collective-permute-start | bytes 1425416 | tf_op jit(solution)/shard_map/ppermute | solution.py:33
  30.6 13.4 %copy-start.5 = (bf16[64,3712]{1,0:T(8,128)(2,1)}, bf16[64,3712]{1,0:T(8,128)(2,1)S(1)}, u32[]{:S(2)}) copy-start(bf16[64,3712]{1,0:T(8,128)(2,1)S(1)} %collective-permute-done.5.refs_2_) | copy-start | bytes 1425412
  30.6 11.4 %collective-permute-start.6 = (bf16[64,3712]{1,0:T(8,128)(2,1)S(1)}, bf16[64,3712]{1,0:T(8,128)(2,1)S(1)}, u32[]{:S(2)}, u32[]{:S(2)}) collective-permute-start(bf16[64,3712]{1,0:T(8,128)(2,1)S(1)} %collective-permute-done.5.refs_2_), channel_id=1, source_target_pairs={{16,0},{0,16},{17,1},{1,17},{18,2},{2,18},{19,3},{3,19},{20,4},{4,... | collective-permute-start | bytes 1425416 | tf_op jit(solution)/shard_map/ppermute | solution.py:33
  32.0 9.9 %collective-permute-start.7 = (bf16[64,3712]{1,0:T(8,128)(2,1)S(1)}, bf16[64,3712]{1,0:T(8,128)(2,1)S(1)}, u32[]{:S(2)}, u32[]{:S(2)}) collective-permute-start(bf16[64,3712]{1,0:T(8,128)(2,1)S(1)} %pad_maximum_fusion.refs_0_), channel_id=1, source_target_pairs={{1,0},{0,1},{3,2},{2,3},{5,4},{4,5},{7,6},{6,7},{9,8},{8,9},{11,10... | collective-permute-start | bytes 1425416 | tf_op jit(solution)/shard_map/ppermute | solution.py:33
  32.0 10.0 %collective-permute-start.9 = (bf16[64,3712]{1,0:T(8,128)(2,1)S(1)}, bf16[64,3712]{1,0:T(8,128)(2,1)S(1)}, u32[]{:S(2)}, u32[]{:S(2)}) collective-permute-start(bf16[64,3712]{1,0:T(8,128)(2,1)S(1)} %collective-permute-done.5.refs_2_), channel_id=1, source_target_pairs={{1,0},{0,1},{3,2},{2,3},{5,4},{4,5},{7,6},{6,7},{9,8},{8,9},{11,10... | collective-permute-start | bytes 1425416 | tf_op jit(solution)/shard_map/ppermute | solution.py:33
  32.6 11.4 %copy-start.6 = (bf16[64,3712]{1,0:T(8,128)(2,1)}, bf16[64,3712]{1,0:T(8,128)(2,1)S(1)}, u32[]{:S(2)}) copy-start(bf16[64,3712]{1,0:T(8,128)(2,1)S(1)} %collective-permute-done.4.refs_1_) | copy-start | bytes 1425412
  32.6 9.4 %collective-permute-start.8 = (bf16[64,3712]{1,0:T(8,128)(2,1)S(1)}, bf16[64,3712]{1,0:T(8,128)(2,1)S(1)}, u32[]{:S(2)}, u32[]{:S(2)}) collective-permute-start(bf16[64,3712]{1,0:T(8,128)(2,1)S(1)} %collective-permute-done.4.refs_1_), channel_id=1, source_target_pairs={{1,0},{0,1},{3,2},{2,3},{5,4},{4,5},{7,6},{6,7},{9,8},{8,9},{11,10... | collective-permute-start | bytes 1425416 | tf_op jit(solution)/shard_map/ppermute | solution.py:33
  42.0 2.0 %copy-start.7 = (bf16[64,3712]{1,0:T(8,128)(2,1)}, bf16[64,3712]{1,0:T(8,128)(2,1)S(1)}, u32[]{:S(2)}) copy-start(bf16[64,3712]{1,0:T(8,128)(2,1)S(1)} %collective-permute-done.6.refs_3_) | copy-start | bytes 1425412
  42.0 2.0 %collective-permute-start.10 = (bf16[64,3712]{1,0:T(8,128)(2,1)S(1)}, bf16[64,3712]{1,0:T(8,128)(2,1)}, u32[]{:S(2)}, u32[]{:S(2)}) collective-permute-start(bf16[64,3712]{1,0:T(8,128)(2,1)S(1)} %collective-permute-done.6.refs_3_), channel_id=1, source_target_pairs={{1,0},{0,1},{3,2},{2,3},{5,4},{4,5},{7,6},{6,7},{9,8},{8,9},{11,10... | collective-permute-start | bytes 1425416 | tf_op jit(solution)/shard_map/ppermute | solution.py:33
  42.0 2.0 %copy-start.8 = (bf16[64,3712]{1,0:T(8,128)(2,1)}, bf16[64,3712]{1,0:T(8,128)(2,1)S(1)}, u32[]{:S(2)}) copy-start(bf16[64,3712]{1,0:T(8,128)(2,1)S(1)} %collective-permute-done.7.refs_4_) | copy-start | bytes 1425412
  44.0 13.8 %copy-start.13 = (s32[1,32]{1,0:T(1,128)S(1)}, s32[1,32]{1,0:T(1,128)}, u32[]{:S(2)}) copy-start(s32[1,32]{1,0:T(1,128)} %param.15) | copy-start | bytes 388
  44.0 13.8 %copy-start.14 = (s32[1,32]{1,0:T(1,128)S(1)}, s32[1,32]{1,0:T(1,128)}, u32[]{:S(2)}) copy-start(s32[1,32]{1,0:T(1,128)} %param.16) | copy-start | bytes 388
  44.0 18.7 %copy-start.4 = (bf16[8,36864]{1,0:T(8,128)(2,1)S(1)}, bf16[8,36864]{1,0:T(8,128)(2,1)}, u32[]{:S(2)}) copy-start(bf16[8,36864]{1,0:T(8,128)(2,1)} %param.14) | copy-start | bytes 1769476
  57.6 18.5 %collective-permute-start.12 = (bf16[64,3584]{1,0:T(8,128)(2,1)}, bf16[64,3584]{1,0:T(8,128)(2,1)S(1)}, u32[]{:S(2)}, u32[]{:S(2)}) collective-permute-start(bf16[64,3584]{1,0:T(8,128)(2,1)} %get-tuple-element.11), channel_id=1, source_target_pairs={{1,0},{0,1},{3,2},{2,3},{5,4},{4,5},{7,6},{6,7},{9,8},{8,9},{11,10... | collective-permute-start | bytes 1376264 | tf_op jit(solution)/shard_map/ppermute | solution.py:33
  58.6 10.5 %all-to-all-start = ((s32[16,1,2]{2,1,0:T(1,128)}), s32[16,1,2]{2,1,0:T(1,128)S(1)}, u32[]{:S(2)}, u32[]{:S(2)}) async-start(s32[16,1,2]{2,1,0:T(1,128)} %copy.21), calls=%async_computation | async-start | bytes 16384 | tf_op jit(solution)/shard_map/all_to_all | solution.py:256
  72.0 34.9 %all-to-all-start.1 = ((bf16[16,288,128]{2,1,0:T(8,128)(2,1)}), bf16[16,288,128]{2,1,0:T(8,128)(2,1)S(1)}, u32[]{:S(2)}, u32[]{:S(2)}) async-start(bf16[16,288,128]{2,1,0:T(8,128)(2,1)} %pick.1), calls=%async_computation.1 | async-start | bytes 2359296 | tf_op jit(solution)/shard_map/all_to_all | solution.py:271
  75.9 22.6 %collective-permute-start.11 = (bf16[192,3584]{1,0:T(8,128)(2,1)}, bf16[192,3584]{1,0:T(8,128)(2,1)S(1)}, u32[]{:S(2)}, u32[]{:S(2)}) collective-permute-start(bf16[192,3584]{1,0:T(8,128)(2,1)} %get-tuple-element.10), channel_id=1, source_target_pairs={{1,0},{0,1},{3,2},{2,3},{5,4},{4,5},{7,6},{6,7},{9,8},{8,9},{11,10... | collective-permute-start | bytes 4128776 | tf_op jit(solution)/shard_map/ppermute | solution.py:33
  77.3 21.2 %collective-permute-start.13 = (bf16[64,3584]{1,0:T(8,128)(2,1)S(1)}, bf16[64,3584]{1,0:T(8,128)(2,1)S(1)}, u32[]{:S(2)}, u32[]{:S(2)}) collective-permute-start(bf16[64,3584]{1,0:T(8,128)(2,1)S(1)} %add_convert_fusion.2), channel_id=1, source_target_pairs={{2,0},{3,1},{0,2},{1,3},{6,4},{7,5},{4,6},{5,7},{10,8},{11,9},{8,1... | collective-permute-start | bytes 1376264 | tf_op jit(solution)/shard_map/ppermute | solution.py:33
  98.5 6.7 %copy-start.11 = (bf16[128,576]{0,1:T(8,128)(2,1)S(1)}, bf16[128,576]{0,1:T(8,128)(2,1)}, u32[]{:S(2)}) copy-start(bf16[128,576]{0,1:T(8,128)(2,1)} %param.13) | copy-start | bytes 442372
  98.5 8.4 %copy-start.3 = (bf16[192,3584]{1,0:T(8,128)(2,1)}, bf16[192,3584]{1,0:T(8,128)(2,1)S(1)}, u32[]{:S(2)}) copy-start(bf16[192,3584]{1,0:T(8,128)(2,1)S(1)} %collective-permute-done.11) | copy-start | bytes 4128772
  101.6 12.2 %collective-permute-start.15 = (bf16[64,3584]{1,0:T(8,128)(2,1)}, bf16[64,3584]{1,0:T(8,128)(2,1)}, u32[]{:S(2)}, u32[]{:S(2)}) collective-permute-start(bf16[64,3584]{1,0:T(8,128)(2,1)} %get-tuple-element.15), channel_id=1, source_target_pairs={{2,0},{3,1},{0,2},{1,3},{6,4},{7,5},{4,6},{5,7},{10,8},{11,9},{8,1... | collective-permute-start | bytes 1376264 | tf_op jit(solution)/shard_map/ppermute | solution.py:33
  103.1 13.7 %collective-permute-start.14 = (bf16[64,3584]{1,0:T(8,128)(2,1)}, bf16[64,3584]{1,0:T(8,128)(2,1)}, u32[]{:S(2)}, u32[]{:S(2)}) collective-permute-start(bf16[64,3584]{1,0:T(8,128)(2,1)} %get-tuple-element.14), channel_id=1, source_target_pairs={{16,0},{0,16},{17,1},{1,17},{18,2},{2,18},{19,3},{3,19},{20,4},{4,... | collective-permute-start | bytes 1376264 | tf_op jit(solution)/shard_map/ppermute | solution.py:33
  106.9 19.5 %copy-start.1 = (bf16[16,288,128]{2,1,0:T(8,128)(2,1)}, bf16[16,288,128]{2,1,0:T(8,128)(2,1)S(1)}, u32[]{:S(2)}) copy-start(bf16[16,288,128]{2,1,0:T(8,128)(2,1)S(1)} %all-to-all-done.1.refs_3_) | copy-start | bytes 3538948
  106.9 41.3 %collective-permute-start = (bf16[16,288,128]{2,1,0:T(8,128)(2,1)S(1)}, bf16[16,288,128]{2,1,0:T(8,128)(2,1)S(1)}, u32[]{:S(2)}, u32[]{:S(2)}) collective-permute-start(bf16[16,288,128]{2,1,0:T(8,128)(2,1)S(1)} %all-to-all-done.1.refs_3_), channel_id=1, source_target_pairs={{16,0},{0,16},{17,1},{1,17},{18,2},{2,18},{19,3},{3,19},{20,4},{4,... | collective-permute-start | bytes 3538952 | tf_op jit(solution)/shard_map/ppermute | solution.py:33
  119.3 58.2 %collective-permute-start.18 = (bf16[16,3584]{1,0:T(8,128)(2,1)}, bf16[16,3584]{1,0:T(8,128)(2,1)S(1)}, u32[]{:S(2)}, u32[]{:S(2)}) collective-permute-start(bf16[16,3584]{1,0:T(8,128)(2,1)} %get-tuple-element.17), channel_id=1, source_target_pairs={{0,12},{1,13},{2,14},{3,15},{4,8},{5,9},{6,10},{7,11},{8,4},{9,5},... | collective-permute-start | bytes 344072 | tf_op jit(solution)/shard_map/ppermute | solution.py:33
  123.6 53.8 %collective-permute-start.17 = (bf16[16,3584]{1,0:T(8,128)(2,1)}, bf16[16,3584]{1,0:T(8,128)(2,1)}, u32[]{:S(2)}, u32[]{:S(2)}) collective-permute-start(bf16[16,3584]{1,0:T(8,128)(2,1)} %get-tuple-element.18), channel_id=1, source_target_pairs={{0,8},{1,9},{2,10},{3,11},{4,12},{5,13},{6,14},{7,15},{8,0},{9,1},... | collective-permute-start | bytes 344072 | tf_op jit(solution)/shard_map/ppermute | solution.py:33
  123.6 53.8 %collective-permute-start.16 = (bf16[16,3584]{1,0:T(8,128)(2,1)S(1)}, bf16[16,3584]{1,0:T(8,128)(2,1)}, u32[]{:S(2)}, u32[]{:S(2)}) collective-permute-start(bf16[16,3584]{1,0:T(8,128)(2,1)S(1)} %get-tuple-element.16), channel_id=1, source_target_pairs={{0,4},{1,5},{2,6},{3,7},{4,0},{5,1},{6,2},{7,3},{8,12},{9,13},{10,... | collective-permute-start | bytes 344072 | tf_op jit(solution)/shard_map/ppermute | solution.py:33
  (4 other events, 5.5 us)
